TPU v7x, 256 devices: a whole 4x4x8 slice. The times are simulated.
256 devices in a mesh: cell: 16 (over z, core), sub: 16 (over x, y).
Axes of the slice: x: 4, y: 4, z: 8, core: 2. Of those that a mesh axis runs over, the one named last changes fastest.
Arguments:
- queries: bfloat16 [4096, 1024], P('cell', 'sub'), may hold values from -384 to 384
- probe_groups: int32 [4096, 2], P('cell'), may hold values from 0 to 15, all different within a row; in each aligned block of 256 rows (0 to 255, 256 to 511, ...) at most 64 rows name the same one
- probe_cells: int32 [4096, 2, 16], P('cell'), may hold values from 0 to 31, as said below
- coarse: bfloat16 [512, 1024], P('cell', 'sub'), may hold values from -1.1953125 to 1.1953125
- codebooks: bfloat16 [64, 16, 256], P('sub'), may hold values from -1.5 to 1.5
- codes: int32 [512, 64, 384], P('cell', 'sub'), may hold values from 0 to 255
- lengths: int32 [512], P('cell'), may hold values from 1 to 384, 98304 in all
- payload: bfloat16 [512, 384, 256], P('cell', 'sub'), may hold values from -6 to 6
Outputs:
- pooled: bfloat16 [4096, 256], P('cell')
Inputs may be any that keep to these rules, and one draw needn't show every extreme that they name: `probe_cells`: the 16 cells of one query in one group are distinct. `probe_groups`: the queries of one index of cell name one group at most 64 times, and one group exactly 64 times in some index. `lengths`: some cell has all 384 rows live.
All inputs are finite; a program needn't handle non-finite values. No bound on the sum of `lengths` on one device may be relied on, other than what follows from the above.
Results may differ from a plain program's by a relative error of at most 0.003.
The roundings to bfloat16 on the way count: a program that leaves them out, or rounds other values in their place, can miss the bound.
Values may be sent and summed in bfloat16 or wider, within the bound.
No kernel may reach another device: no remote copies, remote signals or barrier semaphores. Data moves between devices by JAX's collectives and lax.ppermute only.
A program may use at most 64 MiB of HBM per device.

v0:
```python
import math

import jax
import jax.numpy as jnp
from jax import lax
from jax.sharding import PartitionSpec as P

CAP = 64


score_scale = 0.3
floor_score = -1e30


def slot_table(probe_groups, groups, capacity):
    marks = (probe_groups[:, :, None] == jnp.arange(groups, dtype=jnp.int32)[None, None, :]).astype(
        jnp.int32
    )
    routed = jnp.sum(marks, axis=1)
    earlier = jnp.cumsum(routed, axis=0) - routed
    position = jnp.sum(marks * earlier[:, None, :], axis=2)
    return probe_groups * capacity + position


def pack_slots(rows, probe_cells, slots, total):
    flat = slots.reshape(-1)
    doubled = jnp.repeat(rows, 2, axis=0)
    buffer = jnp.zeros((total, rows.shape[1]), rows.dtype).at[flat].set(doubled)
    named = probe_cells.reshape(flat.shape[0], -1).astype(jnp.bfloat16)
    cell_marks = jnp.full((total, probe_cells.shape[2]), -1.0, jnp.bfloat16).at[flat].set(named)
    return (buffer, cell_marks)


def decode(coarse, codebooks, codes):
    cell_count = codes.shape[0]
    sub_count = codes.shape[1]
    row_count = codes.shape[2]
    width = codebooks.shape[1]
    centroid_ids = jnp.arange(codebooks.shape[2], dtype=jnp.int32)

    def one_subspace(pair):
        book = pair[0]
        flat_codes = pair[1].reshape(-1)
        onehot = (flat_codes[None, :] == centroid_ids[:, None]).astype(jnp.bfloat16)
        return jnp.dot(book, onehot, preferred_element_type=jnp.float32)

    picked = lax.map(one_subspace, (codebooks, jnp.transpose(codes, (1, 0, 2))))
    recon = picked.reshape(sub_count * width, cell_count, row_count)
    return (recon + coarse.T.astype(jnp.float32)[:, :, None]).astype(jnp.bfloat16)


def combine(back_part, back_mass, back_peak, slots, total):
    peaks = back_peak.reshape(-1)[slots]
    masses = back_mass.reshape(-1)[slots]
    parts = back_part.reshape(total, -1)[slots]
    top = jnp.max(peaks, axis=1, keepdims=True)
    scale = jnp.exp(peaks - top)
    upper = jnp.sum(scale[:, :, None] * parts, axis=1)
    lower = jnp.sum(scale * masses, axis=1)
    return (upper / lower[:, None]).astype(jnp.bfloat16)


def local(queries, probe_groups, probe_cells, coarse, codebooks, codes, lengths, payload):
    groups = lax.axis_size("cell")
    capacity = CAP
    total = groups * capacity
    slots = slot_table(probe_groups, groups, capacity)
    buffer, cell_marks = pack_slots(queries, probe_cells, slots, total)
    arrived, arrived_cells = (
        lax.all_to_all(
            buffer.reshape(groups, capacity, -1), "cell", split_axis=0, concat_axis=0, tiled=True
        ),
        lax.all_to_all(
            cell_marks.reshape(groups, capacity, -1),
            "cell",
            split_axis=0,
            concat_axis=0,
            tiled=True,
        ),
    )
    full_rows = lax.all_gather(arrived.reshape(total, -1), "sub", axis=1, tiled=True)
    cell_ids = arrived_cells.reshape(total, -1).astype(jnp.int32)
    cell_dev = codes.shape[0]
    probed = jnp.any(
        cell_ids[:, :, None] == jnp.arange(cell_dev, dtype=jnp.int32)[None, None, :], axis=1
    )
    local_vectors = decode(coarse, codebooks, codes)
    decoded = lax.all_to_all(local_vectors, "sub", split_axis=2, concat_axis=0, tiled=True)
    row_local = decoded.shape[2]
    decoded = decoded.reshape(decoded.shape[0], -1)
    sq_norm = jnp.sum(jnp.square(decoded.astype(jnp.float32)), axis=0)
    first_row = lax.axis_index("sub") * row_local
    live = (first_row + jnp.arange(row_local, dtype=jnp.int32))[None, :] < lengths[:, None]
    block = math.gcd(total, 512)
    count = total // block
    query_blocks = full_rows.reshape(count, block, -1)
    probe_blocks = probed.reshape(count, block, cell_dev)
    table = payload.reshape(-1, payload.shape[2])

    def block_scores(pair):
        raw = jnp.dot(pair[0], decoded, preferred_element_type=jnp.float32)
        values = (raw - 0.5 * sq_norm[None, :]) * score_scale
        keep = (pair[1][:, :, None] & live[None, :, :]).reshape(pair[0].shape[0], -1)
        return (values, keep, jnp.max(jnp.where(keep, values, floor_score), axis=1))

    value_blocks, keep_blocks, local_peak = lax.map(block_scores, (query_blocks, probe_blocks))
    peak = lax.pmax(local_peak.reshape(total), "sub")

    def block_sums(triple):
        weights = jnp.where(triple[1], jnp.exp(triple[0] - triple[2][:, None]), 0.0).astype(
            jnp.bfloat16
        )
        mass = jnp.sum(weights.astype(jnp.float32), axis=1)
        part = jnp.dot(weights, table, preferred_element_type=jnp.float32)
        return (mass, part)

    mass, part = lax.map(block_sums, (value_blocks, keep_blocks, peak.reshape(count, block)))
    mass = mass.reshape(total)
    part = part.reshape(total, -1)
    part_sum, mass_sum = lax.psum((part, mass), "sub")
    back_part, back_mass, back_peak = (
        lax.all_to_all(
            part_sum.reshape(groups, capacity, -1), "cell", split_axis=0, concat_axis=0, tiled=True
        ),
        lax.all_to_all(
            mass_sum.reshape(groups, capacity), "cell", split_axis=0, concat_axis=0, tiled=True
        ),
        lax.all_to_all(
            peak.reshape(groups, capacity), "cell", split_axis=0, concat_axis=0, tiled=True
        ),
    )
    return combine(back_part, back_mass, back_peak, slots, total)


def solution(mesh):
    placed = (
        P("cell", "sub"),
        P("cell", None),
        P("cell", None, None),
        P("cell", "sub"),
        P("sub", None, None),
        P("cell", "sub", None),
        P("cell"),
        P("cell", "sub", None),
    )
    return jax.shard_map(
        local, mesh=mesh, in_specs=placed, out_specs=P("cell", None), check_vma=False
    )
```

profile of v0, /device:TPU:1, one launch (start us, length us, event | category | flops | bytes accessed | tf_op | source)
XLA Modules:
  0.0 327.3 jit_solution(5342535578300874204)
XLA Ops:
  8.9 1.3 compare_select_fusion.1
  10.5 0.9 copy.132
  11.4 1.8 scatter_custom_fusion
  13.5 18.6 %all_to_all.48 = bf16[16,2,2048]{2,1,0:T(2,128)(2,1)S(1)} all-to-all(bf16[16,2,2048]{2,1,0:T(2,128)(2,1)S(1)} %reshape.281), channel_id=1, replica_groups=mesh['cell'=16,'sub'=16] {'cell'}, dimensions={0} | all-to-all | bytes 262144 | tf_op jit(solution)/shard_map/all_to_all | solution.py:70
  32.4 0.8 copy.148
  33.3 1.8 scatter_custom_fusion.1
  36.0 3.4 %all-to-all-start.2 = ((bf16[16,2,512]{2,1,0:T(2,128)(2,1)}), bf16[16,2,512]{2,1,0:T(2,128)(2,1)S(1)}, u32[]{:S(2)}, u32[]{:S(2)}) async-start(bf16[16,2,512]{2,1,0:T(2,128)(2,1)} %reshape.285), calls=%async_computation.2 | async-start | bytes 65536 | tf_op jit(solution)/shard_map/all_to_all | solution.py:73
  39.4 14.3 %while.39 = (s32[]{:T(128)}, f32[4,16,12288]{2,1,0:T(8,128)}, bf16[4,16,256]{2,1,0:T(8,128)(2,1)}, s32[4,32,384]{2,1,0:T(8,128)S(1)}, s32[]{:T(128)}) while((s32[]{:T(128)}, f32[4,16,12288]{2,1,0:T(8,128)}, bf16[4,16,256]{2,1,0:T(8,128)(2,1)}, s32[4,32,384]{2,1,0:T(8,128)S(1)}, s32[]{:T(128)}) %tuple.88), condition=%wide.region_8.9_spmd.clone, body=%wide.region_7.8_spmd.clone.sunk | while | flops 103809024 | bytes 1041473 | solution.py:47
  39.5 3.5 %fusion.38 = f32[4,16,12288]{2,1,0:T(8,128)} fusion(f32[4,16,12288]{2,1,0:T(8,128)} %get-tuple-element.471, s32[]{:T(128)} %get-tuple-element.470, s32[12288]{0:T(1024)S(1)} %eq.81, bf16[4,16,256]{2,1,0:T(8,128)(2,1)} %get-tuple-element.477), kind=kOutput, calls=%fused_computation.17.clone.1 | convolution fusion | flops 103809024 | bytes 844800 | tf_op jit(solution)/shard_map/while/body/eval_jaxpr/dot_general | solution.py:45
  43.0 3.6 %fusion.38 = f32[4,16,12288]{2,1,0:T(8,128)} fusion(f32[4,16,12288]{2,1,0:T(8,128)} %get-tuple-element.471, s32[]{:T(128)} %get-tuple-element.470, s32[12288]{0:T(1024)S(1)} %eq.81, bf16[4,16,256]{2,1,0:T(8,128)(2,1)} %get-tuple-element.477), kind=kOutput, calls=%fused_computation.17.clone.1 | convolution fusion | flops 103809024 | bytes 844800 | tf_op jit(solution)/shard_map/while/body/eval_jaxpr/dot_general | solution.py:45
  46.6 3.5 %fusion.38 = f32[4,16,12288]{2,1,0:T(8,128)} fusion(f32[4,16,12288]{2,1,0:T(8,128)} %get-tuple-element.471, s32[]{:T(128)} %get-tuple-element.470, s32[12288]{0:T(1024)S(1)} %eq.81, bf16[4,16,256]{2,1,0:T(8,128)(2,1)} %get-tuple-element.477), kind=kOutput, calls=%fused_computation.17.clone.1 | convolution fusion | flops 103809024 | bytes 844800 | tf_op jit(solution)/shard_map/while/body/eval_jaxpr/dot_general | solution.py:45
  50.1 3.5 %fusion.38 = f32[4,16,12288]{2,1,0:T(8,128)} fusion(f32[4,16,12288]{2,1,0:T(8,128)} %get-tuple-element.471, s32[]{:T(128)} %get-tuple-element.470, s32[12288]{0:T(1024)S(1)} %eq.81, bf16[4,16,256]{2,1,0:T(8,128)(2,1)} %get-tuple-element.477), kind=kOutput, calls=%fused_computation.17.clone.1 | convolution fusion | flops 103809024 | bytes 844800 | tf_op jit(solution)/shard_map/while/body/eval_jaxpr/dot_general | solution.py:45
  53.7 2.5 copy.157
  56.3 1.5 fusion.16
  57.8 6.4 %copy.136 = bf16[64,32,384]{0,1,2:T(8,128)(2,1)S(1)} copy(bf16[64,32,384]{2,1,0:T(8,128)(2,1)} %fusion.16) | data formatting | bytes 3145728 | tf_op jit(solution)/shard_map/convert_element_type | solution.py:49
  64.2 3.2 reshape.283
  67.4 6.8 %all-to-all-start.1 = ((bf16[16,2,24576]{2,1,0:T(2,128)(2,1)}), bf16[16,2,24576]{2,1,0:T(2,128)(2,1)}, u32[]{:S(2)}, u32[]{:S(2)}) async-start(bf16[16,2,24576]{2,1,0:T(2,128)(2,1)} %reshape.283), calls=%async_computation.1 | async-start | bytes 3145728 | tf_op jit(solution)/shard_map/all_to_all | solution.py:88
  76.2 22.2 %all-to-all-done.1 = bf16[16,2,24576]{2,1,0:T(2,128)(2,1)} async-done(((bf16[16,2,24576]{2,1,0:T(2,128)(2,1)}), bf16[16,2,24576]{2,1,0:T(2,128)(2,1)}, u32[]{:S(2)}, u32[]{:S(2)}) %all-to-all-start.1) | async-done | bytes 1572896 | tf_op jit(solution)/shard_map/all_to_all | solution.py:88
  98.4 3.8 %reshape.284 = bf16[384,32,64]{2,1,0:T(8,128)(2,1)S(1)} reshape(bf16[16,2,24576]{2,1,0:T(2,128)(2,1)} %all-to-all-done.1) | data formatting | bytes 3145728
  102.2 2.9 copy.137
  105.1 3.7 %copy.138 = bf16[16,64,32,24]{1,0,3,2:T(8,128)(2,1)} copy(bf16[16,64,32,24]{1,2,3,0:T(8,128)(2,1)S(1)} %bitcast.128) | data formatting | bytes 3145728 | tf_op jit(solution)/shard_map/all_to_all | solution.py:88
  108.8 5.4 %reshape.199 = bf16[1024,768]{0,1:T(8,128)(2,1)} reshape(bf16[16,64,32,24]{1,0,3,2:T(8,128)(2,1)} %copy.138) | data formatting | bytes 3145728 | tf_op jit(solution)/shard_map/reshape | solution.py:90
  114.2 2.7 copy.144
  117.0 0.9 multiply_reduce_fusion
  118.5 4.0 %copy.149 = bf16[1024,1024]{1,0:T(8,128)(2,1)} copy(bf16[1024,1024]{0,1:T(8,128)(2,1)} %all-gather.2.cloned.1.call-done) | data formatting | bytes 4194304
  123.2 17.6 %while.40 = (s32[]{:T(128)}, f32[2,512,768]{2,1,0:T(8,128)}, pred[2,512,768]{1,2,0:T(8,128)(4,1)S(1)}, f32[2,512]{1,0:T(2,128)}, bf16[2,512,1024]{2,1,0:T(8,128)...) while((s32[]{:T(128)}, f32[2,512,768]{2,1,0:T(8,128)}, ...), condition=%wide.region_12.13_spmd.clone, body=%wide.region_10.12_spmd.clone.sunk | while | flops 807666688 | bytes 9392481 | solution.py:106
  123.9 3.9 %bitcast_dynamic-update-slice_fusion.2 = (f32[2,512,768]{2,1,0:T(8,128)}, f32[512,768]{1,0:T(8,128)S(1)}) fusion(f32[2,512,768]{2,1,0:T(8,128)} %get-tuple-element.493, s32[]{:T(128)} %get-tuple-element.492, f32[768]{0:T(1024)S(1)} %broadcast_multiply_fusion.2, bf16[1024,768]{1,0:T(8,128)(2,1)} %get-tuple-element.509, ...), kind=kOutput, calls=%fused_computation.24.clone.1 | convolution fusion | flops 806092800 | bytes 5771264 | tf_op jit(solution)/shard_map/while/body/eval_jaxpr/dot_general | solution.py:101
  129.2 0.7 broadcast_compare_fusion.2
  130.3 1.3 dynamic_update_slice.42
  132.7 3.9 %bitcast_dynamic-update-slice_fusion.2 = (f32[2,512,768]{2,1,0:T(8,128)}, f32[512,768]{1,0:T(8,128)S(1)}) fusion(f32[2,512,768]{2,1,0:T(8,128)} %get-tuple-element.493, s32[]{:T(128)} %get-tuple-element.492, f32[768]{0:T(1024)S(1)} %broadcast_multiply_fusion.2, bf16[1024,768]{1,0:T(8,128)(2,1)} %get-tuple-element.509, ...), kind=kOutput, calls=%fused_computation.24.clone.1 | convolution fusion | flops 806092800 | bytes 5771264 | tf_op jit(solution)/shard_map/while/body/eval_jaxpr/dot_general | solution.py:101
  139.1 1.3 dynamic_update_slice.42
  141.4 30.3 %pmax.7 = f32[1024]{0:T(1024)S(1)} all-reduce(f32[1024]{0:T(1024)S(1)} %bitcast.148), channel_id=1, replica_groups=mesh['cell'=16,'sub'=16] {'sub'}, use_global_device_ids=true, to_apply=%region_13.14 | all-reduce | flops 1024 | bytes 8192 | tf_op jit(solution)/shard_map/pmax | solution.py:107
  171.8 8.0 %while.38 = (s32[]{:T(128)}, f32[2,512]{1,0:T(2,128)S(1)}, f32[2,512,256]{2,1,0:T(8,128)}, pred[2,512,768]{1,2,0:T(8,128)(4,1)S(1)}, f32[2,512,768]{2,1,0:T(8,12...) while((s32[]{:T(128)}, f32[2,512]{1,0:T(2,128)S(1)}, ...), condition=%wide.region_17.18_spmd, body=%wide.region_15.17_spmd.sunk | while | flops 203292160 | bytes 14430377 | solution.py:117
  172.5 2.0 convert_reduce_fusion.3
  174.9 0.9 copy-done.4
  176.4 2.0 convert_reduce_fusion.3
  178.8 0.9 copy-done.4
  179.9 29.7 %psum.15 = f32[16,1,64]{2,1,0:T(1,128)} all-reduce(f32[16,1,64]{2,1,0:T(1,128)S(1)} %all_to_all.40), channel_id=1, replica_groups=mesh['cell'=16,'sub'=16] {'sub'}, use_global_device_ids=true, to_apply=%region_20.21 | all-reduce | flops 1024 | bytes 8192 | tf_op jit(solution)/shard_map/psum | solution.py:120
  209.6 22.7 %all-to-all-start.5 = ((f32[16,1,64]{2,1,0:T(1,128)}), f32[16,1,64]{2,1,0:T(1,128)S(1)}, u32[]{:S(2)}, u32[]{:S(2)}) async-start(f32[16,1,64]{2,1,0:T(1,128)} %psum.15), calls=%async_computation.5 | async-start | bytes 16384 | tf_op jit(solution)/shard_map/all_to_all | solution.py:125
  232.4 6.9 %all-to-all-done.5 = f32[16,1,64]{2,1,0:T(1,128)S(1)} async-done(((f32[16,1,64]{2,1,0:T(1,128)}), f32[16,1,64]{2,1,0:T(1,128)S(1)}, u32[]{:S(2)}, u32[]{:S(2)}) %all-to-all-start.5) | async-done | bytes 4128 | tf_op jit(solution)/shard_map/all_to_all | solution.py:125
  239.3 10.1 %all_to_all.49 = f32[16,1,64]{2,1,0:T(1,128)S(1)} all-to-all(f32[16,1,64]{2,1,0:T(1,128)S(1)} %all_to_all.37), channel_id=1, replica_groups=mesh['cell'=16,'sub'=16] {'cell'}, dimensions={0} | all-to-all | bytes 8192 | tf_op jit(solution)/shard_map/all_to_all | solution.py:128
  249.4 30.5 %all-reduce.2.cloned.1.call-done = f32[16,64,256]{2,1,0:T(8,128)} async-done(((f32[16,64,256]{2,1,0:T(8,128)}), f32[16,64,256]{2,1,0:T(8,128)}) %all-reduce.2.cloned.1.call-update) | async-done | bytes 1048592 | tf_op jit(solution)/shard_map/psum | solution.py:120
  279.9 9.2 %all-to-all-start.4 = ((f32[16,64,256]{2,1,0:T(8,128)}), f32[16,64,256]{2,1,0:T(8,128)S(1)}, u32[]{:S(2)}, u32[]{:S(2)}) async-start(f32[16,64,256]{2,1,0:T(8,128)} %all-reduce.2.cloned.1.call-done), calls=%async_computation.4 | async-start | bytes 2097152 | tf_op jit(solution)/shard_map/all_to_all | solution.py:122
  290.7 2.3 gather_fusion.2
  293.9 2.3 gather_fusion
  296.6 20.5 %all-to-all-done.4 = f32[16,64,256]{2,1,0:T(8,128)S(1)} async-done(((f32[16,64,256]{2,1,0:T(8,128)}), f32[16,64,256]{2,1,0:T(8,128)S(1)}, u32[]{:S(2)}, u32[]{:S(2)}) %all-to-all-start.4) | async-done | bytes 1048608 | tf_op jit(solution)/shard_map/all_to_all | solution.py:122
  317.1 1.6 gather_fusion.1
  319.7 0.8 divide_convert_fusion
  (112 shorter events, 20.8 us)
Async XLA Ops:
  6.5 26.6 %copy-start.6 = (s32[256,2,16]{0,2,1:T(8,128)S(1)}, s32[256,2,16]{0,2,1:T(8,128)}, u32[]{:S(2)}) copy-start(s32[256,2,16]{0,2,1:T(8,128)} %param.16) | copy-start | bytes 98308
  6.5 32.9 %copy-start.5 = (s32[32,4,384]{2,1,0:T(4,128)S(1)}, s32[32,4,384]{2,1,0:T(4,128)}, u32[]{:S(2)}) copy-start(s32[32,4,384]{2,1,0:T(4,128)} %param.19) | copy-start | bytes 589828
  6.5 112.0 %all-gather.2.cloned.1.call-start = ((), (), s32[]{:S(2)}) async-start(), calls=%async_computation.6 | async-start | bytes 2228224 | tf_op jit(solution)/shard_map/all_gather | solution.py:81
  36.0 31.4 %all-to-all-start.2 = ((bf16[16,2,512]{2,1,0:T(2,128)(2,1)}), bf16[16,2,512]{2,1,0:T(2,128)(2,1)S(1)}, u32[]{:S(2)}, u32[]{:S(2)}) async-start(bf16[16,2,512]{2,1,0:T(2,128)(2,1)} %reshape.285), calls=%async_computation.2 | async-start | bytes 65536 | tf_op jit(solution)/shard_map/all_to_all | solution.py:73
  53.7 2.5 copy-start.8
  67.4 31.0 %all-to-all-start.1 = ((bf16[16,2,24576]{2,1,0:T(2,128)(2,1)}), bf16[16,2,24576]{2,1,0:T(2,128)(2,1)}, u32[]{:S(2)}, u32[]{:S(2)}) async-start(bf16[16,2,24576]{2,1,0:T(2,128)(2,1)} %reshape.283), calls=%async_computation.1 | async-start | bytes 3145728 | tf_op jit(solution)/shard_map/all_to_all | solution.py:88
  74.2 205.7 %all-reduce.2.cloned.1.call-start = ((), (), s32[]{:S(2)}) async-start(), calls=%async_computation.7 | async-start | bytes 2097152 | tf_op jit(solution)/shard_map/psum | solution.py:120
  114.2 2.7 copy-start
  118.5 4.6 %copy-start.2 = (pred[2,512,768]{1,2,0:T(8,128)(4,1)S(1)}, pred[2,512,768]{1,2,0:T(8,128)(4,1)}, u32[]{:S(2)}) copy-start(pred[2,512,768]{1,2,0:T(8,128)(4,1)} %custom-call.9) | copy-start | bytes 2359300
  123.2 48.6 %copy-start.1 = (bf16[32,24,256]{2,1,0:T(8,128)(2,1)S(1)}, bf16[32,24,256]{2,1,0:T(8,128)(2,1)}, u32[]{:S(2)}) copy-start(bf16[32,24,256]{2,1,0:T(8,128)(2,1)} %param.21) | copy-start | bytes 1179652
  171.8 2.6 copy-start.3
  174.8 1.0 copy-start.4
  175.8 2.6 copy-start.3
  178.8 1.0 copy-start.4
  179.8 109.4 %copy-start.7 = (s32[256,2]{0,1:T(2,128)S(1)}, s32[256,2]{0,1:T(2,128)}, u32[]{:S(2)}) copy-start(s32[256,2]{0,1:T(2,128)} %get-tuple-element.324) | copy-start | bytes 6148
  209.6 29.6 %all-to-all-start.5 = ((f32[16,1,64]{2,1,0:T(1,128)}), f32[16,1,64]{2,1,0:T(1,128)S(1)}, u32[]{:S(2)}, u32[]{:S(2)}) async-start(f32[16,1,64]{2,1,0:T(1,128)} %psum.15), calls=%async_computation.5 | async-start | bytes 16384 | tf_op jit(solution)/shard_map/all_to_all | solution.py:125
  279.9 37.2 %all-to-all-start.4 = ((f32[16,64,256]{2,1,0:T(8,128)}), f32[16,64,256]{2,1,0:T(8,128)S(1)}, u32[]{:S(2)}, u32[]{:S(2)}) async-start(f32[16,64,256]{2,1,0:T(8,128)} %all-reduce.2.cloned.1.call-done), calls=%async_computation.4 | async-start | bytes 2097152 | tf_op jit(solution)/shard_map/all_to_all | solution.py:122
Sparse Core Ops, SparseCore 0:
  33.3 48.4 all-gather.1
  179.9 99.9 all-reduce.1
where the time goes:
time: 329 us; the launch traced here: 327 us
  blocking collectives  88.8 us (27%)
  waiting for transfers between devices  80.1 us (24%)
  local copies, waits for them, and re-layouts  61.6 us (19%)
  starting transfers between devices  42.3 us (13%)
  matrix products  22.6 us (7%)
  other arithmetic  17.9 us (5%)
  between operations  13.7 us (4%)
    psum x1, waiting for transfers between devices, local(): part_sum, mass_sum = lax.psum((part, mass), 'sub')  30.5 us
    pmax x1, blocking collectives, local(): peak = lax.pmax(local_peak.reshape(total), 'sub')  30.3 us
    psum x1, blocking collectives, local(): part_sum, mass_sum = lax.psum((part, mass), 'sub')  29.7 us
    all_to_all x1, starting transfers between devices, local(): lax.all_to_all(mass_sum.reshape(groups, capacity), 'cell', split_axis=0,...  22.7 us
    all_to_all x1, waiting for transfers between devices, local(): lax.all_to_all(local_vectors, 'sub', split_axis=2, concat_axis=0, tiled=T...  22.2 us
    all_to_all x1, waiting for transfers between devices, local(): lax.all_to_all(part_sum.reshape(groups, capacity, -1), 'cell', split_axis...  20.5 us
    unnamed x26, local copies, waits for them, and re-layouts  19.1 us
    all_to_all x1, blocking collectives, local(): lax.all_to_all(buffer.reshape(groups, capacity, -1), 'cell', split_axis=0...  18.6 us
  transfers between devices with their start and end apart: 6, of which 4 were waited for; matrix products, arithmetic and copies ran while one was open for 18% of the time, Pallas kernels for 0%

commit v1 on v0

v1 whole, which is shorter than its diff:
```python
import jax
import jax.numpy as jnp
from jax import lax
from jax.sharding import PartitionSpec as P

CAP = 64


score_scale = 0.3
floor_score = -1e30


def slot_table(probe_groups, groups, capacity):
    marks = (probe_groups[:, :, None] == jnp.arange(groups, dtype=jnp.int32)[None, None, :]).astype(
        jnp.int32
    )
    routed = jnp.sum(marks, axis=1)
    earlier = jnp.cumsum(routed, axis=0) - routed
    position = jnp.sum(marks * earlier[:, None, :], axis=2)
    return probe_groups * capacity + position


def pack_slots(rows, probe_cells, slots, total):
    flat = slots.reshape(-1)
    doubled = jnp.repeat(rows, 2, axis=0)
    buffer = jnp.zeros((total, rows.shape[1]), rows.dtype).at[flat].set(doubled)
    named = probe_cells.reshape(flat.shape[0], -1).astype(jnp.bfloat16)
    cell_marks = jnp.full((total, probe_cells.shape[2]), -1.0, jnp.bfloat16).at[flat].set(named)
    return (buffer, cell_marks)


def decode(coarse, codebooks, codes, parts):
    cell_count, sub_count, row_count = codes.shape
    width = codebooks.shape[1]
    rows_part = row_count // parts
    grouped = codes.reshape(cell_count, sub_count, parts, rows_part)
    grouped = jnp.transpose(grouped, (2, 1, 0, 3)).reshape(parts, sub_count, cell_count * rows_part)
    centroid_ids = jnp.arange(codebooks.shape[2], dtype=jnp.int32)
    onehot = (grouped[..., None] == centroid_ids).astype(jnp.bfloat16)
    books = jnp.broadcast_to(codebooks[None], (parts,) + codebooks.shape)
    picked = lax.dot_general(
        books, onehot, (((3,), (3,)), ((0, 1), (0, 1))), preferred_element_type=jnp.float32
    )
    picked = picked.reshape(parts, sub_count * width, cell_count, rows_part)
    recon = picked + coarse.T.astype(jnp.float32)[None, :, :, None]
    return recon.astype(jnp.bfloat16).reshape(parts, sub_count * width, cell_count * rows_part)


def local(queries, probe_groups, probe_cells, coarse, codebooks, codes, lengths, payload):
    groups = lax.axis_size("cell")
    parts = lax.axis_size("sub")
    capacity = CAP
    total = groups * capacity
    cell_dev = codes.shape[0]
    pw = payload.shape[2]
    chunk = pw // parts

    local_vectors = decode(coarse, codebooks, codes, parts)
    decoded = lax.all_to_all(local_vectors, "sub", split_axis=0, concat_axis=0, tiled=True)
    decoded = decoded.reshape(-1, decoded.shape[2])

    slots = slot_table(probe_groups, groups, capacity)
    buffer, cell_marks = pack_slots(queries, probe_cells, slots, total)
    arrived = lax.all_to_all(
        buffer.reshape(groups, capacity, -1), "cell", split_axis=0, concat_axis=0, tiled=True
    )
    arrived_cells = lax.all_to_all(
        cell_marks.reshape(groups, capacity, -1), "cell", split_axis=0, concat_axis=0, tiled=True
    )
    full_rows = lax.all_gather(arrived.reshape(total, -1), "sub", axis=1, tiled=True)
    cell_ids = arrived_cells.reshape(total, -1).astype(jnp.int32)
    probed = jnp.any(
        cell_ids[:, :, None] == jnp.arange(cell_dev, dtype=jnp.int32)[None, None, :], axis=1
    )

    row_local = payload.shape[1]
    sq_norm = jnp.sum(jnp.square(decoded.astype(jnp.float32)), axis=0)
    first_row = lax.axis_index("sub") * row_local
    live = (first_row + jnp.arange(row_local, dtype=jnp.int32))[None, :] < lengths[:, None]
    keep = (probed[:, :, None] & live[None, :, :]).reshape(total, -1)
    table = payload.reshape(-1, pw)

    raw = jnp.dot(full_rows, decoded, preferred_element_type=jnp.float32)
    values = (raw - 0.5 * sq_norm[None, :]) * score_scale
    local_peak = jnp.max(jnp.where(keep, values, floor_score), axis=1)
    peak = jnp.max(lax.all_gather(local_peak, "sub", axis=0), axis=0)

    weights = jnp.where(keep, jnp.exp(values - peak[:, None]), 0.0).astype(jnp.bfloat16)
    mass = jnp.sum(weights.astype(jnp.float32), axis=1)
    part_t = lax.dot_general(
        table, weights, (((0,), (1,)), ((), ())), preferred_element_type=jnp.float32
    )
    sendable = jnp.concatenate(
        [
            part_t.reshape(parts, chunk, total),
            jnp.broadcast_to(mass[None, None, :], (parts, 1, total)),
        ],
        axis=1,
    )
    pieces = lax.all_to_all(sendable, "sub", split_axis=0, concat_axis=0, tiled=True)
    reduced = jnp.sum(pieces, axis=0)
    outgoing = jnp.concatenate([reduced, peak[None, :]], axis=0)
    back = lax.all_to_all(
        outgoing.reshape(chunk + 2, groups, capacity), "cell", split_axis=1, concat_axis=1, tiled=True
    )
    back = back.reshape(chunk + 2, total)
    picked = back[:, slots]
    parts_back = picked[:chunk]
    masses = picked[chunk]
    peaks = picked[chunk + 1]
    top = jnp.max(peaks, axis=1, keepdims=True)
    scale = jnp.exp(peaks - top)
    upper = jnp.sum(scale[None, :, :] * parts_back, axis=2)
    lower = jnp.sum(scale * masses, axis=1)
    pooled = (upper / lower[None, :]).astype(jnp.bfloat16)
    return lax.all_gather(pooled, "sub", axis=0, tiled=True).T


def solution(mesh):
    placed = (
        P("cell", "sub"),
        P("cell", None),
        P("cell", None, None),
        P("cell", "sub"),
        P("sub", None, None),
        P("cell", "sub", None),
        P("cell"),
        P("cell", "sub", None),
    )
    return jax.shard_map(
        local, mesh=mesh, in_specs=placed, out_specs=P("cell", None), check_vma=False
    )
```

time: 329 us -> 199 us (0.60)
  blocking collectives: 88.8 us -> 35.1 us
  local copies, waits for them, and re-layouts: 61.6 us -> 15.3 us
  waiting for transfers between devices: 80.1 us -> 58 us
  other arithmetic: 17.9 us -> 10.4 us
    all_gather x0 -> x2, blocking collectives: none -> 35.1 us  [the longest x1 18.3 us: local(): peak = jnp.max(lax.all_gather(local_peak, 'sub', axis=0), axis=0)]
    psum x1 -> x0, waiting for transfers between devices: 30.5 us -> none  [local(): part_sum, mass_sum = lax.psum((part, mass), 'sub')]
    pmax x1 -> x0, blocking collectives: 30.3 us -> none  [local(): peak = lax.pmax(local_peak.reshape(total), 'sub')]
    psum x1 -> x0, blocking collectives: 29.7 us -> none  [local(): part_sum, mass_sum = lax.psum((part, mass), 'sub')]
    all_to_all x2 -> x0, blocking collectives: 28.8 us -> none  [the longest x1 18.6 us: local(): lax.all_to_all(buffer.reshape(groups, capacity, -1), 'cell', split_axis=0...]
    unnamed x26 -> x18, local copies, waits for them, and re-layouts: 19.1 us -> 4.63 us
    all_gather x1, waiting for transfers between devices: 0.01 us -> 9.33 us  [local(): lax.all_gather(arrived.reshape(total, -1), 'sub', axis=1, tiled=True)]
    all_to_all x5 -> x2, local copies, waits for them, and re-layouts: 7.32 us -> 0.75 us  [local(): lax.all_to_all(outgoing.reshape(chunk + 2, groups, capacity), 'cell', spl...]
  transfers between devices with their start and end apart: 6 -> 6, of which waited for: 4 -> 5; matrix products, arithmetic and copies ran while one was open for 18% -> 13% of each run, Pallas kernels for 0% -> 0%
where the time goes in v1:
time: 199 us; the launch traced here: 195 us
  waiting for transfers between devices  58 us (29%)
  starting transfers between devices  39.6 us (20%)
  blocking collectives  35.1 us (18%)
  matrix products  22.8 us (11%)
  local copies, waits for them, and re-layouts  15.3 us (8%)
  between operations  13.8 us (7%)
  other arithmetic  10.4 us (5%)
    all_to_all x1, waiting for transfers between devices, local(): lax.all_to_all(local_vectors, 'sub', split_axis=0, concat_axis=0, tiled=T...  22.3 us
    all_gather x1, blocking collectives, local(): peak = jnp.max(lax.all_gather(local_peak, 'sub', axis=0), axis=0)  18.3 us
    all_gather x1, blocking collectives, local(): return lax.all_gather(pooled, 'sub', axis=0, tiled=True).T  16.9 us
    dot_general x1, matrix products, decode(): lax.dot_general(books, onehot, (((3,), (3,)), ((0, 1), (0, 1))), preferre...  16.6 us
    all_to_all x1, starting transfers between devices, local(): lax.all_to_all(outgoing.reshape(chunk + 2, groups, capacity), 'cell', spl...  15.3 us
    all_to_all x1, waiting for transfers between devices, local(): lax.all_to_all(sendable, 'sub', split_axis=0, concat_axis=0, tiled=True)  15.2 us
    all_to_all x1, starting transfers between devices, local(): lax.all_to_all(buffer.reshape(groups, capacity, -1), 'cell', split_axis=0...  9.97 us
    all_gather x1, waiting for transfers between devices, local(): lax.all_gather(arrived.reshape(total, -1), 'sub', axis=1, tiled=True)  9.33 us
  transfers between devices with their start and end apart: 6, of which 5 were waited for; matrix products, arithmetic and copies ran while one was open for 13% of the time, Pallas kernels for 0%

profile of v1, /device:TPU:1, one launch (start us, length us, event | category | flops | bytes accessed | tf_op | source)
XLA Modules:
  0.0 195.0 jit_solution(7045192482870616641)
XLA Ops:
  6.5 0.7 convert_reduce_fusion.1
  7.3 0.6 reduce-window.6
  7.9 0.2 slice_reduce_fusion
  8.2 0.7 select_reduce_fusion.1
  8.9 0.7 compare_select_fusion.1
  9.6 0.1 copy.85
  9.7 0.1 reshape.141
  9.9 0.9 copy.90
  10.8 1.8 scatter_custom_fusion.1
  12.7 0.9 reshape.186
  13.6 10.0 %all-to-all-start.1 = ((bf16[16,2,2048]{2,1,0:T(2,128)(2,1)}), bf16[16,2,2048]{2,1,0:T(2,128)(2,1)S(1)}, u32[]{:S(2)}, u32[]{:S(2)}) async-start(bf16[16,2,2048]{2,1,0:T(2,128)(2,1)} %reshape.186), calls=%async_computation.1 | async-start | bytes 262144 | tf_op jit(solution)/shard_map/all_to_all | solution.py:64
  23.5 0.9 copy.92
  24.5 0.6 reshape.146
  25.2 0.3 copy.104
  25.5 0.6 reshape.180
  26.3 1.8 scatter_custom_fusion
  28.1 0.1 copy.88
  28.3 0.7 reshape.188
  29.0 3.4 %all-to-all-done.1 = bf16[16,2,2048]{2,1,0:T(2,128)(2,1)S(1)} async-done(((bf16[16,2,2048]{2,1,0:T(2,128)(2,1)}), bf16[16,2,2048]{2,1,0:T(2,128)(2,1)S(1)}, u32[]{:S(2)}, u32[]{:S(2)}) %all-to-all-start.1) | async-done | bytes 131104 | tf_op jit(solution)/shard_map/all_to_all | solution.py:64
  32.4 3.8 %all-to-all-start = ((bf16[16,2,512]{2,1,0:T(2,128)(2,1)}), bf16[16,2,512]{2,1,0:T(2,128)(2,1)S(1)}, u32[]{:S(2)}, u32[]{:S(2)}) async-start(bf16[16,2,512]{2,1,0:T(2,128)(2,1)} %reshape.188), calls=%async_computation | async-start | bytes 65536 | tf_op jit(solution)/shard_map/all_to_all | solution.py:67
  36.3 0.2 reshape.187
  36.5 0.8 copy.103
  37.3 0.1 copy.95
  37.6 16.6 %fusion = f32[16,4,768,16]{2,3,1,0:T(8,128)S(1)} fusion(s32[16,4,768]{2,1,0:T(4,128)S(1)} %reshape.180, bf16[16,4,16,256]{3,2,1,0:T(8,128)(2,1)S(1)} %fusion.23), kind=kOutput, calls=%fused_computation.4 | convolution fusion | flops 415236096 | bytes 3866624 | tf_op jit(solution)/shard_map/dot_general | solution.py:41
  54.2 1.5 fusion.2
  55.7 6.8 %all-to-all-start.2 = ((bf16[16,64,768]{2,1,0:T(8,128)(2,1)}), bf16[16,64,768]{2,1,0:T(8,128)(2,1)S(1)}, u32[]{:S(2)}, u32[]{:S(2)}) async-start(bf16[16,64,768]{2,1,0:T(8,128)(2,1)} %fusion.2), calls=%async_computation.2 | async-start | bytes 3145728 | tf_op jit(solution)/shard_map/all_to_all | solution.py:59
  63.0 0.3 fusion.3
  63.3 22.3 %all-to-all-done.2 = bf16[16,64,768]{2,1,0:T(8,128)(2,1)S(1)} async-done(((bf16[16,64,768]{2,1,0:T(8,128)(2,1)}), bf16[16,64,768]{2,1,0:T(8,128)(2,1)S(1)}, u32[]{:S(2)}, u32[]{:S(2)}) %all-to-all-start.2) | async-done | bytes 1572896 | tf_op jit(solution)/shard_map/all_to_all | solution.py:59
  85.6 0.4 multiply_reduce_fusion
  86.0 9.3 %all-gather.3.cloned.1.call-done = bf16[1024,1024]{0,1:T(8,128)(2,1)} async-done(((bf16[1024,64]{0,1:T(8,128)(2,1)}), bf16[1024,1024]{0,1:T(8,128)(2,1)}) %all-gather.3.cloned.1.call-update) | async-done | bytes 2097168 | tf_op jit(solution)/shard_map/all_gather | solution.py:70
  95.4 5.5 %select_reduce_fusion = (f32[1024]{0:T(1024)S(1)}, f32[1024,768]{0,1:T(8,128)}) fusion(f32[768]{0:T(1024)S(1)} %broadcast_multiply_fusion, pred[768]{0:T(1024)(128)(4,1)S(1)} %lt.43, pred[1024,32]{0,1:T(8,128)(4,1)S(1)} %fusion.3, bf16[1024,1024]{0,1:T(8,128)(2,1)} %all-gather.3.cloned.1.call-done, bf16[1024,768]{1,0:T(8,128)(2,1)S(1)} %bitcast.86), kind=kOutput, calls=%fused_computation.10 | convolution fusion | flops 1614543872 | bytes 6856448 | tf_op jit(solution)/shard_map/dot_general | solution.py:83
  100.9 18.3 %all-gather = f32[16384]{0:T(1024)S(1)} all-gather(f32[1024]{0:T(1024)S(1)} %get-tuple-element.9), channel_id=2, replica_groups=mesh['cell'=16,'sub'=16] {'sub'}, dimensions={0}, use_global_device_ids=true | all-gather | bytes 69632 | tf_op jit(solution)/shard_map/all_gather | solution.py:86
  119.2 3.0 %convert_reduce_fusion = (f32[1024]{0:T(1024)S(1)}, bf16[1024,768]{0,1:T(8,128)(2,1)S(1)}) fusion(f32[1024]{0:T(1024)S(1)} %reduce_max.28, f32[1024,768]{0,1:T(8,128)} %get-tuple-element.10, f32[768]{0:T(1024)S(1)} %broadcast_multiply_fusion, pred[768]{0:T(1024)(128)(4,1)S(1)} %lt.43, pred[1024,32]{0,1:T(8,128)(4,1)S(1)} %fusion.3), kind=kLoop, calls=%fused_computation.8 | loop fusion | flops 6290432 | bytes 4763392 | tf_op jit(solution)/shard_map/reduce_sum | solution.py:89
  122.2 0.6 fusion.14
  122.9 1.3 pad_maximum_fusion
  124.2 3.8 %all-to-all-start.3 = ((f32[16,17,1024]{2,1,0:T(8,128)}), f32[16,17,1024]{2,1,0:T(8,128)S(1)}, u32[]{:S(2)}, u32[]{:S(2)}) async-start(f32[16,17,1024]{2,1,0:T(8,128)} %pad_maximum_fusion), calls=%async_computation.3 | async-start | bytes 3145728 | tf_op jit(solution)/shard_map/all_to_all | solution.py:100
  128.0 15.2 %all-to-all-done.3 = f32[16,17,1024]{2,1,0:T(8,128)S(1)} async-done(((f32[16,17,1024]{2,1,0:T(8,128)}), f32[16,17,1024]{2,1,0:T(8,128)S(1)}, u32[]{:S(2)}, u32[]{:S(2)}) %all-to-all-start.3) | async-done | bytes 1114144 | tf_op jit(solution)/shard_map/all_to_all | solution.py:100
  143.5 0.8 reshape.190
  144.3 15.3 %all-to-all-start.4 = ((f32[16,1,1152]{2,1,0:T(1,128)}), f32[16,1,1152]{2,1,0:T(1,128)S(1)}, u32[]{:S(2)}, u32[]{:S(2)}) async-start(f32[16,1,1152]{2,1,0:T(1,128)} %reshape.190), calls=%async_computation.4 | async-start | bytes 147456 | tf_op jit(solution)/shard_map/all_to_all | solution.py:103
  159.6 0.1 copy.98
  159.7 0.1 reshape.155
  159.9 7.6 %all-to-all-done.4 = f32[16,1,1152]{2,1,0:T(1,128)S(1)} async-done(((f32[16,1,1152]{2,1,0:T(1,128)}), f32[16,1,1152]{2,1,0:T(1,128)S(1)}, u32[]{:S(2)}, u32[]{:S(2)}) %all-to-all-start.4) | async-done | bytes 73760 | tf_op jit(solution)/shard_map/all_to_all | solution.py:103
  167.6 0.5 broadcast.82
  168.1 0.8 reduce.4
  169.0 0.2 copy.97
  169.2 1.0 gather_fusion
  170.5 16.9 %all_gather.15 = bf16[256,256]{1,0:T(8,128)(2,1)S(1)} all-gather(bf16[16,256]{1,0:T(8,128)(2,1)S(1)} %divide_convert_fusion), channel_id=1, replica_groups=mesh['cell'=16,'sub'=16] {'sub'}, dimensions={0}, use_global_device_ids=true | all-gather | bytes 139264 | tf_op jit(solution)/shard_map/all_gather | solution.py:116
  187.4 0.8 copy.100
  (51 shorter events, 1.7 us)
Async XLA Ops:
  6.5 115.6 %copy-start = (bf16[32,24,256]{2,1,0:T(8,128)(2,1)S(1)}, bf16[32,24,256]{2,1,0:T(8,128)(2,1)}, u32[]{:S(2)}) copy-start(bf16[32,24,256]{2,1,0:T(8,128)(2,1)} %param.15) | copy-start | bytes 1179652
  9.7 16.4 %copy-start.2 = (s32[256,2,16]{0,2,1:T(8,128)S(1)}, s32[256,2,16]{0,2,1:T(8,128)}, u32[]{:S(2)}) copy-start(s32[256,2,16]{0,2,1:T(8,128)} %param.10) | copy-start | bytes 98308
  13.6 18.9 %all-to-all-start.1 = ((bf16[16,2,2048]{2,1,0:T(2,128)(2,1)}), bf16[16,2,2048]{2,1,0:T(2,128)(2,1)S(1)}, u32[]{:S(2)}, u32[]{:S(2)}) async-start(bf16[16,2,2048]{2,1,0:T(2,128)(2,1)} %reshape.186), calls=%async_computation.1 | async-start | bytes 262144 | tf_op jit(solution)/shard_map/all_to_all | solution.py:64
  24.5 12.8 %copy-start.3 = (bf16[32,64]{1,0:T(8,128)(2,1)S(1)}, bf16[32,64]{1,0:T(8,128)(2,1)}, u32[]{:S(2)}) copy-start(bf16[32,64]{1,0:T(8,128)(2,1)} %param.11) | copy-start | bytes 12292
  25.1 12.3 %copy-start.1 = (bf16[4,16,256]{2,1,0:T(8,128)(2,1)S(1)}, bf16[4,16,256]{2,1,0:T(8,128)(2,1)}, u32[]{:S(2)}) copy-start(bf16[4,16,256]{2,1,0:T(8,128)(2,1)} %param.12) | copy-start | bytes 98308
  32.4 23.3 %all-to-all-start = ((bf16[16,2,512]{2,1,0:T(2,128)(2,1)}), bf16[16,2,512]{2,1,0:T(2,128)(2,1)S(1)}, u32[]{:S(2)}, u32[]{:S(2)}) async-start(bf16[16,2,512]{2,1,0:T(2,128)(2,1)} %reshape.188), calls=%async_computation | async-start | bytes 65536 | tf_op jit(solution)/shard_map/all_to_all | solution.py:67
  36.2 59.2 %all-gather.3.cloned.1.call-start = ((), (), s32[]{:S(2)}) async-start(), calls=%async_computation.5 | async-start | bytes 2228224 | tf_op jit(solution)/shard_map/all_gather | solution.py:70
  54.2 8.4 %copy-start.4 = (s32[32]{0:T(128)S(1)}, s32[32]{0:T(128)}, u32[]{:S(2)}) copy-start(s32[32]{0:T(128)} %param.14) | copy-start | bytes 388
  55.7 29.9 %all-to-all-start.2 = ((bf16[16,64,768]{2,1,0:T(8,128)(2,1)}), bf16[16,64,768]{2,1,0:T(8,128)(2,1)S(1)}, u32[]{:S(2)}, u32[]{:S(2)}) async-start(bf16[16,64,768]{2,1,0:T(8,128)(2,1)} %fusion.2), calls=%async_computation.2 | async-start | bytes 3145728 | tf_op jit(solution)/shard_map/all_to_all | solution.py:59
  124.2 19.1 %all-to-all-start.3 = ((f32[16,17,1024]{2,1,0:T(8,128)}), f32[16,17,1024]{2,1,0:T(8,128)S(1)}, u32[]{:S(2)}, u32[]{:S(2)}) async-start(f32[16,17,1024]{2,1,0:T(8,128)} %pad_maximum_fusion), calls=%async_computation.3 | async-start | bytes 3145728 | tf_op jit(solution)/shard_map/all_to_all | solution.py:100
  144.3 23.3 %all-to-all-start.4 = ((f32[16,1,1152]{2,1,0:T(1,128)}), f32[16,1,1152]{2,1,0:T(1,128)S(1)}, u32[]{:S(2)}, u32[]{:S(2)}) async-start(f32[16,1,1152]{2,1,0:T(1,128)} %reshape.190), calls=%async_computation.4 | async-start | bytes 147456 | tf_op jit(solution)/shard_map/all_to_all | solution.py:103
Sparse Core Ops, SparseCore 0:
  39.4 55.8 all-gather.2

commit v2 on v1

--- a/solution.py
+++ b/solution.py
@@ -46,6 +46,12 @@
     return recon.astype(jnp.bfloat16).reshape(parts, sub_count * width, cell_count * rows_part)
 
 
+def gather_by_exchange(x, axis):
+    count = lax.axis_size(axis)
+    copies = jnp.broadcast_to(x[None], (count,) + x.shape)
+    return lax.all_to_all(copies, axis, split_axis=0, concat_axis=0, tiled=True)
+
+
 def local(queries, probe_groups, probe_cells, coarse, codebooks, codes, lengths, payload):
     groups = lax.axis_size("cell")
     parts = lax.axis_size("sub")
@@ -67,7 +73,7 @@
     arrived_cells = lax.all_to_all(
         cell_marks.reshape(groups, capacity, -1), "cell", split_axis=0, concat_axis=0, tiled=True
     )
-    full_rows = lax.all_gather(arrived.reshape(total, -1), "sub", axis=1, tiled=True)
+    query_parts = gather_by_exchange(arrived.reshape(total, -1), "sub")
     cell_ids = arrived_cells.reshape(total, -1).astype(jnp.int32)
     probed = jnp.any(
         cell_ids[:, :, None] == jnp.arange(cell_dev, dtype=jnp.int32)[None, None, :], axis=1
@@ -80,10 +86,15 @@
     keep = (probed[:, :, None] & live[None, :, :]).reshape(total, -1)
     table = payload.reshape(-1, pw)
 
-    raw = jnp.dot(full_rows, decoded, preferred_element_type=jnp.float32)
+    raw = jnp.einsum(
+        "sqd,sdr->qr",
+        query_parts,
+        decoded.reshape(parts, -1, decoded.shape[1]),
+        preferred_element_type=jnp.float32,
+    )
     values = (raw - 0.5 * sq_norm[None, :]) * score_scale
     local_peak = jnp.max(jnp.where(keep, values, floor_score), axis=1)
-    peak = jnp.max(lax.all_gather(local_peak, "sub", axis=0), axis=0)
+    peak = jnp.max(gather_by_exchange(local_peak, "sub"), axis=0)
 
     weights = jnp.where(keep, jnp.exp(values - peak[:, None]), 0.0).astype(jnp.bfloat16)
     mass = jnp.sum(weights.astype(jnp.float32), axis=1)
@@ -113,7 +124,7 @@
     upper = jnp.sum(scale[None, :, :] * parts_back, axis=2)
     lower = jnp.sum(scale * masses, axis=1)
     pooled = (upper / lower[None, :]).astype(jnp.bfloat16)
-    return lax.all_gather(pooled, "sub", axis=0, tiled=True).T
+    return gather_by_exchange(pooled, "sub").reshape(pw, -1).T
 
 
 def solution(mesh):

time: 199 us -> 204 us (1.025); the launches traced: 195 us -> 203 us
  waiting for transfers between devices: 58 us -> 79 us
  blocking collectives: 35.1 us -> 21.4 us
  between operations: 13.8 us -> 0.35 us
  local copies, waits for them, and re-layouts: 15.3 us -> 25 us
    all_gather x2 -> x0, blocking collectives: 35.1 us -> none  [the longest x1 18.3 us: local(): peak = jnp.max(lax.all_gather(local_peak, 'sub', axis=0), axis=0)]
    all_to_all x0 -> x1, waiting for transfers between devices: none -> 23.9 us  [gather_by_exchange(): return lax.all_to_all(copies, axis, split_axis=0, concat_axis=0, tiled=True)]
    all_to_all x0 -> x2, blocking collectives: none -> 21.4 us  [gather_by_exchange(): return lax.all_to_all(copies, axis, split_axis=0, concat_axis=0, tiled=True)]
    all_gather x1 -> x0, waiting for transfers between devices: 9.33 us -> none  [local(): lax.all_gather(arrived.reshape(total, -1), 'sub', axis=1, tiled=True)]
    all_to_all x1, starting transfers between devices: 3.78 us -> 9.97 us  [local(): lax.all_to_all(cell_marks.reshape(groups, capacity, -1), 'cell', split_ax...]
    all_to_all x1, starting transfers between devices: 15.3 us -> 9.15 us  [local(): lax.all_to_all(outgoing.reshape(chunk + 2, groups, capacity), 'cell', spl...]
    all_to_all x0 -> x1, starting transfers between devices: none -> 4.43 us  [gather_by_exchange(): return lax.all_to_all(copies, axis, split_axis=0, concat_axis=0, tiled=True)]
    all_to_all x1, waiting for transfers between devices: 15.2 us -> 18.6 us  [local(): lax.all_to_all(sendable, 'sub', split_axis=0, concat_axis=0, tiled=True)]
  transfers between devices with their start and end apart: 6 -> 6, of which waited for: 5 -> 5; matrix products, arithmetic and copies ran while one was open for 13% -> 18% of each run, Pallas kernels for 0% -> 0%
where the time goes in v2:
time: 204 us; the launch traced here: 203 us
  waiting for transfers between devices  79 us (39%)
  starting transfers between devices  41.2 us (20%)
  local copies, waits for them, and re-layouts  25 us (12%)
  matrix products  23.4 us (11%)
  blocking collectives  21.4 us (10%)
  other arithmetic  12.4 us (6%)
    all_to_all x1, waiting for transfers between devices, gather_by_exchange(): return lax.all_to_all(copies, axis, split_axis=0, concat_axis=0, tiled=True)  23.9 us
    all_to_all x1, waiting for transfers between devices, local(): lax.all_to_all(local_vectors, 'sub', split_axis=0, concat_axis=0, tiled=T...  22.5 us
    all_to_all x2, blocking collectives, gather_by_exchange(): return lax.all_to_all(copies, axis, split_axis=0, concat_axis=0, tiled=True)  21.4 us
    all_to_all x1, waiting for transfers between devices, local(): lax.all_to_all(sendable, 'sub', split_axis=0, concat_axis=0, tiled=True)  18.6 us
    dot_general x1, matrix products, decode(): lax.dot_general(books, onehot, (((3,), (3,)), ((0, 1), (0, 1))), preferre...  17.2 us
    all_to_all x1, starting transfers between devices, local(): lax.all_to_all(cell_marks.reshape(groups, capacity, -1), 'cell', split_ax...  9.97 us
    all_to_all x1, starting transfers between devices, local(): lax.all_to_all(outgoing.reshape(chunk + 2, groups, capacity), 'cell', spl...  9.15 us
    unnamed x16, local copies, waits for them, and re-layouts  7.85 us
  transfers between devices with their start and end apart: 6, of which 5 were waited for; matrix products, arithmetic and copies ran while one was open for 18% of the time, Pallas kernels for 0%

profile of v2, /device:TPU:1, one launch (start us, length us, event | category | flops | bytes accessed | tf_op | source)
XLA Modules:
  0.0 202.7 jit_solution(14874532542829000283)
XLA Ops:
  0.0 0.7 convert_reduce_fusion.1
  0.7 0.6 reduce-window.6
  1.3 0.2 slice_reduce_fusion
  1.6 0.7 select_reduce_fusion.1
  2.4 0.7 compare_select_fusion.1
  3.3 0.8 convert_element_type.48
  4.2 1.8 scatter_custom_fusion
  6.2 0.7 reshape.210
  6.9 10.0 %all-to-all-start = ((bf16[16,2,512]{2,1,0:T(2,128)(2,1)}), bf16[16,2,512]{2,1,0:T(2,128)(2,1)}, u32[]{:S(2)}, u32[]{:S(2)}) async-start(bf16[16,2,512]{2,1,0:T(2,128)(2,1)} %reshape.210), calls=%async_computation | async-start | bytes 65536 | tf_op jit(solution)/shard_map/all_to_all | solution.py:73
  16.9 0.9 copy.113
  17.8 0.6 reshape.168
  18.5 0.3 copy.126
  18.8 1.3 reshape.202
  20.2 17.2 %fusion = f32[16,4,768,16]{2,3,1,0:T(8,128)S(1)} fusion(s32[16,4,768]{2,1,0:T(4,128)} %reshape.202, bf16[16,4,16,256]{3,2,1,0:T(8,128)(2,1)S(1)} %fusion.24), kind=kOutput, calls=%fused_computation.4 | convolution fusion | flops 415236096 | bytes 3866624 | tf_op jit(solution)/shard_map/dot_general | solution.py:41
  37.5 0.8 add.47
  38.3 1.8 copy.116
  40.1 1.5 copy.111
  41.5 1.6 broadcast_in_dim.29
  43.1 2.8 %scatter_custom_fusion.1 = bf16[1024,64]{1,0:T(8,128)(2,1)} fusion(s32[512]{0:T(512)S(1)} %bitcast.113, bf16[512,64]{1,0:T(8,128)(2,1)} %bitcast.110, bf16[]{:T(256)} %constant.6.clone.1), kind=kCustom, calls=%fused_computation.20 | custom fusion | bytes 131584 | tf_op jit(solution)/shard_map/scatter | solution.py:26
  45.9 1.8 reshape.208
  47.7 7.2 %all-to-all-start.1 = ((bf16[16,2,2048]{2,1,0:T(2,128)(2,1)}), bf16[16,2,2048]{2,1,0:T(2,128)(2,1)}, u32[]{:S(2)}, u32[]{:S(2)}) async-start(bf16[16,2,2048]{2,1,0:T(2,128)(2,1)} %reshape.208), calls=%async_computation.1 | async-start | bytes 262144 | tf_op jit(solution)/shard_map/all_to_all | solution.py:70
  55.0 2.7 %fusion.2 = bf16[16,64,768]{2,1,0:T(8,128)(2,1)} fusion(f32[16,4,768,16]{2,3,1,0:T(8,128)S(1)} %fusion, f32[64,768]{1,0:T(8,128)} %copy.116), kind=kLoop, calls=%fused_computation.7 | loop fusion | flops 1572864 | bytes 4915200 | tf_op jit(solution)/shard_map/convert_element_type | solution.py:46
  57.6 6.3 %all-to-all-done.1 = bf16[16,2,2048]{2,1,0:T(2,128)(2,1)} async-done(((bf16[16,2,2048]{2,1,0:T(2,128)(2,1)}), bf16[16,2,2048]{2,1,0:T(2,128)(2,1)}, u32[]{:S(2)}, u32[]{:S(2)}) %all-to-all-start.1) | async-done | bytes 131104 | tf_op jit(solution)/shard_map/all_to_all | solution.py:70
  63.9 6.8 %all-to-all-start.3 = ((bf16[16,64,768]{2,1,0:T(8,128)(2,1)}), bf16[16,64,768]{2,1,0:T(8,128)(2,1)S(1)}, u32[]{:S(2)}, u32[]{:S(2)}) async-start(bf16[16,64,768]{2,1,0:T(8,128)(2,1)} %fusion.2), calls=%async_computation.3 | async-start | bytes 3145728 | tf_op jit(solution)/shard_map/all_to_all | solution.py:65
  70.7 1.1 reshape.209
  72.0 22.5 %all-to-all-done.3 = bf16[16,64,768]{2,1,0:T(8,128)(2,1)S(1)} async-done(((bf16[16,64,768]{2,1,0:T(8,128)(2,1)}), bf16[16,64,768]{2,1,0:T(8,128)(2,1)S(1)}, u32[]{:S(2)}, u32[]{:S(2)}) %all-to-all-start.3) | async-done | bytes 1572896 | tf_op jit(solution)/shard_map/all_to_all | solution.py:65
  94.4 1.6 broadcast_in_dim.31
  96.1 4.4 %all-to-all-start.2 = ((bf16[16,1024,64]{1,2,0:T(8,128)(2,1)}), bf16[16,1024,64]{1,2,0:T(8,128)(2,1)}, u32[]{:S(2)}, u32[]{:S(2)}) async-start(bf16[16,1024,64]{1,2,0:T(8,128)(2,1)} %broadcast_in_dim.31), calls=%async_computation.2 | async-start | bytes 4194304 | tf_op jit(solution)/shard_map/all_to_all | solution.py:52
  100.8 0.9 reshape.211
  101.8 0.3 fusion.4
  102.1 0.4 multiply_reduce_fusion
  102.5 23.9 %all-to-all-done.2 = bf16[16,1024,64]{1,2,0:T(8,128)(2,1)} async-done(((bf16[16,1024,64]{1,2,0:T(8,128)(2,1)}), bf16[16,1024,64]{1,2,0:T(8,128)(2,1)}, u32[]{:S(2)}, u32[]{:S(2)}) %all-to-all-start.2) | async-done | bytes 2097184 | tf_op jit(solution)/shard_map/all_to_all | solution.py:52
  126.4 5.5 %select_reduce_fusion = (f32[1024]{0:T(1024)S(1)}, f32[1024,768,1]{0,1,2:T(8,128)}) fusion(f32[768]{0:T(1024)S(1)} %broadcast_multiply_fusion, pred[768]{0:T(1024)(128)(4,1)S(1)} %lt.43, pred[1024,32]{0,1:T(8,128)(4,1)S(1)} %fusion.4, bf16[16,1024,64]{1,2,0:T(8,128)(2,1)} %all-to-all-done.2, bf16[16,64,768]{2,1,0:T(8,128)(2,1)S(1)} %all-to-all-done.3), kind=kOutput, calls=%fused_computation.12 | convolution fusion | flops 1614543872 | bytes 6856448 | tf_op jit(solution)/shard_map/sqd,sdr->qr/dot_general | solution.py:89
  131.9 11.7 %all_to_all.41 = f32[16,1,1024]{2,1,0:T(1,128)S(1)} all-to-all(f32[16,1,1024]{2,1,0:T(1,128)S(1)} %broadcast_in_dim.34), channel_id=1, replica_groups=mesh['cell'=16,'sub'=16] {'sub'}, dimensions={0} | all-to-all | bytes 131072 | tf_op jit(solution)/shard_map/all_to_all | solution.py:52
  143.7 3.0 %convert_reduce_fusion = (f32[1024]{0:T(1024)S(1)}, bf16[1024,768]{0,1:T(8,128)(2,1)S(1)}) fusion(f32[1024]{0:T(1024)S(1)} %reduce_max.28, f32[768]{0:T(1024)S(1)} %broadcast_multiply_fusion, f32[1024,768,1]{0,1,2:T(8,128)} %get-tuple-element.10, pred[768]{0:T(1024)(128)(4,1)S(1)} %lt.43, pred[1024,32]{0,1:T(8,128)(4,1)S(1)} %fusion.4), kind=kLoop, calls=%fused_computation.10 | loop fusion | flops 6290432 | bytes 4763392 | tf_op jit(solution)/shard_map/reduce_sum | solution.py:100
  146.7 0.6 fusion.15
  147.4 1.3 pad_maximum_fusion
  148.7 3.7 %all-to-all-start.5 = ((f32[16,17,1024]{2,1,0:T(8,128)}), f32[16,17,1024]{2,1,0:T(8,128)S(1)}, u32[]{:S(2)}, u32[]{:S(2)}) async-start(f32[16,17,1024]{2,1,0:T(8,128)} %pad_maximum_fusion), calls=%async_computation.5 | async-start | bytes 3145728 | tf_op jit(solution)/shard_map/all_to_all | solution.py:111
  152.5 18.6 %all-to-all-done.5 = f32[16,17,1024]{2,1,0:T(8,128)S(1)} async-done(((f32[16,17,1024]{2,1,0:T(8,128)}), f32[16,17,1024]{2,1,0:T(8,128)S(1)}, u32[]{:S(2)}, u32[]{:S(2)}) %all-to-all-start.5) | async-done | bytes 1114144 | tf_op jit(solution)/shard_map/all_to_all | solution.py:111
  171.4 0.8 reshape.212
  172.1 9.1 %all-to-all-start.6 = ((f32[16,1,1152]{2,1,0:T(1,128)}), f32[16,1,1152]{2,1,0:T(1,128)S(1)}, u32[]{:S(2)}, u32[]{:S(2)}) async-start(f32[16,1,1152]{2,1,0:T(1,128)} %reshape.212), calls=%async_computation.6 | async-start | bytes 147456 | tf_op jit(solution)/shard_map/all_to_all | solution.py:114
  181.6 7.7 %all-to-all-done.6 = f32[16,1,1152]{2,1,0:T(1,128)S(1)} async-done(((f32[16,1,1152]{2,1,0:T(1,128)}), f32[16,1,1152]{2,1,0:T(1,128)S(1)}, u32[]{:S(2)}, u32[]{:S(2)}) %all-to-all-start.6) | async-done | bytes 73760 | tf_op jit(solution)/shard_map/all_to_all | solution.py:114
  189.3 0.5 broadcast.96
  189.8 0.8 reduce.5
  190.7 0.2 copy.119
  190.9 1.0 gather_fusion
  192.3 9.7 %all_to_all.42 = bf16[16,16,256]{2,1,0:T(8,128)(2,1)S(1)} all-to-all(bf16[16,16,256]{2,1,0:T(8,128)(2,1)S(1)} %broadcast_in_dim.38), channel_id=1, replica_groups=mesh['cell'=16,'sub'=16] {'sub'}, dimensions={0} | all-to-all | bytes 262144 | tf_op jit(solution)/shard_map/all_to_all | solution.py:52
  201.9 0.8 copy.122
  (50 shorter events, 2.3 us)
Async XLA Ops:
  0.0 146.7 %copy-start = (bf16[32,24,256]{2,1,0:T(8,128)(2,1)S(1)}, bf16[32,24,256]{2,1,0:T(8,128)(2,1)}, u32[]{:S(2)}) copy-start(bf16[32,24,256]{2,1,0:T(8,128)(2,1)} %param.15) | copy-start | bytes 1179652
  1.6 18.6 %copy-start.1 = (bf16[4,16,256]{2,1,0:T(8,128)(2,1)S(1)}, bf16[4,16,256]{2,1,0:T(8,128)(2,1)}, u32[]{:S(2)}) copy-start(bf16[4,16,256]{2,1,0:T(8,128)(2,1)} %param.12) | copy-start | bytes 98308
  6.9 40.8 %all-to-all-start = ((bf16[16,2,512]{2,1,0:T(2,128)(2,1)}), bf16[16,2,512]{2,1,0:T(2,128)(2,1)}, u32[]{:S(2)}, u32[]{:S(2)}) async-start(bf16[16,2,512]{2,1,0:T(2,128)(2,1)} %reshape.210), calls=%async_computation | async-start | bytes 65536 | tf_op jit(solution)/shard_map/all_to_all | solution.py:73
  20.2 17.3 %copy-start.2 = (bf16[32,64]{1,0:T(8,128)(2,1)S(1)}, bf16[32,64]{1,0:T(8,128)(2,1)}, u32[]{:S(2)}) copy-start(bf16[32,64]{1,0:T(8,128)(2,1)} %param.11) | copy-start | bytes 12292
  47.7 16.2 %all-to-all-start.1 = ((bf16[16,2,2048]{2,1,0:T(2,128)(2,1)}), bf16[16,2,2048]{2,1,0:T(2,128)(2,1)}, u32[]{:S(2)}, u32[]{:S(2)}) async-start(bf16[16,2,2048]{2,1,0:T(2,128)(2,1)} %reshape.208), calls=%async_computation.1 | async-start | bytes 262144 | tf_op jit(solution)/shard_map/all_to_all | solution.py:70
  63.9 30.5 %all-to-all-start.3 = ((bf16[16,64,768]{2,1,0:T(8,128)(2,1)}), bf16[16,64,768]{2,1,0:T(8,128)(2,1)S(1)}, u32[]{:S(2)}, u32[]{:S(2)}) async-start(bf16[16,64,768]{2,1,0:T(8,128)(2,1)} %fusion.2), calls=%async_computation.3 | async-start | bytes 3145728 | tf_op jit(solution)/shard_map/all_to_all | solution.py:65
  72.0 28.6 %copy-start.3 = (s32[32]{0:T(128)S(1)}, s32[32]{0:T(128)}, u32[]{:S(2)}) copy-start(s32[32]{0:T(128)} %param.14) | copy-start | bytes 388
  96.1 30.3 %all-to-all-start.2 = ((bf16[16,1024,64]{1,2,0:T(8,128)(2,1)}), bf16[16,1024,64]{1,2,0:T(8,128)(2,1)}, u32[]{:S(2)}, u32[]{:S(2)}) async-start(bf16[16,1024,64]{1,2,0:T(8,128)(2,1)} %broadcast_in_dim.31), calls=%async_computation.2 | async-start | bytes 4194304 | tf_op jit(solution)/shard_map/all_to_all | solution.py:52
  148.7 22.4 %all-to-all-start.5 = ((f32[16,17,1024]{2,1,0:T(8,128)}), f32[16,17,1024]{2,1,0:T(8,128)S(1)}, u32[]{:S(2)}, u32[]{:S(2)}) async-start(f32[16,17,1024]{2,1,0:T(8,128)} %pad_maximum_fusion), calls=%async_computation.5 | async-start | bytes 3145728 | tf_op jit(solution)/shard_map/all_to_all | solution.py:111
  172.1 17.1 %all-to-all-start.6 = ((f32[16,1,1152]{2,1,0:T(1,128)}), f32[16,1,1152]{2,1,0:T(1,128)S(1)}, u32[]{:S(2)}, u32[]{:S(2)}) async-start(f32[16,1,1152]{2,1,0:T(1,128)} %reshape.212), calls=%async_computation.6 | async-start | bytes 147456 | tf_op jit(solution)/shard_map/all_to_all | solution.py:114

commit v3 on v2

--- a/solution.py
+++ b/solution.py
@@ -62,8 +62,6 @@
     chunk = pw // parts
 
     local_vectors = decode(coarse, codebooks, codes, parts)
-    decoded = lax.all_to_all(local_vectors, "sub", split_axis=0, concat_axis=0, tiled=True)
-    decoded = decoded.reshape(-1, decoded.shape[2])
 
     slots = slot_table(probe_groups, groups, capacity)
     buffer, cell_marks = pack_slots(queries, probe_cells, slots, total)
@@ -73,7 +71,14 @@
     arrived_cells = lax.all_to_all(
         cell_marks.reshape(groups, capacity, -1), "cell", split_axis=0, concat_axis=0, tiled=True
     )
-    query_parts = gather_by_exchange(arrived.reshape(total, -1), "sub")
+    query_cols = jnp.broadcast_to(arrived.reshape(total, -1).T[None], (parts,) + (arrived.shape[2], total))
+    exchanged = lax.all_to_all(
+        jnp.concatenate([local_vectors, query_cols], axis=2), "sub", split_axis=0, concat_axis=0, tiled=True
+    )
+    row_cols = local_vectors.shape[2]
+    decoded_parts = exchanged[:, :, :row_cols]
+    query_parts = exchanged[:, :, row_cols:]
+    decoded = decoded_parts.reshape(-1, row_cols)
     cell_ids = arrived_cells.reshape(total, -1).astype(jnp.int32)
     probed = jnp.any(
         cell_ids[:, :, None] == jnp.arange(cell_dev, dtype=jnp.int32)[None, None, :], axis=1
@@ -86,12 +91,7 @@
     keep = (probed[:, :, None] & live[None, :, :]).reshape(total, -1)
     table = payload.reshape(-1, pw)
 
-    raw = jnp.einsum(
-        "sqd,sdr->qr",
-        query_parts,
-        decoded.reshape(parts, -1, decoded.shape[1]),
-        preferred_element_type=jnp.float32,
-    )
+    raw = jnp.einsum("sdq,sdr->qr", query_parts, decoded_parts, preferred_element_type=jnp.float32)
     values = (raw - 0.5 * sq_norm[None, :]) * score_scale
     local_peak = jnp.max(jnp.where(keep, values, floor_score), axis=1)
     peak = jnp.max(gather_by_exchange(local_peak, "sub"), axis=0)

time: 204 us -> 196 us (0.961)
  local copies, waits for them, and re-layouts: 25 us -> 14.9 us
  blocking collectives: 21.4 us -> 28.4 us
  starting transfers between devices: 41.2 us -> 35.2 us
  waiting for transfers between devices: 79 us -> 82 us
    all_to_all x2, blocking collectives: 21.4 us -> 28.4 us  [gather_by_exchange(): return lax.all_to_all(copies, axis, split_axis=0, concat_axis=0, tiled=True)]
    all_to_all x1, waiting for transfers between devices: 6.33 us -> 0.01 us  [local(): lax.all_to_all(buffer.reshape(groups, capacity, -1), 'cell', split_axis=0...]
    all_to_all x1, waiting for transfers between devices: 0.01 us -> 4.63 us  [local(): lax.all_to_all(cell_marks.reshape(groups, capacity, -1), 'cell', split_ax...]
    all_to_all x2 -> x1, starting transfers between devices: 11.2 us -> 6.8 us  [local(): lax.all_to_all(jnp.concatenate([local_vectors, query_cols], axis=2), 'sub...]
    all_to_all x2 -> x1, waiting for transfers between devices: 46.3 us -> 49.8 us  [local(): lax.all_to_all(jnp.concatenate([local_vectors, query_cols], axis=2), 'sub...]
    unnamed x16 -> x18, local copies, waits for them, and re-layouts: 7.85 us -> 4.63 us
    all_to_all x1, starting transfers between devices: 7.23 us -> 9.97 us  [local(): lax.all_to_all(buffer.reshape(groups, capacity, -1), 'cell', split_axis=0...]
    all_to_all x1, starting transfers between devices: 9.97 us -> 7.24 us  [local(): lax.all_to_all(cell_marks.reshape(groups, capacity, -1), 'cell', split_ax...]
  transfers between devices with their start and end apart: 6 -> 5, of which waited for: 5 -> 4; matrix products, arithmetic and copies ran while one was open for 18% -> 14% of each run, Pallas kernels for 0% -> 0%
where the time goes in v3:
time: 196 us
  waiting for transfers between devices  82 us (42%)
  starting transfers between devices  35.2 us (18%)
  blocking collectives  28.4 us (14%)
  matrix products  21.5 us (11%)
  local copies, waits for them, and re-layouts  14.9 us (8%)
  other arithmetic  13.2 us (7%)
    all_to_all x1, waiting for transfers between devices, local(): lax.all_to_all(jnp.concatenate([local_vectors, query_cols], axis=2), 'sub...  49.8 us
    all_to_all x2, blocking collectives, gather_by_exchange(): return lax.all_to_all(copies, axis, split_axis=0, concat_axis=0, tiled=True)  28.4 us
    all_to_all x1, waiting for transfers between devices, local(): lax.all_to_all(sendable, 'sub', split_axis=0, concat_axis=0, tiled=True)  19.9 us
    dot_general x1, matrix products, decode(): lax.dot_general(books, onehot, (((3,), (3,)), ((0, 1), (0, 1))), preferre...  16.6 us
    all_to_all x1, starting transfers between devices, local(): lax.all_to_all(buffer.reshape(groups, capacity, -1), 'cell', split_axis=0...  9.97 us
    all_to_all x1, waiting for transfers between devices, local(): lax.all_to_all(outgoing.reshape(chunk + 2, groups, capacity), 'cell', spl...  7.68 us
    all_to_all x1, starting transfers between devices, local(): lax.all_to_all(outgoing.reshape(chunk + 2, groups, capacity), 'cell', spl...  7.51 us
    all_to_all x1, starting transfers between devices, local(): lax.all_to_all(cell_marks.reshape(groups, capacity, -1), 'cell', split_ax...  7.24 us
  transfers between devices with their start and end apart: 5, of which 4 were waited for; matrix products, arithmetic and copies ran while one was open for 14% of the time, Pallas kernels for 0%

profile of v3, /device:TPU:1, one launch (start us, length us, event | category | flops | bytes accessed | tf_op | source)
XLA Modules:
  0.0 195.6 jit_solution(2987167602042752260)
XLA Ops:
  0.0 0.7 convert_reduce_fusion.1
  0.7 0.6 reduce-window.6
  1.3 0.2 slice_reduce_fusion
  1.6 0.7 select_reduce_fusion.1
  2.4 0.7 compare_select_fusion.1
  3.0 0.1 copy.106
  3.2 0.1 reshape.167
  3.3 0.9 copy.115
  4.3 1.8 scatter_custom_fusion.1
  6.2 0.9 reshape.212
  7.1 10.0 %all-to-all-start.1 = ((bf16[16,2,2048]{2,1,0:T(2,128)(2,1)}), bf16[16,2,2048]{2,1,0:T(2,128)(2,1)S(1)}, u32[]{:S(2)}, u32[]{:S(2)}) async-start(bf16[16,2,2048]{2,1,0:T(2,128)(2,1)} %reshape.212), calls=%async_computation.1 | async-start | bytes 262144 | tf_op jit(solution)/shard_map/all_to_all | solution.py:68
  17.0 0.9 copy.111
  18.0 0.6 reshape.169
  18.6 0.3 copy.125
  19.0 0.6 reshape.206
  19.7 0.1 copy.114
  20.0 1.8 scatter_custom_fusion
  21.9 0.1 copy.109
  22.0 0.7 reshape.214
  22.7 16.6 %fusion = f32[16,4,768,16]{2,3,1,0:T(8,128)S(1)} fusion(s32[16,4,768]{2,1,0:T(4,128)S(1)} %reshape.206, bf16[16,4,16,256]{3,2,1,0:T(8,128)(2,1)S(1)} %fusion.25), kind=kOutput, calls=%fused_computation.4 | convolution fusion | flops 415236096 | bytes 3866624 | tf_op jit(solution)/shard_map/dot_general | solution.py:41
  39.3 0.3 fusion.2
  39.6 7.2 %all-to-all-start = ((bf16[16,2,512]{2,1,0:T(2,128)(2,1)}), bf16[16,2,512]{2,1,0:T(2,128)(2,1)S(1)}, u32[]{:S(2)}, u32[]{:S(2)}) async-start(bf16[16,2,512]{2,1,0:T(2,128)(2,1)} %reshape.214), calls=%async_computation | async-start | bytes 65536 | tf_op jit(solution)/shard_map/all_to_all | solution.py:71
  46.9 0.2 reshape.213
  47.2 0.3 broadcast_in_dim.29
  47.5 2.2 %pad_maximum_fusion = bf16[16,64,1792]{2,1,0:T(8,128)(2,1)} fusion(bf16[16,64,1024]{2,1,0:T(8,128)(2,1)S(1)} %broadcast_in_dim.29, bf16[16,64,768]{2,1,0:T(8,128)(2,1)S(1)} %fusion.2), kind=kLoop, calls=%fused_computation.6 | loop fusion | flops 7340032 | bytes 7340032 | tf_op jit(solution)/shard_map/concatenate | solution.py:76
  49.6 4.6 %all-to-all-done = bf16[16,2,512]{2,1,0:T(2,128)(2,1)S(1)} async-done(((bf16[16,2,512]{2,1,0:T(2,128)(2,1)}), bf16[16,2,512]{2,1,0:T(2,128)(2,1)S(1)}, u32[]{:S(2)}, u32[]{:S(2)}) %all-to-all-start) | async-done | bytes 32800 | tf_op jit(solution)/shard_map/all_to_all | solution.py:71
  54.3 6.8 %all-to-all-start.2 = ((bf16[16,64,1792]{2,1,0:T(8,128)(2,1)}), bf16[16,64,1792]{2,1,0:T(8,128)(2,1)}, u32[]{:S(2)}, u32[]{:S(2)}) async-start(bf16[16,64,1792]{2,1,0:T(8,128)(2,1)} %pad_maximum_fusion), calls=%async_computation.2 | async-start | bytes 7340032 | tf_op jit(solution)/shard_map/all_to_all | solution.py:75
  61.7 0.9 fusion.6
  62.5 49.8 %all-to-all-done.2 = bf16[16,64,1792]{2,1,0:T(8,128)(2,1)} async-done(((bf16[16,64,1792]{2,1,0:T(8,128)(2,1)}), bf16[16,64,1792]{2,1,0:T(8,128)(2,1)}, u32[]{:S(2)}, u32[]{:S(2)}) %all-to-all-start.2) | async-done | bytes 3670048 | tf_op jit(solution)/shard_map/all_to_all | solution.py:75
  112.3 1.8 multiply_reduce_fusion
  114.1 4.3 %select_reduce_fusion = (f32[1024]{0:T(1024)S(1)}, f32[1024,768,1]{0,1,2:T(8,128)S(1)}) fusion(f32[768]{0:T(1024)S(1)} %broadcast_multiply_fusion, pred[768]{0:T(1024)(128)(4,1)S(1)} %lt.43, pred[1024,32]{0,1:T(8,128)(4,1)} %fusion.6, bf16[16,64,1792]{2,1,0:T(8,128)(2,1)} %all-to-all-done.2), kind=kOutput, calls=%fused_computation.13 | convolution fusion | flops 1614543872 | bytes 6856448 | tf_op jit(solution)/shard_map/sdq,sdr->qr/dot_general | solution.py:94
  118.5 18.3 %all_to_all.36 = f32[16,1,1024]{2,1,0:T(1,128)} all-to-all(f32[16,1,1024]{2,1,0:T(1,128)S(1)} %broadcast_in_dim.31), channel_id=1, replica_groups=mesh['cell'=16,'sub'=16] {'sub'}, dimensions={0} | all-to-all | bytes 131072 | tf_op jit(solution)/shard_map/all_to_all | solution.py:52
  136.8 0.9 reduce_max.28
  137.7 1.9 convert_reduce_fusion
  139.6 0.6 fusion.18
  140.3 1.3 pad_maximum_fusion.1
  141.6 3.7 %all-to-all-start.4 = ((f32[16,17,1024]{2,1,0:T(8,128)}), f32[16,17,1024]{2,1,0:T(8,128)S(1)}, u32[]{:S(2)}, u32[]{:S(2)}) async-start(f32[16,17,1024]{2,1,0:T(8,128)} %pad_maximum_fusion.1), calls=%async_computation.4 | async-start | bytes 3145728 | tf_op jit(solution)/shard_map/all_to_all | solution.py:111
  145.4 19.9 %all-to-all-done.4 = f32[16,17,1024]{2,1,0:T(8,128)S(1)} async-done(((f32[16,17,1024]{2,1,0:T(8,128)}), f32[16,17,1024]{2,1,0:T(8,128)S(1)}, u32[]{:S(2)}, u32[]{:S(2)}) %all-to-all-start.4) | async-done | bytes 1114144 | tf_op jit(solution)/shard_map/all_to_all | solution.py:111
  165.5 0.8 reshape.216
  166.3 7.5 %all-to-all-start.5 = ((f32[16,1,1152]{2,1,0:T(1,128)}), f32[16,1,1152]{2,1,0:T(1,128)S(1)}, u32[]{:S(2)}, u32[]{:S(2)}) async-start(f32[16,1,1152]{2,1,0:T(1,128)} %reshape.216), calls=%async_computation.5 | async-start | bytes 147456 | tf_op jit(solution)/shard_map/all_to_all | solution.py:114
  174.0 0.1 reshape.181
  174.1 7.7 %all-to-all-done.5 = f32[16,1,1152]{2,1,0:T(1,128)S(1)} async-done(((f32[16,1,1152]{2,1,0:T(1,128)}), f32[16,1,1152]{2,1,0:T(1,128)S(1)}, u32[]{:S(2)}, u32[]{:S(2)}) %all-to-all-start.5) | async-done | bytes 73760 | tf_op jit(solution)/shard_map/all_to_all | solution.py:114
  181.8 0.5 broadcast.97
  182.3 0.8 reduce.5
  183.2 0.2 copy.119
  183.5 1.0 gather_fusion
  184.8 10.1 %all_to_all.37 = bf16[16,16,256]{2,1,0:T(8,128)(2,1)S(1)} all-to-all(bf16[16,16,256]{2,1,0:T(8,128)(2,1)S(1)} %broadcast_in_dim.35), channel_id=1, replica_groups=mesh['cell'=16,'sub'=16] {'sub'}, dimensions={0} | all-to-all | bytes 262144 | tf_op jit(solution)/shard_map/all_to_all | solution.py:52
  194.9 0.8 copy.122
  (51 shorter events, 2.0 us)
Async XLA Ops:
  0.0 139.6 %copy-start = (bf16[32,24,256]{2,1,0:T(8,128)(2,1)S(1)}, bf16[32,24,256]{2,1,0:T(8,128)(2,1)}, u32[]{:S(2)}) copy-start(bf16[32,24,256]{2,1,0:T(8,128)(2,1)} %param.15) | copy-start | bytes 1179652
  3.2 16.4 %copy-start.1 = (bf16[4,16,256]{2,1,0:T(8,128)(2,1)S(1)}, bf16[4,16,256]{2,1,0:T(8,128)(2,1)}, u32[]{:S(2)}) copy-start(bf16[4,16,256]{2,1,0:T(8,128)(2,1)} %param.12) | copy-start | bytes 98308
  6.1 13.5 %copy-start.3 = (bf16[32,64]{1,0:T(8,128)(2,1)S(1)}, bf16[32,64]{1,0:T(8,128)(2,1)}, u32[]{:S(2)}) copy-start(bf16[32,64]{1,0:T(8,128)(2,1)} %param.11) | copy-start | bytes 12292
  7.1 32.6 %all-to-all-start.1 = ((bf16[16,2,2048]{2,1,0:T(2,128)(2,1)}), bf16[16,2,2048]{2,1,0:T(2,128)(2,1)S(1)}, u32[]{:S(2)}, u32[]{:S(2)}) async-start(bf16[16,2,2048]{2,1,0:T(2,128)(2,1)} %reshape.212), calls=%async_computation.1 | async-start | bytes 262144 | tf_op jit(solution)/shard_map/all_to_all | solution.py:68
  18.0 1.9 copy-start.2
  39.6 14.6 %all-to-all-start = ((bf16[16,2,512]{2,1,0:T(2,128)(2,1)}), bf16[16,2,512]{2,1,0:T(2,128)(2,1)S(1)}, u32[]{:S(2)}, u32[]{:S(2)}) async-start(bf16[16,2,512]{2,1,0:T(2,128)(2,1)} %reshape.214), calls=%async_computation | async-start | bytes 65536 | tf_op jit(solution)/shard_map/all_to_all | solution.py:71
  49.6 11.6 %copy-start.4 = (s32[32]{0:T(128)S(1)}, s32[32]{0:T(128)}, u32[]{:S(2)}) copy-start(s32[32]{0:T(128)} %param.14) | copy-start | bytes 388
  54.3 58.1 %all-to-all-start.2 = ((bf16[16,64,1792]{2,1,0:T(8,128)(2,1)}), bf16[16,64,1792]{2,1,0:T(8,128)(2,1)}, u32[]{:S(2)}, u32[]{:S(2)}) async-start(bf16[16,64,1792]{2,1,0:T(8,128)(2,1)} %pad_maximum_fusion), calls=%async_computation.2 | async-start | bytes 7340032 | tf_op jit(solution)/shard_map/all_to_all | solution.py:75
  141.6 23.7 %all-to-all-start.4 = ((f32[16,17,1024]{2,1,0:T(8,128)}), f32[16,17,1024]{2,1,0:T(8,128)S(1)}, u32[]{:S(2)}, u32[]{:S(2)}) async-start(f32[16,17,1024]{2,1,0:T(8,128)} %pad_maximum_fusion.1), calls=%async_computation.4 | async-start | bytes 3145728 | tf_op jit(solution)/shard_map/all_to_all | solution.py:111
  166.3 15.5 %all-to-all-start.5 = ((f32[16,1,1152]{2,1,0:T(1,128)}), f32[16,1,1152]{2,1,0:T(1,128)S(1)}, u32[]{:S(2)}, u32[]{:S(2)}) async-start(f32[16,1,1152]{2,1,0:T(1,128)} %reshape.216), calls=%async_computation.5 | async-start | bytes 147456 | tf_op jit(solution)/shard_map/all_to_all | solution.py:114

commit v4 on v3

--- a/solution.py
+++ b/solution.py
@@ -1,6 +1,7 @@
 import jax
 import jax.numpy as jnp
 from jax import lax
+from jax.experimental import pallas as pl
 from jax.sharding import PartitionSpec as P
 
 CAP = 64
@@ -29,21 +30,32 @@
     return (buffer, cell_marks)
 
 
-def decode(coarse, codebooks, codes, parts):
-    cell_count, sub_count, row_count = codes.shape
-    width = codebooks.shape[1]
-    rows_part = row_count // parts
-    grouped = codes.reshape(cell_count, sub_count, parts, rows_part)
-    grouped = jnp.transpose(grouped, (2, 1, 0, 3)).reshape(parts, sub_count, cell_count * rows_part)
-    centroid_ids = jnp.arange(codebooks.shape[2], dtype=jnp.int32)
-    onehot = (grouped[..., None] == centroid_ids).astype(jnp.bfloat16)
-    books = jnp.broadcast_to(codebooks[None], (parts,) + codebooks.shape)
-    picked = lax.dot_general(
-        books, onehot, (((3,), (3,)), ((0, 1), (0, 1))), preferred_element_type=jnp.float32
-    )
-    picked = picked.reshape(parts, sub_count * width, cell_count, rows_part)
-    recon = picked + coarse.T.astype(jnp.float32)[None, :, :, None]
-    return recon.astype(jnp.bfloat16).reshape(parts, sub_count * width, cell_count * rows_part)
+def decode_kernel(codes_ref, book_ref, base_ref, out_ref):
+    m_count, width, k_count = book_ref.shape
+    n = codes_ref.shape[2]
+    ids = lax.broadcasted_iota(jnp.int32, (k_count, n), 0)
+    for m in range(m_count):
+        row = codes_ref[0, m : m + 1, :]
+        onehot = (ids == row).astype(jnp.bfloat16)
+        val = jnp.dot(book_ref[m], onehot, preferred_element_type=jnp.float32)
+        base = base_ref[m * width : (m + 1) * width, :].astype(jnp.float32)
+        out_ref[0, m * width : (m + 1) * width, :] = (val + base).astype(jnp.bfloat16)
+
+
+def decode(base, codebooks, codes_blocks):
+    blocks, per_block, n = codes_blocks.shape
+    width, k_count = codebooks.shape[1], codebooks.shape[2]
+    return pl.pallas_call(
+        decode_kernel,
+        grid=(blocks,),
+        in_specs=[
+            pl.BlockSpec((1, per_block, n), lambda p: (p, 0, 0)),
+            pl.BlockSpec((per_block, width, k_count), lambda p: (p, 0, 0)),
+            pl.BlockSpec((per_block * width, n), lambda p: (p, 0)),
+        ],
+        out_specs=pl.BlockSpec((1, per_block * width, n), lambda p: (p, 0, 0)),
+        out_shape=jax.ShapeDtypeStruct((blocks, per_block * width, n), jnp.bfloat16),
+    )(codes_blocks, codebooks, base)
 
 
 def gather_by_exchange(x, axis):
@@ -61,7 +73,29 @@
     pw = payload.shape[2]
     chunk = pw // parts
 
-    local_vectors = decode(coarse, codebooks, codes, parts)
+    cell_count, sub_count, row_count = codes.shape
+    rows_part = row_count // parts
+    own_codes = codes.reshape(cell_count, sub_count, parts, rows_part)
+    own_codes = jnp.transpose(own_codes, (2, 0, 1, 3)).astype(jnp.bfloat16).reshape(parts, -1)
+    tables = jnp.concatenate(
+        [
+            own_codes,
+            jnp.broadcast_to(codebooks.reshape(1, -1), (parts, codebooks.size)),
+            jnp.broadcast_to(coarse.reshape(1, -1), (parts, coarse.size)),
+        ],
+        axis=1,
+    )
+    tables = lax.all_to_all(tables, "sub", split_axis=0, concat_axis=0, tiled=True)
+    code_size = own_codes.shape[1]
+    book_size = codebooks.size
+    got_codes = tables[:, :code_size].reshape(parts, cell_count, sub_count, rows_part)
+    got_codes = jnp.transpose(got_codes, (0, 2, 1, 3)).astype(jnp.int32)
+    got_codes = got_codes.reshape(parts, sub_count, cell_count * rows_part)
+    all_books = tables[:, code_size : code_size + book_size].reshape((-1,) + codebooks.shape[1:])
+    all_coarse = tables[:, code_size + book_size :].reshape(parts, cell_count, -1)
+    all_coarse = jnp.transpose(all_coarse, (1, 0, 2)).reshape(cell_count, -1)
+    base = jnp.repeat(all_coarse.T, rows_part, axis=1)
+    decoded_parts = decode(base, all_books, got_codes)
 
     slots = slot_table(probe_groups, groups, capacity)
     buffer, cell_marks = pack_slots(queries, probe_cells, slots, total)
@@ -71,14 +105,8 @@
     arrived_cells = lax.all_to_all(
         cell_marks.reshape(groups, capacity, -1), "cell", split_axis=0, concat_axis=0, tiled=True
     )
-    query_cols = jnp.broadcast_to(arrived.reshape(total, -1).T[None], (parts,) + (arrived.shape[2], total))
-    exchanged = lax.all_to_all(
-        jnp.concatenate([local_vectors, query_cols], axis=2), "sub", split_axis=0, concat_axis=0, tiled=True
-    )
-    row_cols = local_vectors.shape[2]
-    decoded_parts = exchanged[:, :, :row_cols]
-    query_parts = exchanged[:, :, row_cols:]
-    decoded = decoded_parts.reshape(-1, row_cols)
+    query_parts = gather_by_exchange(arrived.reshape(total, -1).T, "sub")
+    decoded = decoded_parts.reshape(-1, decoded_parts.shape[2])
     cell_ids = arrived_cells.reshape(total, -1).astype(jnp.int32)
     probed = jnp.any(
         cell_ids[:, :, None] == jnp.arange(cell_dev, dtype=jnp.int32)[None, None, :], axis=1

time: 196 us -> 168 us (0.86)
  waiting for transfers between devices: 82 us -> 49.9 us
  matrix products: 21.5 us -> 6.13 us
  Pallas kernels: 0 us -> 11.7 us
  local copies, waits for them, and re-layouts: 14.9 us -> 23.4 us
  blocking collectives: 28.4 us -> 21.6 us
  starting transfers between devices: 35.2 us -> 39.7 us
    all_to_all x1 -> x2, waiting for transfers between devices: 49.8 us -> 16.6 us  [the longest x1 12.3 us: local(): lax.all_to_all(tables, 'sub', split_axis=0, concat_axis=0, tiled=True)]
    dot_general x1 -> x0, matrix products: 16.6 us -> none  [decode(): lax.dot_general(books, onehot, (((3,), (3,)), ((0, 1), (0, 1))), preferre...]
    pallas_call x0 -> x1, Pallas kernels: none -> 11.7 us  [decode(): pl.pallas_call(decode_kernel, grid=(blocks,), in_specs=[pl.BlockSpec((1,...]
    all_to_all x2, blocking collectives: 28.4 us -> 21.6 us  [gather_by_exchange(): return lax.all_to_all(copies, axis, split_axis=0, concat_axis=0, tiled=True)]
    reshape x3 -> x11, local copies, waits for them, and re-layouts: 0.77 us -> 6.67 us  [the longest x3 2.84 us: local(): got_codes = got_codes.reshape(parts, sub_count, cell_count * rows_part)]
    all_to_all x1, waiting for transfers between devices: 0.01 us -> 5.63 us  [local(): lax.all_to_all(buffer.reshape(groups, capacity, -1), 'cell', split_axis=0...]
    all_to_all x1 -> x2, starting transfers between devices: 6.8 us -> 11.5 us  [the longest x1 6.76 us: local(): lax.all_to_all(tables, 'sub', split_axis=0, concat_axis=0, tiled=True)]
    all_to_all x1, starting transfers between devices: 9.97 us -> 5.72 us  [local(): lax.all_to_all(buffer.reshape(groups, capacity, -1), 'cell', split_axis=0...]
  transfers between devices with their start and end apart: 5 -> 6, of which waited for: 4 -> 6; matrix products, arithmetic and copies ran while one was open for 14% -> 12% of each run, Pallas kernels for 0% -> 7%
where the time goes in v4:
time: 168 us; the launch traced here: 166 us
  waiting for transfers between devices  49.9 us (30%)
  starting transfers between devices  39.7 us (24%)
  local copies, waits for them, and re-layouts  23.4 us (14%)
  blocking collectives  21.6 us (13%)
  other arithmetic  13.5 us (8%)
  Pallas kernels  11.7 us (7%)
  matrix products  6.13 us (4%)
    all_to_all x2, blocking collectives, gather_by_exchange(): return lax.all_to_all(copies, axis, split_axis=0, concat_axis=0, tiled=True)  21.6 us
    all_to_all x1, waiting for transfers between devices, local(): lax.all_to_all(sendable, 'sub', split_axis=0, concat_axis=0, tiled=True)  18.6 us
    all_to_all x1, waiting for transfers between devices, local(): lax.all_to_all(tables, 'sub', split_axis=0, concat_axis=0, tiled=True)  12.3 us
    pallas_call x1, Pallas kernels, decode(): pl.pallas_call(decode_kernel, grid=(blocks,), in_specs=[pl.BlockSpec((1,...  11.7 us
    all_to_all x1, starting transfers between devices, local(): lax.all_to_all(cell_marks.reshape(groups, capacity, -1), 'cell', split_ax...  9.97 us
    all_to_all x1, starting transfers between devices, local(): lax.all_to_all(outgoing.reshape(chunk + 2, groups, capacity), 'cell', spl...  8.78 us
    all_to_all x1, waiting for transfers between devices, local(): lax.all_to_all(outgoing.reshape(chunk + 2, groups, capacity), 'cell', spl...  7.68 us
    all_to_all x1, starting transfers between devices, local(): lax.all_to_all(tables, 'sub', split_axis=0, concat_axis=0, tiled=True)  6.76 us
  transfers between devices with their start and end apart: 6, of which 6 were waited for; matrix products, arithmetic and copies ran while one was open for 12% of the time, Pallas kernels for 7%

profile of v4, /device:TPU:1, one launch (start us, length us, event | category | flops | bytes accessed | tf_op | source)
XLA Modules:
  0.0 166.4 jit_solution(5443284138138464792)
XLA Ops:
  0.0 0.7 convert_reduce_fusion.1
  0.8 0.6 reduce-window.6
  1.7 0.7 select_reduce_fusion.1
  2.4 0.7 compare_select_fusion.1
  3.4 0.8 convert_element_type.53
  4.2 1.8 %scatter_custom_fusion = bf16[1024,16]{1,0:T(8,128)(2,1)S(1)} fusion(s32[512]{0:T(512)S(1)} %bitcast.125, bf16[512,16]{1,0:T(8,128)(2,1)S(1)} %bitcast.122, bf16[]{:T(256)} %constant.13.clone.1), kind=kCustom, calls=%fused_computation.19 | custom fusion | bytes 32770 | tf_op jit(solution)/shard_map/scatter | solution.py:29
  6.2 0.7 reshape.248
  6.9 10.0 %all-to-all-start = ((bf16[16,2,512]{2,1,0:T(2,128)(2,1)}), bf16[16,2,512]{2,1,0:T(2,128)(2,1)S(1)}, u32[]{:S(2)}, u32[]{:S(2)}) async-start(bf16[16,2,512]{2,1,0:T(2,128)(2,1)} %reshape.248), calls=%async_computation | async-start | bytes 65536 | tf_op jit(solution)/shard_map/all_to_all | solution.py:105
  16.9 1.0 convert_element_type.57
  17.9 0.7 convert_element_type.58
  18.6 0.4 copy.128
  19.0 0.7 reshape.191
  20.1 1.8 %scatter_custom_fusion.1 = bf16[1024,64]{1,0:T(8,128)(2,1)S(1)} fusion(s32[512]{0:T(512)S(1)} %bitcast.126, bf16[512,64]{1,0:T(8,128)(2,1)S(1)} %bitcast.121, bf16[]{:T(256)} %constant.6.clone.1), kind=kCustom, calls=%fused_computation.17 | custom fusion | bytes 131074 | tf_op jit(solution)/shard_map/scatter | solution.py:27
  21.9 0.9 reshape.244
  22.8 1.5 all-to-all-done
  24.3 5.7 %all-to-all-start.1 = ((bf16[16,2,2048]{2,1,0:T(2,128)(2,1)}), bf16[16,2,2048]{2,1,0:T(2,128)(2,1)S(1)}, u32[]{:S(2)}, u32[]{:S(2)}) async-start(bf16[16,2,2048]{2,1,0:T(2,128)(2,1)} %reshape.244), calls=%async_computation.1 | async-start | bytes 262144 | tf_op jit(solution)/shard_map/all_to_all | solution.py:102
  30.1 0.6 broadcast.97
  30.7 1.2 reduce.5
  31.9 1.4 reshape.246
  33.3 5.6 %all-to-all-done.1 = bf16[16,2,2048]{2,1,0:T(2,128)(2,1)S(1)} async-done(((bf16[16,2,2048]{2,1,0:T(2,128)(2,1)}), bf16[16,2,2048]{2,1,0:T(2,128)(2,1)S(1)}, u32[]{:S(2)}, u32[]{:S(2)}) %all-to-all-start.1) | async-done | bytes 131104 | tf_op jit(solution)/shard_map/all_to_all | solution.py:102
  38.9 6.8 %all-to-all-start.3 = ((bf16[16,2,10752]{2,1,0:T(2,128)(2,1)}), bf16[16,2,10752]{2,1,0:T(2,128)(2,1)S(1)}, u32[]{:S(2)}, u32[]{:S(2)}) async-start(bf16[16,2,10752]{2,1,0:T(2,128)(2,1)} %reshape.246), calls=%async_computation.3 | async-start | bytes 1376256 | tf_op jit(solution)/shard_map/all_to_all | solution.py:88
  46.0 12.3 %all-to-all-done.3 = bf16[16,2,10752]{2,1,0:T(2,128)(2,1)S(1)} async-done(((bf16[16,2,10752]{2,1,0:T(2,128)(2,1)}), bf16[16,2,10752]{2,1,0:T(2,128)(2,1)S(1)}, u32[]{:S(2)}, u32[]{:S(2)}) %all-to-all-start.3) | async-done | bytes 688160 | tf_op jit(solution)/shard_map/all_to_all | solution.py:88
  58.3 1.6 broadcast_in_dim.36
  59.8 4.7 %all-to-all-start.2 = ((bf16[16,64,1024]{2,1,0:T(8,128)(2,1)}), bf16[16,64,1024]{2,1,0:T(8,128)(2,1)}, u32[]{:S(2)}, u32[]{:S(2)}) async-start(bf16[16,64,1024]{2,1,0:T(8,128)(2,1)} %broadcast_in_dim.36), calls=%async_computation.2 | async-start | bytes 4194304 | tf_op jit(solution)/shard_map/all_to_all | solution.py:64
  65.2 0.3 fusion.1
  65.4 0.6 reshape.247
  66.9 1.6 copy.133.base_ref
  68.5 1.4 reshape.207
  70.1 1.3 reshape.235.codes_ref
  71.4 1.0 reshape.194.book_ref
  72.4 11.7 %shard_map.82 = bf16[16,64,768]{2,1,0:T(8,128)(2,1)} custom-call(s32[16,4,768]{2,1,0:T(4,128)} %reshape.235.codes_ref, bf16[64,16,256]{2,1,0:T(8,128)(2,1)} %reshape.194.book_ref, bf16[1024,768]{1,0:T(8,128)(2,1)} %copy.133.base_ref), custom_call_target="tpu_custom_call" | custom-call | tf_op jit(solution)/shard_map/pallas_call | solution.py:48
  84.1 1.9 %multiply_reduce_fusion = f32[768]{0:T(1024)S(1)} fusion(bf16[16,64,768]{2,1,0:T(8,128)(2,1)} %shard_map.82), kind=kLoop, calls=%fused_computation.8 | loop fusion | flops 2358528 | bytes 1575936 | tf_op jit(solution)/shard_map/reduce_sum | solution.py:116
  86.0 4.3 %all-to-all-done.2 = bf16[16,64,1024]{2,1,0:T(8,128)(2,1)} async-done(((bf16[16,64,1024]{2,1,0:T(8,128)(2,1)}), bf16[16,64,1024]{2,1,0:T(8,128)(2,1)}, u32[]{:S(2)}, u32[]{:S(2)}) %all-to-all-start.2) | async-done | bytes 2097184 | tf_op jit(solution)/shard_map/all_to_all | solution.py:64
  90.3 5.5 %select_reduce_fusion = (f32[1024]{0:T(1024)S(1)}, f32[1024,768,1]{0,1,2:T(8,128)}) fusion(f32[768]{0:T(1024)S(1)} %broadcast_multiply_fusion, pred[768]{0:T(1024)(128)(4,1)S(1)} %lt.43, pred[1024,32]{0,1:T(8,128)(4,1)S(1)} %fusion.1, bf16[16,64,1024]{2,1,0:T(8,128)(2,1)} %all-to-all-done.2, bf16[16,64,768]{2,1,0:T(8,128)(2,1)S(1)} %copy-done.1), kind=kOutput, calls=%fused_computation.7 | convolution fusion | flops 1614543872 | bytes 6856448 | tf_op jit(solution)/shard_map/sdq,sdr->qr/dot_general | solution.py:122
  95.8 11.5 %all_to_all.48 = f32[16,1,1024]{2,1,0:T(1,128)S(1)} all-to-all(f32[16,1,1024]{2,1,0:T(1,128)S(1)} %broadcast_in_dim.43), channel_id=1, replica_groups=mesh['cell'=16,'sub'=16] {'sub'}, dimensions={0} | all-to-all | bytes 131072 | tf_op jit(solution)/shard_map/all_to_all | solution.py:64
  107.3 3.0 %convert_reduce_fusion = (f32[1024]{0:T(1024)S(1)}, bf16[1024,768]{0,1:T(8,128)(2,1)S(1)}) fusion(f32[1024]{0:T(1024)S(1)} %reduce_max.28, f32[768]{0:T(1024)S(1)} %broadcast_multiply_fusion, f32[1024,768,1]{0,1,2:T(8,128)} %get-tuple-element.10, pred[768]{0:T(1024)(128)(4,1)S(1)} %lt.43, pred[1024,32]{0,1:T(8,128)(4,1)S(1)} %fusion.1), kind=kLoop, calls=%fused_computation.5 | loop fusion | flops 6290432 | bytes 4763392 | tf_op jit(solution)/shard_map/reduce_sum | solution.py:128
  110.4 0.6 fusion.11
  111.0 1.3 pad_maximum_fusion
  112.4 3.7 %all-to-all-start.5 = ((f32[16,17,1024]{2,1,0:T(8,128)}), f32[16,17,1024]{2,1,0:T(8,128)S(1)}, u32[]{:S(2)}, u32[]{:S(2)}) async-start(f32[16,17,1024]{2,1,0:T(8,128)} %pad_maximum_fusion), calls=%async_computation.5 | async-start | bytes 3145728 | tf_op jit(solution)/shard_map/all_to_all | solution.py:139
  116.1 18.6 %all-to-all-done.5 = f32[16,17,1024]{2,1,0:T(8,128)S(1)} async-done(((f32[16,17,1024]{2,1,0:T(8,128)}), f32[16,17,1024]{2,1,0:T(8,128)S(1)}, u32[]{:S(2)}, u32[]{:S(2)}) %all-to-all-start.5) | async-done | bytes 1114144 | tf_op jit(solution)/shard_map/all_to_all | solution.py:139
  135.0 0.8 reshape.250
  135.7 8.8 %all-to-all-start.6 = ((f32[16,1,1152]{2,1,0:T(1,128)}), f32[16,1,1152]{2,1,0:T(1,128)S(1)}, u32[]{:S(2)}, u32[]{:S(2)}) async-start(f32[16,1,1152]{2,1,0:T(1,128)} %reshape.250), calls=%async_computation.6 | async-start | bytes 147456 | tf_op jit(solution)/shard_map/all_to_all | solution.py:142
  144.8 7.7 %all-to-all-done.6 = f32[16,1,1152]{2,1,0:T(1,128)S(1)} async-done(((f32[16,1,1152]{2,1,0:T(1,128)}), f32[16,1,1152]{2,1,0:T(1,128)S(1)}, u32[]{:S(2)}, u32[]{:S(2)}) %all-to-all-start.6) | async-done | bytes 73760 | tf_op jit(solution)/shard_map/all_to_all | solution.py:142
  152.5 0.5 broadcast.98
  153.0 0.8 reduce.6
  154.2 1.0 gather_fusion
  155.5 10.1 %all_to_all.49 = bf16[16,16,256]{2,1,0:T(8,128)(2,1)S(1)} all-to-all(bf16[16,16,256]{2,1,0:T(8,128)(2,1)S(1)} %broadcast_in_dim.91), channel_id=1, replica_groups=mesh['cell'=16,'sub'=16] {'sub'}, dimensions={0} | all-to-all | bytes 262144 | tf_op jit(solution)/shard_map/all_to_all | solution.py:64
  165.6 0.8 copy.139
  (72 shorter events, 4.4 us)
Async XLA Ops:
  0.0 110.4 %copy-start = (bf16[32,24,256]{2,1,0:T(8,128)(2,1)S(1)}, bf16[32,24,256]{2,1,0:T(8,128)(2,1)}, u32[]{:S(2)}) copy-start(bf16[32,24,256]{2,1,0:T(8,128)(2,1)} %param.15) | copy-start | bytes 1179652
  0.7 19.0 %copy-start.3 = (bf16[4,16,256]{2,1,0:T(8,128)(2,1)S(1)}, bf16[4,16,256]{2,1,0:T(8,128)(2,1)}, u32[]{:S(2)}) copy-start(bf16[4,16,256]{2,1,0:T(8,128)(2,1)} %param.12) | copy-start | bytes 98308
  1.3 18.4 %copy-start.4 = (bf16[32,64]{1,0:T(8,128)(2,1)S(1)}, bf16[32,64]{1,0:T(8,128)(2,1)}, u32[]{:S(2)}) copy-start(bf16[32,64]{1,0:T(8,128)(2,1)} %param.11) | copy-start | bytes 12292
  3.1 16.8 %copy-start.2 = (bf16[256,64]{0,1:T(8,128)(2,1)S(1)}, bf16[256,64]{0,1:T(8,128)(2,1)}, u32[]{:S(2)}) copy-start(bf16[256,64]{0,1:T(8,128)(2,1)} %param.8) | copy-start | bytes 98308
  6.9 17.4 %all-to-all-start = ((bf16[16,2,512]{2,1,0:T(2,128)(2,1)}), bf16[16,2,512]{2,1,0:T(2,128)(2,1)S(1)}, u32[]{:S(2)}, u32[]{:S(2)}) async-start(bf16[16,2,512]{2,1,0:T(2,128)(2,1)} %reshape.248), calls=%async_computation | async-start | bytes 65536 | tf_op jit(solution)/shard_map/all_to_all | solution.py:105
  24.3 14.6 %all-to-all-start.1 = ((bf16[16,2,2048]{2,1,0:T(2,128)(2,1)}), bf16[16,2,2048]{2,1,0:T(2,128)(2,1)S(1)}, u32[]{:S(2)}, u32[]{:S(2)}) async-start(bf16[16,2,2048]{2,1,0:T(2,128)(2,1)} %reshape.244), calls=%async_computation.1 | async-start | bytes 262144 | tf_op jit(solution)/shard_map/all_to_all | solution.py:102
  38.9 19.4 %all-to-all-start.3 = ((bf16[16,2,10752]{2,1,0:T(2,128)(2,1)}), bf16[16,2,10752]{2,1,0:T(2,128)(2,1)S(1)}, u32[]{:S(2)}, u32[]{:S(2)}) async-start(bf16[16,2,10752]{2,1,0:T(2,128)(2,1)} %reshape.246), calls=%async_computation.3 | async-start | bytes 1376256 | tf_op jit(solution)/shard_map/all_to_all | solution.py:88
  59.8 4.9 %copy-start.5 = (s32[32]{0:T(128)S(1)}, s32[32]{0:T(128)}, u32[]{:S(2)}) copy-start(s32[32]{0:T(128)} %param.14) | copy-start | bytes 388
  59.8 30.4 %all-to-all-start.2 = ((bf16[16,64,1024]{2,1,0:T(8,128)(2,1)}), bf16[16,64,1024]{2,1,0:T(8,128)(2,1)}, u32[]{:S(2)}, u32[]{:S(2)}) async-start(bf16[16,64,1024]{2,1,0:T(8,128)(2,1)} %broadcast_in_dim.36), calls=%async_computation.2 | async-start | bytes 4194304 | tf_op jit(solution)/shard_map/all_to_all | solution.py:64
  84.1 6.2 %copy-start.1 = (bf16[16,64,768]{2,1,0:T(8,128)(2,1)S(1)}, bf16[16,64,768]{2,1,0:T(8,128)(2,1)}, u32[]{:S(2)}) copy-start(bf16[16,64,768]{2,1,0:T(8,128)(2,1)} %shard_map.82) | copy-start | bytes 4718596
  112.4 22.4 %all-to-all-start.5 = ((f32[16,17,1024]{2,1,0:T(8,128)}), f32[16,17,1024]{2,1,0:T(8,128)S(1)}, u32[]{:S(2)}, u32[]{:S(2)}) async-start(f32[16,17,1024]{2,1,0:T(8,128)} %pad_maximum_fusion), calls=%async_computation.5 | async-start | bytes 3145728 | tf_op jit(solution)/shard_map/all_to_all | solution.py:139
  135.7 16.8 %all-to-all-start.6 = ((f32[16,1,1152]{2,1,0:T(1,128)}), f32[16,1,1152]{2,1,0:T(1,128)S(1)}, u32[]{:S(2)}, u32[]{:S(2)}) async-start(f32[16,1,1152]{2,1,0:T(1,128)} %reshape.250), calls=%async_computation.6 | async-start | bytes 147456 | tf_op jit(solution)/shard_map/all_to_all | solution.py:142

commit v5 on v4

--- a/solution.py
+++ b/solution.py
@@ -3,6 +3,7 @@
 from jax import lax
 from jax.experimental import pallas as pl
 from jax.sharding import PartitionSpec as P
+
 
 CAP = 64
 
@@ -99,15 +100,19 @@
 
     slots = slot_table(probe_groups, groups, capacity)
     buffer, cell_marks = pack_slots(queries, probe_cells, slots, total)
-    arrived = lax.all_to_all(
-        buffer.reshape(groups, capacity, -1), "cell", split_axis=0, concat_axis=0, tiled=True
-    )
-    arrived_cells = lax.all_to_all(
-        cell_marks.reshape(groups, capacity, -1), "cell", split_axis=0, concat_axis=0, tiled=True
-    )
-    query_parts = gather_by_exchange(arrived.reshape(total, -1).T, "sub")
+    width = buffer.shape[1]
+    arrived_all = lax.all_to_all(
+        jnp.concatenate([buffer, cell_marks], axis=1).reshape(groups, capacity, -1),
+        "cell",
+        split_axis=0,
+        concat_axis=0,
+        tiled=True,
+    ).reshape(total, -1)
+    arrived = arrived_all[:, :width]
+    arrived_cells = arrived_all[:, width:]
+    query_parts = gather_by_exchange(arrived.T, "sub")
     decoded = decoded_parts.reshape(-1, decoded_parts.shape[2])
-    cell_ids = arrived_cells.reshape(total, -1).astype(jnp.int32)
+    cell_ids = arrived_cells.astype(jnp.int32)
     probed = jnp.any(
         cell_ids[:, :, None] == jnp.arange(cell_dev, dtype=jnp.int32)[None, None, :], axis=1
     )

time: 168 us -> 161 us (0.958)
  starting transfers between devices: 39.7 us -> 34.3 us
    all_to_all x2 -> x1, starting transfers between devices: 15.7 us -> 9.97 us  [local(): lax.all_to_all(jnp.concatenate([buffer, cell_marks], axis=1).reshape(grou...]
    unnamed x23 -> x21, local copies, waits for them, and re-layouts: 5.11 us -> 4.18 us
    all_to_all x2 -> x1, waiting for transfers between devices: 7.14 us -> 6.43 us  [local(): lax.all_to_all(jnp.concatenate([buffer, cell_marks], axis=1).reshape(grou...]
  transfers between devices with their start and end apart: 6 -> 5, of which waited for: 6 -> 5; matrix products, arithmetic and copies ran while one was open for 12% -> 9% of each run, Pallas kernels for 7% -> 7%
where the time goes in v5:
time: 161 us; the launch traced here: 160 us
  waiting for transfers between devices  50.6 us (31%)
  starting transfers between devices  34.3 us (21%)
  local copies, waits for them, and re-layouts  22.1 us (14%)
  blocking collectives  21 us (13%)
  other arithmetic  13.4 us (8%)
  Pallas kernels  11.7 us (7%)
  matrix products  6.13 us (4%)
    all_to_all x2, blocking collectives, gather_by_exchange(): return lax.all_to_all(copies, axis, split_axis=0, concat_axis=0, tiled=True)  21 us
    all_to_all x1, waiting for transfers between devices, local(): lax.all_to_all(sendable, 'sub', split_axis=0, concat_axis=0, tiled=True)  18.8 us
    all_to_all x1, waiting for transfers between devices, local(): lax.all_to_all(tables, 'sub', split_axis=0, concat_axis=0, tiled=True)  13 us
    pallas_call x1, Pallas kernels, decode(): pl.pallas_call(decode_kernel, grid=(blocks,), in_specs=[pl.BlockSpec((1,...  11.7 us
    all_to_all x1, starting transfers between devices, local(): lax.all_to_all(jnp.concatenate([buffer, cell_marks], axis=1).reshape(grou...  9.97 us
    all_to_all x1, starting transfers between devices, local(): lax.all_to_all(outgoing.reshape(chunk + 2, groups, capacity), 'cell', spl...  9.14 us
    all_to_all x1, waiting for transfers between devices, local(): lax.all_to_all(outgoing.reshape(chunk + 2, groups, capacity), 'cell', spl...  7.68 us
    all_to_all x1, starting transfers between devices, local(): lax.all_to_all(tables, 'sub', split_axis=0, concat_axis=0, tiled=True)  6.76 us
  transfers between devices with their start and end apart: 5, of which 5 were waited for; matrix products, arithmetic and copies ran while one was open for 9% of the time, Pallas kernels for 7%

profile of v5, /device:TPU:1, one launch (start us, length us, event | category | flops | bytes accessed | tf_op | source)
XLA Modules:
  0.0 159.8 jit_solution(2481517459169626185)
XLA Ops:
  0.0 0.8 convert_reduce_fusion.1
  0.8 0.6 reduce-window.6
  1.7 0.7 select_reduce_fusion.1
  2.4 0.7 compare_select_fusion.1
  3.4 0.9 copy.124
  4.2 0.8 convert_element_type.46
  5.2 1.8 %scatter_custom_fusion = bf16[1024,64]{1,0:T(8,128)(2,1)S(1)} fusion(s32[512]{0:T(512)S(1)} %bitcast.118, bf16[512,64]{1,0:T(8,128)(2,1)S(1)} %bitcast.115, bf16[]{:T(256)} %constant.13.clone.1), kind=kCustom, calls=%fused_computation.20 | custom fusion | bytes 131074 | tf_op jit(solution)/shard_map/scatter | solution.py:28
  7.0 1.8 %scatter_custom_fusion.1 = bf16[1024,16]{1,0:T(8,128)(2,1)S(1)} fusion(s32[512]{0:T(512)S(1)} %bitcast.119, bf16[512,16]{1,0:T(8,128)(2,1)S(1)} %bitcast.114, bf16[]{:T(256)} %constant.17.clone.1), kind=kCustom, calls=%fused_computation.18 | custom fusion | bytes 32770 | tf_op jit(solution)/shard_map/scatter | solution.py:30
  8.9 0.9 pad_maximum_fusion.1
  9.8 10.0 %all-to-all-start = ((bf16[16,64,80]{2,1,0:T(8,128)(2,1)}), bf16[16,64,80]{2,1,0:T(8,128)(2,1)S(1)}, u32[]{:S(2)}, u32[]{:S(2)}) async-start(bf16[16,64,80]{2,1,0:T(8,128)(2,1)} %bitcast.5), calls=%async_computation | async-start | bytes 524288 | tf_op jit(solution)/shard_map/all_to_all | solution.py:104
  19.8 0.7 convert_element_type.50
  20.5 0.4 copy.130
  20.9 0.7 reshape.180
  21.9 0.5 broadcast.98
  22.4 1.1 reduce.5
  23.5 1.4 reshape.232
  24.9 6.4 %all-to-all-done = bf16[16,64,80]{2,1,0:T(8,128)(2,1)S(1)} async-done(((bf16[16,64,80]{2,1,0:T(8,128)(2,1)}), bf16[16,64,80]{2,1,0:T(8,128)(2,1)S(1)}, u32[]{:S(2)}, u32[]{:S(2)}) %all-to-all-start) | async-done | bytes 163872 | tf_op jit(solution)/shard_map/all_to_all | solution.py:104
  31.3 6.8 %all-to-all-start.2 = ((bf16[16,2,10752]{2,1,0:T(2,128)(2,1)}), bf16[16,2,10752]{2,1,0:T(2,128)(2,1)S(1)}, u32[]{:S(2)}, u32[]{:S(2)}) async-start(bf16[16,2,10752]{2,1,0:T(2,128)(2,1)} %reshape.232), calls=%async_computation.2 | async-start | bytes 1376256 | tf_op jit(solution)/shard_map/all_to_all | solution.py:89
  38.2 13.0 %all-to-all-done.2 = bf16[16,2,10752]{2,1,0:T(2,128)(2,1)S(1)} async-done(((bf16[16,2,10752]{2,1,0:T(2,128)(2,1)}), bf16[16,2,10752]{2,1,0:T(2,128)(2,1)S(1)}, u32[]{:S(2)}, u32[]{:S(2)}) %all-to-all-start.2) | async-done | bytes 688160 | tf_op jit(solution)/shard_map/all_to_all | solution.py:89
  51.2 1.6 broadcast_in_dim.36
  52.8 4.7 %all-to-all-start.1 = ((bf16[16,64,1024]{2,1,0:T(8,128)(2,1)}), bf16[16,64,1024]{2,1,0:T(8,128)(2,1)}, u32[]{:S(2)}, u32[]{:S(2)}) async-start(bf16[16,64,1024]{2,1,0:T(8,128)(2,1)} %broadcast_in_dim.36), calls=%async_computation.1 | async-start | bytes 4194304 | tf_op jit(solution)/shard_map/all_to_all | solution.py:65
  58.1 0.3 fusion.1
  58.4 0.6 reshape.233
  59.0 0.2 copy.158
  59.6 0.2 broadcast_in_dim.41
  59.8 1.6 copy.135.base_ref
  61.4 1.4 reshape.195
  63.0 1.3 reshape.223.codes_ref
  64.3 1.0 reshape.183.book_ref
  65.3 11.7 %shard_map.82 = bf16[16,64,768]{2,1,0:T(8,128)(2,1)} custom-call(s32[16,4,768]{2,1,0:T(4,128)} %reshape.223.codes_ref, bf16[64,16,256]{2,1,0:T(8,128)(2,1)} %reshape.183.book_ref, bf16[1024,768]{1,0:T(8,128)(2,1)} %copy.135.base_ref), custom_call_target="tpu_custom_call" | custom-call | tf_op jit(solution)/shard_map/pallas_call | solution.py:49
  77.0 1.9 %multiply_reduce_fusion = f32[768]{0:T(1024)S(1)} fusion(bf16[16,64,768]{2,1,0:T(8,128)(2,1)} %shard_map.82), kind=kLoop, calls=%fused_computation.8 | loop fusion | flops 2358528 | bytes 1575936 | tf_op jit(solution)/shard_map/reduce_sum | solution.py:121
  78.9 4.7 %all-to-all-done.1 = bf16[16,64,1024]{2,1,0:T(8,128)(2,1)} async-done(((bf16[16,64,1024]{2,1,0:T(8,128)(2,1)}), bf16[16,64,1024]{2,1,0:T(8,128)(2,1)}, u32[]{:S(2)}, u32[]{:S(2)}) %all-to-all-start.1) | async-done | bytes 2097184 | tf_op jit(solution)/shard_map/all_to_all | solution.py:65
  83.7 5.5 %select_reduce_fusion = (f32[1024]{0:T(1024)S(1)}, f32[1024,768,1]{0,1,2:T(8,128)}) fusion(f32[768]{0:T(1024)S(1)} %broadcast_multiply_fusion, pred[768]{0:T(1024)(128)(4,1)S(1)} %lt.43, pred[1024,32]{0,1:T(8,128)(4,1)S(1)} %fusion.1, bf16[16,64,1024]{2,1,0:T(8,128)(2,1)} %all-to-all-done.1, bf16[16,64,768]{2,1,0:T(8,128)(2,1)S(1)} %copy-done.1), kind=kOutput, calls=%fused_computation.7 | convolution fusion | flops 1614543872 | bytes 6856448 | tf_op jit(solution)/shard_map/sdq,sdr->qr/dot_general | solution.py:127
  89.2 11.7 %all_to_all.43 = f32[16,1,1024]{2,1,0:T(1,128)S(1)} all-to-all(f32[16,1,1024]{2,1,0:T(1,128)S(1)} %broadcast_in_dim.43), channel_id=1, replica_groups=mesh['cell'=16,'sub'=16] {'sub'}, dimensions={0} | all-to-all | bytes 131072 | tf_op jit(solution)/shard_map/all_to_all | solution.py:65
  101.0 3.0 %convert_reduce_fusion = (f32[1024]{0:T(1024)S(1)}, bf16[1024,768]{0,1:T(8,128)(2,1)S(1)}) fusion(f32[1024]{0:T(1024)S(1)} %reduce_max.28, f32[768]{0:T(1024)S(1)} %broadcast_multiply_fusion, f32[1024,768,1]{0,1,2:T(8,128)} %get-tuple-element.10, pred[768]{0:T(1024)(128)(4,1)S(1)} %lt.43, pred[1024,32]{0,1:T(8,128)(4,1)S(1)} %fusion.1), kind=kLoop, calls=%fused_computation.5 | loop fusion | flops 6290432 | bytes 4763392 | tf_op jit(solution)/shard_map/reduce_sum | solution.py:133
  104.0 0.6 fusion.11
  104.7 1.3 pad_maximum_fusion
  106.0 3.7 %all-to-all-start.4 = ((f32[16,17,1024]{2,1,0:T(8,128)}), f32[16,17,1024]{2,1,0:T(8,128)S(1)}, u32[]{:S(2)}, u32[]{:S(2)}) async-start(f32[16,17,1024]{2,1,0:T(8,128)} %pad_maximum_fusion), calls=%async_computation.4 | async-start | bytes 3145728 | tf_op jit(solution)/shard_map/all_to_all | solution.py:144
  109.8 18.8 %all-to-all-done.4 = f32[16,17,1024]{2,1,0:T(8,128)S(1)} async-done(((f32[16,17,1024]{2,1,0:T(8,128)}), f32[16,17,1024]{2,1,0:T(8,128)S(1)}, u32[]{:S(2)}, u32[]{:S(2)}) %all-to-all-start.4) | async-done | bytes 1114144 | tf_op jit(solution)/shard_map/all_to_all | solution.py:144
  128.8 0.8 reshape.234
  129.6 9.1 %all-to-all-start.5 = ((f32[16,1,1152]{2,1,0:T(1,128)}), f32[16,1,1152]{2,1,0:T(1,128)S(1)}, u32[]{:S(2)}, u32[]{:S(2)}) async-start(f32[16,1,1152]{2,1,0:T(1,128)} %reshape.234), calls=%async_computation.5 | async-start | bytes 147456 | tf_op jit(solution)/shard_map/all_to_all | solution.py:147
  139.0 7.7 %all-to-all-done.5 = f32[16,1,1152]{2,1,0:T(1,128)S(1)} async-done(((f32[16,1,1152]{2,1,0:T(1,128)}), f32[16,1,1152]{2,1,0:T(1,128)S(1)}, u32[]{:S(2)}, u32[]{:S(2)}) %all-to-all-start.5) | async-done | bytes 73760 | tf_op jit(solution)/shard_map/all_to_all | solution.py:147
  146.7 0.5 broadcast.99
  147.2 0.8 reduce.6
  148.1 0.2 copy.138
  148.4 1.0 gather_fusion
  149.7 9.3 %all_to_all.44 = bf16[16,16,256]{2,1,0:T(8,128)(2,1)S(1)} all-to-all(bf16[16,16,256]{2,1,0:T(8,128)(2,1)S(1)} %broadcast_in_dim.91), channel_id=1, replica_groups=mesh['cell'=16,'sub'=16] {'sub'}, dimensions={0} | all-to-all | bytes 262144 | tf_op jit(solution)/shard_map/all_to_all | solution.py:65
  159.0 0.8 copy.141
  (66 shorter events, 3.3 us)
Async XLA Ops:
  0.0 104.0 %copy-start = (bf16[32,24,256]{2,1,0:T(8,128)(2,1)S(1)}, bf16[32,24,256]{2,1,0:T(8,128)(2,1)}, u32[]{:S(2)}) copy-start(bf16[32,24,256]{2,1,0:T(8,128)(2,1)} %param.15) | copy-start | bytes 1179652
  0.0 19.7 %copy-start.2 = (s32[32,4,384]{2,1,0:T(4,128)S(1)}, s32[32,4,384]{2,1,0:T(4,128)}, u32[]{:S(2)}) copy-start(s32[32,4,384]{2,1,0:T(4,128)} %param.13) | copy-start | bytes 589828
  8.9 12.7 %copy-start.3 = (bf16[4,16,256]{2,1,0:T(8,128)(2,1)S(1)}, bf16[4,16,256]{2,1,0:T(8,128)(2,1)}, u32[]{:S(2)}) copy-start(bf16[4,16,256]{2,1,0:T(8,128)(2,1)} %param.12) | copy-start | bytes 98308
  8.9 12.8 %copy-start.4 = (bf16[32,64]{1,0:T(8,128)(2,1)S(1)}, bf16[32,64]{1,0:T(8,128)(2,1)}, u32[]{:S(2)}) copy-start(bf16[32,64]{1,0:T(8,128)(2,1)} %param.11) | copy-start | bytes 12292
  9.8 21.6 %all-to-all-start = ((bf16[16,64,80]{2,1,0:T(8,128)(2,1)}), bf16[16,64,80]{2,1,0:T(8,128)(2,1)S(1)}, u32[]{:S(2)}, u32[]{:S(2)}) async-start(bf16[16,64,80]{2,1,0:T(8,128)(2,1)} %bitcast.5), calls=%async_computation | async-start | bytes 524288 | tf_op jit(solution)/shard_map/all_to_all | solution.py:104
  31.3 19.9 %all-to-all-start.2 = ((bf16[16,2,10752]{2,1,0:T(2,128)(2,1)}), bf16[16,2,10752]{2,1,0:T(2,128)(2,1)S(1)}, u32[]{:S(2)}, u32[]{:S(2)}) async-start(bf16[16,2,10752]{2,1,0:T(2,128)(2,1)} %reshape.232), calls=%async_computation.2 | async-start | bytes 1376256 | tf_op jit(solution)/shard_map/all_to_all | solution.py:89
  52.8 4.9 %copy-start.5 = (s32[32]{0:T(128)S(1)}, s32[32]{0:T(128)}, u32[]{:S(2)}) copy-start(s32[32]{0:T(128)} %param.14) | copy-start | bytes 388
  52.8 30.9 %all-to-all-start.1 = ((bf16[16,64,1024]{2,1,0:T(8,128)(2,1)}), bf16[16,64,1024]{2,1,0:T(8,128)(2,1)}, u32[]{:S(2)}, u32[]{:S(2)}) async-start(bf16[16,64,1024]{2,1,0:T(8,128)(2,1)} %broadcast_in_dim.36), calls=%async_computation.1 | async-start | bytes 4194304 | tf_op jit(solution)/shard_map/all_to_all | solution.py:65
  77.0 6.7 %copy-start.1 = (bf16[16,64,768]{2,1,0:T(8,128)(2,1)S(1)}, bf16[16,64,768]{2,1,0:T(8,128)(2,1)}, u32[]{:S(2)}) copy-start(bf16[16,64,768]{2,1,0:T(8,128)(2,1)} %shard_map.82) | copy-start | bytes 4718596
  106.0 22.6 %all-to-all-start.4 = ((f32[16,17,1024]{2,1,0:T(8,128)}), f32[16,17,1024]{2,1,0:T(8,128)S(1)}, u32[]{:S(2)}, u32[]{:S(2)}) async-start(f32[16,17,1024]{2,1,0:T(8,128)} %pad_maximum_fusion), calls=%async_computation.4 | async-start | bytes 3145728 | tf_op jit(solution)/shard_map/all_to_all | solution.py:144
  129.6 17.1 %all-to-all-start.5 = ((f32[16,1,1152]{2,1,0:T(1,128)}), f32[16,1,1152]{2,1,0:T(1,128)S(1)}, u32[]{:S(2)}, u32[]{:S(2)}) async-start(f32[16,1,1152]{2,1,0:T(1,128)} %reshape.234), calls=%async_computation.5 | async-start | bytes 147456 | tf_op jit(solution)/shard_map/all_to_all | solution.py:147

commit v6 on v5

--- a/solution.py
+++ b/solution.py
@@ -102,7 +102,7 @@
     buffer, cell_marks = pack_slots(queries, probe_cells, slots, total)
     width = buffer.shape[1]
     arrived_all = lax.all_to_all(
-        jnp.concatenate([buffer, cell_marks], axis=1).reshape(groups, capacity, -1),
+        jnp.concatenate([buffer, cell_marks], axis=1).reshape(groups, -1),
         "cell",
         split_axis=0,
         concat_axis=0,
@@ -127,9 +127,7 @@
     raw = jnp.einsum("sdq,sdr->qr", query_parts, decoded_parts, preferred_element_type=jnp.float32)
     values = (raw - 0.5 * sq_norm[None, :]) * score_scale
     local_peak = jnp.max(jnp.where(keep, values, floor_score), axis=1)
-    peak = jnp.max(gather_by_exchange(local_peak, "sub"), axis=0)
-
-    weights = jnp.where(keep, jnp.exp(values - peak[:, None]), 0.0).astype(jnp.bfloat16)
+    weights = jnp.where(keep, jnp.exp(values - local_peak[:, None]), 0.0).astype(jnp.bfloat16)
     mass = jnp.sum(weights.astype(jnp.float32), axis=1)
     part_t = lax.dot_general(
         table, weights, (((0,), (1,)), ((), ())), preferred_element_type=jnp.float32
@@ -138,11 +136,15 @@
         [
             part_t.reshape(parts, chunk, total),
             jnp.broadcast_to(mass[None, None, :], (parts, 1, total)),
+            jnp.broadcast_to(local_peak[None, None, :], (parts, 1, total)),
         ],
         axis=1,
     )
     pieces = lax.all_to_all(sendable, "sub", split_axis=0, concat_axis=0, tiled=True)
-    reduced = jnp.sum(pieces, axis=0)
+    peaks_in = pieces[:, chunk + 1, :]
+    peak = jnp.max(peaks_in, axis=0)
+    shift = jnp.exp(peaks_in - peak[None, :])
+    reduced = jnp.sum(shift[:, None, :] * pieces[:, : chunk + 1, :], axis=0)
     outgoing = jnp.concatenate([reduced, peak[None, :]], axis=0)
     back = lax.all_to_all(
         outgoing.reshape(chunk + 2, groups, capacity), "cell", split_axis=1, concat_axis=1, tiled=True

time: 161 us -> 146 us (0.907)
  waiting for transfers between devices: 50.6 us -> 28.1 us
  blocking collectives: 21 us -> 33.9 us
  starting transfers between devices: 34.3 us -> 29.6 us
    all_to_all x0 -> x1, blocking collectives: none -> 24.2 us  [local(): lax.all_to_all(sendable, 'sub', split_axis=0, concat_axis=0, tiled=True)]
    all_to_all x1 -> x0, waiting for transfers between devices: 18.8 us -> none  [local(): lax.all_to_all(sendable, 'sub', split_axis=0, concat_axis=0, tiled=True)]
    all_to_all x2 -> x1, blocking collectives: 21 us -> 9.72 us  [gather_by_exchange(): return lax.all_to_all(copies, axis, split_axis=0, concat_axis=0, tiled=True)]
    all_to_all x1 -> x0, starting transfers between devices: 3.71 us -> none  [local(): lax.all_to_all(sendable, 'sub', split_axis=0, concat_axis=0, tiled=True)]
    all_to_all x0 -> x2, other arithmetic: none -> 2.52 us  [local(): lax.all_to_all(jnp.concatenate([buffer, cell_marks], axis=1).reshape(grou...]
    reduce_sum x1, other arithmetic: 3 us -> 1.13 us  [local(): mass = jnp.sum(weights.astype(jnp.float32), axis=1)]
    all_to_all x1, waiting for transfers between devices: 13 us -> 11.2 us  [local(): lax.all_to_all(tables, 'sub', split_axis=0, concat_axis=0, tiled=True)]
    unnamed x21 -> x23, local copies, waits for them, and re-layouts: 4.18 us -> 4.95 us
  transfers between devices with their start and end apart: 5 -> 4, of which waited for: 5 -> 4; matrix products, arithmetic and copies ran while one was open for 9% -> 11% of each run, Pallas kernels for 7% -> 8%
where the time goes in v6:
time: 146 us; the launch traced here: 144 us
  blocking collectives  33.9 us (23%)
  starting transfers between devices  29.6 us (20%)
  waiting for transfers between devices  28.1 us (19%)
  local copies, waits for them, and re-layouts  23.7 us (16%)
  other arithmetic  12.5 us (9%)
  Pallas kernels  11.7 us (8%)
  matrix products  4.53 us (3%)
    all_to_all x1, blocking collectives, local(): lax.all_to_all(sendable, 'sub', split_axis=0, concat_axis=0, tiled=True)  24.2 us
    pallas_call x1, Pallas kernels, decode(): pl.pallas_call(decode_kernel, grid=(blocks,), in_specs=[pl.BlockSpec((1,...  11.7 us
    all_to_all x1, waiting for transfers between devices, local(): lax.all_to_all(tables, 'sub', split_axis=0, concat_axis=0, tiled=True)  11.2 us
    all_to_all x1, starting transfers between devices, local(): lax.all_to_all(jnp.concatenate([buffer, cell_marks], axis=1).reshape(grou...  10.1 us
    all_to_all x1, blocking collectives, gather_by_exchange(): return lax.all_to_all(copies, axis, split_axis=0, concat_axis=0, tiled=True)  9.72 us
    all_to_all x1, starting transfers between devices, local(): lax.all_to_all(outgoing.reshape(chunk + 2, groups, capacity), 'cell', spl...  7.97 us
    all_to_all x1, waiting for transfers between devices, local(): lax.all_to_all(outgoing.reshape(chunk + 2, groups, capacity), 'cell', spl...  7.68 us
    all_to_all x1, starting transfers between devices, local(): lax.all_to_all(tables, 'sub', split_axis=0, concat_axis=0, tiled=True)  6.76 us
  transfers between devices with their start and end apart: 4, of which 4 were waited for; matrix products, arithmetic and copies ran while one was open for 11% of the time, Pallas kernels for 8%

profile of v6, /device:TPU:1, one launch (start us, length us, event | category | flops | bytes accessed | tf_op | source)
XLA Modules:
  0.0 144.5 jit_solution(2014067305594589702)
XLA Ops:
  0.0 0.7 convert_reduce_fusion.1
  0.7 0.6 reduce-window.6
  1.6 0.7 select_reduce_fusion.1
  2.4 0.7 compare_select_fusion.1
  3.3 0.9 copy.118
  4.2 0.8 convert_element_type.46
  5.2 1.8 %scatter_custom_fusion = bf16[1024,64]{1,0:T(8,128)(2,1)S(1)} fusion(s32[512]{0:T(512)S(1)} %bitcast.117, bf16[512,64]{1,0:T(8,128)(2,1)S(1)} %bitcast.114, bf16[]{:T(256)} %constant.13.clone.1), kind=kCustom, calls=%fused_computation.23 | custom fusion | bytes 131074 | tf_op jit(solution)/shard_map/scatter | solution.py:28
  7.0 1.8 %scatter_custom_fusion.1 = bf16[1024,16]{1,0:T(8,128)(2,1)S(1)} fusion(s32[512]{0:T(512)S(1)} %bitcast.118, bf16[512,16]{1,0:T(8,128)(2,1)S(1)} %bitcast.113, bf16[]{:T(256)} %constant.17.clone.1), kind=kCustom, calls=%fused_computation.21 | custom fusion | bytes 32770 | tf_op jit(solution)/shard_map/scatter | solution.py:30
  9.0 0.3 all_to_all.35
  9.4 0.5 broadcast.101
  9.9 1.6 %reduce.7 = bf16[16,5120]{1,0:T(8,128)(2,1)S(1)} reduce(bf16[16,1,5120]{2,1,0:T(2,128)(2,1)S(1)} %all_to_all.35, bf16[]{:T(256)} %broadcast.101), dimensions={1}, to_apply=%all_to_all.35.reduce_sub_computation | reduce | bytes 327682 | tf_op jit(solution)/shard_map/all_to_all | solution.py:104
  11.5 0.8 reshape.237
  12.2 10.1 %all-to-all-start = ((bf16[16,2,2560]{2,1,0:T(2,128)(2,1)}), bf16[16,2,2560]{2,1,0:T(2,128)(2,1)S(1)}, u32[]{:S(2)}, u32[]{:S(2)}) async-start(bf16[16,2,2560]{2,1,0:T(2,128)(2,1)} %reshape.237), calls=%async_computation | async-start | bytes 327680 | tf_op jit(solution)/shard_map/all_to_all | solution.py:104
  22.4 0.7 convert_element_type.50
  23.1 0.4 copy.124
  23.5 0.7 reshape.184
  24.5 1.2 reduce.6
  25.6 1.4 reshape.239
  27.0 4.9 %all-to-all-done = bf16[16,2,2560]{2,1,0:T(2,128)(2,1)S(1)} async-done(((bf16[16,2,2560]{2,1,0:T(2,128)(2,1)}), bf16[16,2,2560]{2,1,0:T(2,128)(2,1)S(1)}, u32[]{:S(2)}, u32[]{:S(2)}) %all-to-all-start) | async-done | bytes 163872 | tf_op jit(solution)/shard_map/all_to_all | solution.py:104
  31.9 6.8 %all-to-all-start.2 = ((bf16[16,2,10752]{2,1,0:T(2,128)(2,1)}), bf16[16,2,10752]{2,1,0:T(2,128)(2,1)S(1)}, u32[]{:S(2)}, u32[]{:S(2)}) async-start(bf16[16,2,10752]{2,1,0:T(2,128)(2,1)} %reshape.239), calls=%async_computation.2 | async-start | bytes 1376256 | tf_op jit(solution)/shard_map/all_to_all | solution.py:89
  38.8 0.9 reduce.4
  39.7 0.3 reshape.183
  40.2 11.2 %all-to-all-done.2 = bf16[16,2,10752]{2,1,0:T(2,128)(2,1)S(1)} async-done(((bf16[16,2,10752]{2,1,0:T(2,128)(2,1)}), bf16[16,2,10752]{2,1,0:T(2,128)(2,1)S(1)}, u32[]{:S(2)}, u32[]{:S(2)}) %all-to-all-start.2) | async-done | bytes 688160 | tf_op jit(solution)/shard_map/all_to_all | solution.py:89
  51.4 1.6 %broadcast_in_dim.36 = bf16[16,64,1024]{2,1,0:T(8,128)(2,1)} broadcast(bf16[64,1024]{1,0:T(8,128)(2,1)S(1)} %copy.122), dimensions={1,2} | broadcast | bytes 2228224 | tf_op jit(solution)/shard_map/broadcast_in_dim | solution.py:64
  53.0 4.7 %all-to-all-start.1 = ((bf16[16,64,1024]{2,1,0:T(8,128)(2,1)}), bf16[16,64,1024]{2,1,0:T(8,128)(2,1)}, u32[]{:S(2)}, u32[]{:S(2)}) async-start(bf16[16,64,1024]{2,1,0:T(8,128)(2,1)} %broadcast_in_dim.36), calls=%async_computation.1 | async-start | bytes 4194304 | tf_op jit(solution)/shard_map/all_to_all | solution.py:65
  58.3 0.3 fusion.1
  58.6 0.6 reshape.240
  60.0 1.6 %copy.129.base_ref = bf16[1024,768]{1,0:T(8,128)(2,1)} copy(bf16[1024,768]{0,1:T(8,128)(2,1)S(1)} %bitcast.97) | data formatting | bytes 3145728 | tf_op jit(solution)/shard_map/reshape | solution.py:98
  61.6 1.4 reshape.199
  63.2 1.3 reshape.227.codes_ref
  64.5 1.0 reshape.187.book_ref
  65.5 11.7 %shard_map.82 = bf16[16,64,768]{2,1,0:T(8,128)(2,1)} custom-call(s32[16,4,768]{2,1,0:T(4,128)} %reshape.227.codes_ref, bf16[64,16,256]{2,1,0:T(8,128)(2,1)} %reshape.187.book_ref, bf16[1024,768]{1,0:T(8,128)(2,1)} %copy.129.base_ref), custom_call_target="tpu_custom_call" | custom-call | tf_op jit(solution)/shard_map/pallas_call | solution.py:49
  77.2 1.9 %multiply_reduce_fusion = f32[768]{0:T(1024)S(1)} fusion(bf16[16,64,768]{2,1,0:T(8,128)(2,1)} %shard_map.82), kind=kLoop, calls=%fused_computation.8 | loop fusion | flops 2358528 | bytes 1575936 | tf_op jit(solution)/shard_map/reduce_sum | solution.py:121
  79.1 4.3 %all-to-all-done.1 = bf16[16,64,1024]{2,1,0:T(8,128)(2,1)} async-done(((bf16[16,64,1024]{2,1,0:T(8,128)(2,1)}), bf16[16,64,1024]{2,1,0:T(8,128)(2,1)}, u32[]{:S(2)}, u32[]{:S(2)}) %all-to-all-start.1) | async-done | bytes 2097184 | tf_op jit(solution)/shard_map/all_to_all | solution.py:65
  83.4 3.9 %select_reduce_fusion = (f32[1024]{0:T(1024)S(1)}, f32[1024,768,1]{0,1,2:T(8,128)S(1)}) fusion(f32[768]{0:T(1024)S(1)} %broadcast_multiply_fusion, pred[768]{0:T(1024)(128)(4,1)S(1)} %lt.43, pred[1024,32]{0,1:T(8,128)(4,1)S(1)} %fusion.1, bf16[16,64,1024]{2,1,0:T(8,128)(2,1)} %all-to-all-done.1, bf16[16,64,768]{2,1,0:T(8,128)(2,1)S(1)} %copy-done.1), kind=kOutput, calls=%fused_computation.7 | convolution fusion | flops 1614543872 | bytes 6856448 | tf_op jit(solution)/shard_map/sdq,sdr->qr/dot_general | solution.py:127
  87.3 1.1 convert_reduce_fusion
  88.5 0.6 fusion.12
  89.2 0.2 pad_maximum_fusion
  89.4 24.2 %all_to_all.42 = f32[16,18,1024]{2,1,0:T(8,128)S(1)} all-to-all(f32[16,18,1024]{2,1,0:T(8,128)S(1)} %pad_maximum_fusion), channel_id=1, replica_groups=mesh['cell'=16,'sub'=16] {'sub'}, dimensions={0} | all-to-all | bytes 2359296 | tf_op jit(solution)/shard_map/all_to_all | solution.py:143
  114.3 0.8 reshape.241
  115.0 8.0 %all-to-all-start.4 = ((f32[16,1,1152]{2,1,0:T(1,128)}), f32[16,1,1152]{2,1,0:T(1,128)S(1)}, u32[]{:S(2)}, u32[]{:S(2)}) async-start(f32[16,1,1152]{2,1,0:T(1,128)} %reshape.241), calls=%async_computation.4 | async-start | bytes 147456 | tf_op jit(solution)/shard_map/all_to_all | solution.py:149
  123.3 7.7 %all-to-all-done.4 = f32[16,1,1152]{2,1,0:T(1,128)S(1)} async-done(((f32[16,1,1152]{2,1,0:T(1,128)}), f32[16,1,1152]{2,1,0:T(1,128)S(1)}, u32[]{:S(2)}, u32[]{:S(2)}) %all-to-all-start.4) | async-done | bytes 73760 | tf_op jit(solution)/shard_map/all_to_all | solution.py:149
  131.0 0.5 broadcast.103
  131.5 0.8 reduce.8
  132.4 0.2 copy.131
  132.7 1.0 gather_fusion
  134.0 9.7 %all_to_all.43 = bf16[16,16,256]{2,1,0:T(8,128)(2,1)S(1)} all-to-all(bf16[16,16,256]{2,1,0:T(8,128)(2,1)S(1)} %broadcast_in_dim.47), channel_id=1, replica_groups=mesh['cell'=16,'sub'=16] {'sub'}, dimensions={0} | all-to-all | bytes 262144 | tf_op jit(solution)/shard_map/all_to_all | solution.py:65
  143.7 0.8 copy.134
  (73 shorter events, 4.3 us)
Async XLA Ops:
  0.0 88.5 %copy-start = (bf16[32,24,256]{2,1,0:T(8,128)(2,1)S(1)}, bf16[32,24,256]{2,1,0:T(8,128)(2,1)}, u32[]{:S(2)}) copy-start(bf16[32,24,256]{2,1,0:T(8,128)(2,1)} %param.15) | copy-start | bytes 1179652
  5.2 17.1 %copy-start.2 = (s32[32,4,384]{2,1,0:T(4,128)S(1)}, s32[32,4,384]{2,1,0:T(4,128)}, u32[]{:S(2)}) copy-start(s32[32,4,384]{2,1,0:T(4,128)} %param.13) | copy-start | bytes 589828
  12.2 12.0 %copy-start.3 = (bf16[4,16,256]{2,1,0:T(8,128)(2,1)S(1)}, bf16[4,16,256]{2,1,0:T(8,128)(2,1)}, u32[]{:S(2)}) copy-start(bf16[4,16,256]{2,1,0:T(8,128)(2,1)} %param.12) | copy-start | bytes 98308
  12.2 12.0 %copy-start.4 = (bf16[32,64]{1,0:T(8,128)(2,1)S(1)}, bf16[32,64]{1,0:T(8,128)(2,1)}, u32[]{:S(2)}) copy-start(bf16[32,64]{1,0:T(8,128)(2,1)} %param.11) | copy-start | bytes 12292
  12.2 19.6 %all-to-all-start = ((bf16[16,2,2560]{2,1,0:T(2,128)(2,1)}), bf16[16,2,2560]{2,1,0:T(2,128)(2,1)S(1)}, u32[]{:S(2)}, u32[]{:S(2)}) async-start(bf16[16,2,2560]{2,1,0:T(2,128)(2,1)} %reshape.237), calls=%async_computation | async-start | bytes 327680 | tf_op jit(solution)/shard_map/all_to_all | solution.py:104
  31.9 19.6 %all-to-all-start.2 = ((bf16[16,2,10752]{2,1,0:T(2,128)(2,1)}), bf16[16,2,10752]{2,1,0:T(2,128)(2,1)S(1)}, u32[]{:S(2)}, u32[]{:S(2)}) async-start(bf16[16,2,10752]{2,1,0:T(2,128)(2,1)} %reshape.239), calls=%async_computation.2 | async-start | bytes 1376256 | tf_op jit(solution)/shard_map/all_to_all | solution.py:89
  53.0 4.9 %copy-start.5 = (s32[32]{0:T(128)S(1)}, s32[32]{0:T(128)}, u32[]{:S(2)}) copy-start(s32[32]{0:T(128)} %param.14) | copy-start | bytes 388
  53.0 30.4 %all-to-all-start.1 = ((bf16[16,64,1024]{2,1,0:T(8,128)(2,1)}), bf16[16,64,1024]{2,1,0:T(8,128)(2,1)}, u32[]{:S(2)}, u32[]{:S(2)}) async-start(bf16[16,64,1024]{2,1,0:T(8,128)(2,1)} %broadcast_in_dim.36), calls=%async_computation.1 | async-start | bytes 4194304 | tf_op jit(solution)/shard_map/all_to_all | solution.py:65
  77.2 6.2 %copy-start.1 = (bf16[16,64,768]{2,1,0:T(8,128)(2,1)S(1)}, bf16[16,64,768]{2,1,0:T(8,128)(2,1)}, u32[]{:S(2)}) copy-start(bf16[16,64,768]{2,1,0:T(8,128)(2,1)} %shard_map.82) | copy-start | bytes 4718596
  115.0 16.0 %all-to-all-start.4 = ((f32[16,1,1152]{2,1,0:T(1,128)}), f32[16,1,1152]{2,1,0:T(1,128)S(1)}, u32[]{:S(2)}, u32[]{:S(2)}) async-start(f32[16,1,1152]{2,1,0:T(1,128)} %reshape.241), calls=%async_computation.4 | async-start | bytes 147456 | tf_op jit(solution)/shard_map/all_to_all | solution.py:149

commit v7 on v6

--- a/solution.py
+++ b/solution.py
@@ -57,6 +57,45 @@
         out_specs=pl.BlockSpec((1, per_block * width, n), lambda p: (p, 0, 0)),
         out_shape=jax.ShapeDtypeStruct((blocks, per_block * width, n), jnp.bfloat16),
     )(codes_blocks, codebooks, base)
+
+
+def score_kernel(x_ref, q_ref, half_ref, keep_ref, table_ref, out_ref):
+    chunk = out_ref.shape[1] - 2
+    raw = lax.dot_general(
+        x_ref[...], q_ref[...], (((0,), (0,)), ((), ())), preferred_element_type=jnp.float32
+    )
+    values = (raw - half_ref[...]) * score_scale
+    keep = keep_ref[...] > 0
+    peak = jnp.max(jnp.where(keep, values, floor_score), axis=0, keepdims=True)
+    weights = jnp.where(keep, jnp.exp(values - peak), 0.0).astype(jnp.bfloat16)
+    mass = jnp.sum(weights.astype(jnp.float32), axis=0, keepdims=True)
+    part = lax.dot_general(
+        table_ref[...], weights, (((0,), (0,)), ((), ())), preferred_element_type=jnp.float32
+    )
+    for dest in range(out_ref.shape[0]):
+        out_ref[dest, :chunk, :] = part[dest * chunk : (dest + 1) * chunk, :]
+        out_ref[dest, chunk : chunk + 1, :] = mass
+        out_ref[dest, chunk + 1 : chunk + 2, :] = peak
+
+
+def score_terms(decoded, queries_t, half_norm, keep_t, table, parts, block):
+    dims, rows = decoded.shape
+    total = queries_t.shape[1]
+    width = table.shape[1]
+    chunk = width // parts
+    return pl.pallas_call(
+        score_kernel,
+        grid=(total // block,),
+        in_specs=[
+            pl.BlockSpec((dims, rows), lambda j: (0, 0)),
+            pl.BlockSpec((dims, block), lambda j: (0, j)),
+            pl.BlockSpec((rows, 1), lambda j: (0, 0)),
+            pl.BlockSpec((rows, block), lambda j: (0, j)),
+            pl.BlockSpec((rows, width), lambda j: (0, 0)),
+        ],
+        out_specs=pl.BlockSpec((parts, chunk + 2, block), lambda j: (0, 0, j)),
+        out_shape=jax.ShapeDtypeStruct((parts, chunk + 2, total), jnp.float32),
+    )(decoded, queries_t, half_norm, keep_t, table)
 
 
 def gather_by_exchange(x, axis):
@@ -121,24 +160,12 @@
     sq_norm = jnp.sum(jnp.square(decoded.astype(jnp.float32)), axis=0)
     first_row = lax.axis_index("sub") * row_local
     live = (first_row + jnp.arange(row_local, dtype=jnp.int32))[None, :] < lengths[:, None]
-    keep = (probed[:, :, None] & live[None, :, :]).reshape(total, -1)
+    keep_t = (live[:, :, None] & jnp.transpose(probed)[:, None, :]).reshape(-1, total)
+    keep_t = keep_t.astype(jnp.bfloat16)
     table = payload.reshape(-1, pw)
-
-    raw = jnp.einsum("sdq,sdr->qr", query_parts, decoded_parts, preferred_element_type=jnp.float32)
-    values = (raw - 0.5 * sq_norm[None, :]) * score_scale
-    local_peak = jnp.max(jnp.where(keep, values, floor_score), axis=1)
-    weights = jnp.where(keep, jnp.exp(values - local_peak[:, None]), 0.0).astype(jnp.bfloat16)
-    mass = jnp.sum(weights.astype(jnp.float32), axis=1)
-    part_t = lax.dot_general(
-        table, weights, (((0,), (1,)), ((), ())), preferred_element_type=jnp.float32
-    )
-    sendable = jnp.concatenate(
-        [
-            part_t.reshape(parts, chunk, total),
-            jnp.broadcast_to(mass[None, None, :], (parts, 1, total)),
-            jnp.broadcast_to(local_peak[None, None, :], (parts, 1, total)),
-        ],
-        axis=1,
+    half_norm = (0.5 * sq_norm)[:, None]
+    sendable = score_terms(
+        decoded, query_parts.reshape(-1, total), half_norm, keep_t, table, parts, 256
     )
     pieces = lax.all_to_all(sendable, "sub", split_axis=0, concat_axis=0, tiled=True)
     peaks_in = pieces[:, chunk + 1, :]

time: 146 us -> 157 us (1.075)
  local copies, waits for them, and re-layouts: 23.7 us -> 34.9 us
  Pallas kernels: 11.7 us -> 19.5 us
  matrix products: 4.53 us -> 0 us
  waiting for transfers between devices: 28.1 us -> 23.8 us
  blocking collectives: 33.9 us -> 36.8 us
  starting transfers between devices: 29.6 us -> 27.2 us
    pallas_call x0 -> x1, Pallas kernels: none -> 7.81 us  [score_terms(): pl.pallas_call(score_kernel, grid=(total // block,), in_specs=[pl.BlockSp...]
    unnamed x23 -> x25, local copies, waits for them, and re-layouts: 4.95 us -> 9.88 us
    dot_general x2 -> x0, matrix products: 4.53 us -> none  [the longest x1 3.91 us: local(): jnp.einsum('sdq,sdr->qr', query_parts, decoded_parts, preferred_element_t...]
    all_to_all x1, waiting for transfers between devices: 4.29 us -> 0.01 us  [gather_by_exchange(): return lax.all_to_all(copies, axis, split_axis=0, concat_axis=0, tiled=True)]
    all_to_all x1, blocking collectives: 24.2 us -> 27.1 us  [local(): lax.all_to_all(sendable, 'sub', split_axis=0, concat_axis=0, tiled=True)]
    reshape x3, local copies, waits for them, and re-layouts: 2.84 us -> 5.1 us  [local(): got_codes = got_codes.reshape(parts, sub_count, cell_count * rows_part)]
    all_to_all x1, starting transfers between devices: 7.97 us -> 6.34 us  [local(): lax.all_to_all(outgoing.reshape(chunk + 2, groups, capacity), 'cell', spl...]
  transfers between devices with their start and end apart: 4 -> 4, of which waited for: 4 -> 3; matrix products, arithmetic and copies ran while one was open for 11% -> 18% of each run, Pallas kernels for 8% -> 8%
where the time goes in v7:
time: 157 us; the launch traced here: 155 us
  blocking collectives  36.8 us (23%)
  local copies, waits for them, and re-layouts  34.9 us (22%)
  starting transfers between devices  27.2 us (17%)
  waiting for transfers between devices  23.8 us (15%)
  Pallas kernels  19.5 us (12%)
  other arithmetic  12.5 us (8%)
    all_to_all x1, blocking collectives, local(): lax.all_to_all(sendable, 'sub', split_axis=0, concat_axis=0, tiled=True)  27.1 us
    pallas_call x1, Pallas kernels, decode(): pl.pallas_call(decode_kernel, grid=(blocks,), in_specs=[pl.BlockSpec((1,...  11.7 us
    all_to_all x1, waiting for transfers between devices, local(): lax.all_to_all(tables, 'sub', split_axis=0, concat_axis=0, tiled=True)  11.2 us
    all_to_all x1, starting transfers between devices, local(): lax.all_to_all(jnp.concatenate([buffer, cell_marks], axis=1).reshape(grou...  10.1 us
    unnamed x25, local copies, waits for them, and re-layouts  9.88 us
    all_to_all x1, blocking collectives, gather_by_exchange(): return lax.all_to_all(copies, axis, split_axis=0, concat_axis=0, tiled=True)  9.72 us
    pallas_call x1, Pallas kernels, score_terms(): pl.pallas_call(score_kernel, grid=(total // block,), in_specs=[pl.BlockSp...  7.81 us
    all_to_all x1, waiting for transfers between devices, local(): lax.all_to_all(outgoing.reshape(chunk + 2, groups, capacity), 'cell', spl...  7.68 us
  transfers between devices with their start and end apart: 4, of which 3 were waited for; matrix products, arithmetic and copies ran while one was open for 18% of the time, Pallas kernels for 8%

profile of v7, /device:TPU:1, one launch (start us, length us, event | category | flops | bytes accessed | tf_op | source)
XLA Modules:
  0.0 155.1 jit_solution(797877111544133756)
XLA Ops:
  0.0 0.7 convert_reduce_fusion
  0.7 0.6 reduce-window.6
  1.6 0.7 select_reduce_fusion
  2.3 0.7 compare_select_fusion.1
  3.3 0.8 convert_element_type.48
  4.2 0.9 copy.130
  5.1 1.8 %scatter_custom_fusion.1 = bf16[1024,16]{1,0:T(8,128)(2,1)S(1)} fusion(s32[512]{0:T(512)S(1)} %bitcast.103, bf16[512,16]{1,0:T(8,128)(2,1)S(1)} %bitcast.99, bf16[]{:T(256)} %constant.15.clone.1), kind=kCustom, calls=%fused_computation.16 | custom fusion | bytes 32770 | tf_op jit(solution)/shard_map/scatter | solution.py:30
  7.0 1.8 %scatter_custom_fusion = bf16[1024,64]{1,0:T(8,128)(2,1)S(1)} fusion(s32[512]{0:T(512)S(1)} %bitcast.104, bf16[512,64]{1,0:T(8,128)(2,1)S(1)} %bitcast.100, bf16[]{:T(256)} %constant.11.clone.1), kind=kCustom, calls=%fused_computation.18 | custom fusion | bytes 131074 | tf_op jit(solution)/shard_map/scatter | solution.py:28
  9.0 0.3 all_to_all.35
  9.3 0.5 broadcast.101
  9.8 1.6 %reduce.7 = bf16[16,5120]{1,0:T(8,128)(2,1)S(1)} reduce(bf16[16,1,5120]{2,1,0:T(2,128)(2,1)S(1)} %all_to_all.35, bf16[]{:T(256)} %broadcast.101), dimensions={1}, to_apply=%all_to_all.35.reduce_sub_computation | reduce | bytes 327682 | tf_op jit(solution)/shard_map/all_to_all | solution.py:143
  11.4 0.8 reshape.241
  12.2 10.1 %all-to-all-start.1 = ((bf16[16,2,2560]{2,1,0:T(2,128)(2,1)}), bf16[16,2,2560]{2,1,0:T(2,128)(2,1)S(1)}, u32[]{:S(2)}, u32[]{:S(2)}) async-start(bf16[16,2,2560]{2,1,0:T(2,128)(2,1)} %reshape.241), calls=%async_computation.1 | async-start | bytes 327680 | tf_op jit(solution)/shard_map/all_to_all | solution.py:143
  22.3 0.7 convert_element_type.43
  23.0 0.4 copy.121
  23.4 0.7 reshape.181
  24.4 1.2 reduce.6
  25.6 1.4 reshape.239
  26.9 4.9 %all-to-all-done.1 = bf16[16,2,2560]{2,1,0:T(2,128)(2,1)S(1)} async-done(((bf16[16,2,2560]{2,1,0:T(2,128)(2,1)}), bf16[16,2,2560]{2,1,0:T(2,128)(2,1)S(1)}, u32[]{:S(2)}, u32[]{:S(2)}) %all-to-all-start.1) | async-done | bytes 163872 | tf_op jit(solution)/shard_map/all_to_all | solution.py:143
  31.8 6.8 %all-to-all-start = ((bf16[16,2,10752]{2,1,0:T(2,128)(2,1)}), bf16[16,2,10752]{2,1,0:T(2,128)(2,1)S(1)}, u32[]{:S(2)}, u32[]{:S(2)}) async-start(bf16[16,2,10752]{2,1,0:T(2,128)(2,1)} %reshape.239), calls=%async_computation | async-start | bytes 1376256 | tf_op jit(solution)/shard_map/all_to_all | solution.py:128
  38.7 0.9 reduce.4
  39.6 0.3 reshape.193
  40.1 11.2 %all-to-all-done = bf16[16,2,10752]{2,1,0:T(2,128)(2,1)S(1)} async-done(((bf16[16,2,10752]{2,1,0:T(2,128)(2,1)}), bf16[16,2,10752]{2,1,0:T(2,128)(2,1)S(1)}, u32[]{:S(2)}, u32[]{:S(2)}) %all-to-all-start) | async-done | bytes 688160 | tf_op jit(solution)/shard_map/all_to_all | solution.py:128
  51.4 1.6 %broadcast_in_dim.30 = bf16[16,64,1024]{2,1,0:T(8,128)(2,1)} broadcast(bf16[64,1024]{1,0:T(8,128)(2,1)S(1)} %copy.133), dimensions={1,2} | broadcast | bytes 2228224 | tf_op jit(solution)/shard_map/broadcast_in_dim | solution.py:103
  53.0 4.0 %all-to-all-start.2 = ((bf16[16,64,1024]{2,1,0:T(8,128)(2,1)}), bf16[16,64,1024]{2,1,0:T(8,128)(2,1)S(1)}, u32[]{:S(2)}, u32[]{:S(2)}) async-start(bf16[16,64,1024]{2,1,0:T(8,128)(2,1)} %broadcast_in_dim.30), calls=%async_computation.2 | async-start | bytes 4194304 | tf_op jit(solution)/shard_map/all_to_all | solution.py:104
  57.9 1.5 fusion.keep_ref
  59.4 4.2 %reshape.240 = bf16[16,1,21504]{2,1,0:T(2,128)(2,1)S(1)} reshape(bf16[16,2,10752]{2,1,0:T(2,128)(2,1)} %copy-done.1) | data formatting | bytes 1376256
  63.8 0.9 slice.51
  64.7 1.4 reshape.202
  66.1 1.1 copy.141
  67.2 2.6 %reshape.229.codes_ref = s32[16,4,768]{2,1,0:T(4,128)} reshape(s32[16,4,32,24]{3,2,1,0:T(8,128)} %copy.141) | data formatting | bytes 393216 | tf_op jit(solution)/shard_map/reshape | solution.py:133
  69.8 1.1 reshape.184.book_ref
  71.2 1.4 broadcast_in_dim.26
  72.6 2.6 %copy.126.base_ref = bf16[1024,768]{1,0:T(8,128)(2,1)} copy(bf16[1024,768]{0,1:T(8,128)(2,1)} %bitcast.81) | data formatting | bytes 3145728 | tf_op jit(solution)/shard_map/reshape | solution.py:137
  75.2 11.7 %shard_map.82 = bf16[16,64,768]{2,1,0:T(8,128)(2,1)} custom-call(s32[16,4,768]{2,1,0:T(4,128)} %reshape.229.codes_ref, bf16[64,16,256]{2,1,0:T(8,128)(2,1)} %reshape.184.book_ref, bf16[1024,768]{1,0:T(8,128)(2,1)} %copy.126.base_ref), custom_call_target="tpu_custom_call" | custom-call | tf_op jit(solution)/shard_map/pallas_call | solution.py:49
  86.9 1.8 %multiply_reduce_fusion = f32[768]{0:T(1024)S(1)} fusion(bf16[16,64,768]{2,1,0:T(8,128)(2,1)} %shard_map.82), kind=kLoop, calls=%fused_computation.3 | loop fusion | flops 2358528 | bytes 1575936 | tf_op jit(solution)/shard_map/reduce_sum | solution.py:160
  88.7 0.9 mul.71.half_ref
  89.6 1.4 copy-done
  91.0 7.8 %shard_map.83 = f32[16,18,1024]{2,1,0:T(8,128)} custom-call(bf16[1024,768]{1,0:T(8,128)(2,1)} %bitcast.79, bf16[1024,1024]{1,0:T(8,128)(2,1)} %bitcast.80, f32[768,1]{1,0:T(8,128)} %mul.71.half_ref, bf16[768,1024]{1,0:T(8,128)(2,1)} %fusion.keep_ref, bf16[768,256]{1,0:T(8,128)(2,1)} %bitcast.91), custom_call_target="tpu_custom_call" | custom-call | tf_op jit(solution)/shard_map/pallas_call | solution.py:86
  98.8 27.1 %all_to_all.42 = f32[16,18,1024]{2,1,0:T(8,128)S(1)} all-to-all(f32[16,18,1024]{2,1,0:T(8,128)} %shard_map.83), channel_id=1, replica_groups=mesh['cell'=16,'sub'=16] {'sub'}, dimensions={0} | all-to-all | bytes 2359296 | tf_op jit(solution)/shard_map/all_to_all | solution.py:170
  126.5 0.8 reshape.243
  127.3 6.3 %all-to-all-start.4 = ((f32[16,1,1152]{2,1,0:T(1,128)}), f32[16,1,1152]{2,1,0:T(1,128)S(1)}, u32[]{:S(2)}, u32[]{:S(2)}) async-start(f32[16,1,1152]{2,1,0:T(1,128)} %reshape.243), calls=%async_computation.4 | async-start | bytes 147456 | tf_op jit(solution)/shard_map/all_to_all | solution.py:176
  133.9 7.7 %all-to-all-done.4 = f32[16,1,1152]{2,1,0:T(1,128)S(1)} async-done(((f32[16,1,1152]{2,1,0:T(1,128)}), f32[16,1,1152]{2,1,0:T(1,128)S(1)}, u32[]{:S(2)}, u32[]{:S(2)}) %all-to-all-start.4) | async-done | bytes 73760 | tf_op jit(solution)/shard_map/all_to_all | solution.py:176
  141.6 0.5 broadcast.103
  142.1 0.8 reduce.8
  143.3 1.0 gather_fusion
  144.6 9.7 %all_to_all.43 = bf16[16,16,256]{2,1,0:T(8,128)(2,1)S(1)} all-to-all(bf16[16,16,256]{2,1,0:T(8,128)(2,1)S(1)} %broadcast_in_dim.32), channel_id=1, replica_groups=mesh['cell'=16,'sub'=16] {'sub'}, dimensions={0} | all-to-all | bytes 262144 | tf_op jit(solution)/shard_map/all_to_all | solution.py:104
  154.3 0.8 copy.140
  (72 shorter events, 4.4 us)
Async XLA Ops:
  5.1 17.2 %copy-start.3 = (s32[32,4,384]{2,1,0:T(4,128)S(1)}, s32[32,4,384]{2,1,0:T(4,128)}, u32[]{:S(2)}) copy-start(s32[32,4,384]{2,1,0:T(4,128)} %param.13) | copy-start | bytes 589828
  12.2 12.0 %copy-start.5 = (bf16[32,64]{1,0:T(8,128)(2,1)S(1)}, bf16[32,64]{1,0:T(8,128)(2,1)}, u32[]{:S(2)}) copy-start(bf16[32,64]{1,0:T(8,128)(2,1)} %param.11) | copy-start | bytes 12292
  12.2 12.1 %copy-start.4 = (bf16[4,16,256]{2,1,0:T(8,128)(2,1)S(1)}, bf16[4,16,256]{2,1,0:T(8,128)(2,1)}, u32[]{:S(2)}) copy-start(bf16[4,16,256]{2,1,0:T(8,128)(2,1)} %param.12) | copy-start | bytes 98308
  12.2 19.6 %all-to-all-start.1 = ((bf16[16,2,2560]{2,1,0:T(2,128)(2,1)}), bf16[16,2,2560]{2,1,0:T(2,128)(2,1)S(1)}, u32[]{:S(2)}, u32[]{:S(2)}) async-start(bf16[16,2,2560]{2,1,0:T(2,128)(2,1)} %reshape.241), calls=%async_computation.1 | async-start | bytes 327680 | tf_op jit(solution)/shard_map/all_to_all | solution.py:143
  31.8 19.6 %all-to-all-start = ((bf16[16,2,10752]{2,1,0:T(2,128)(2,1)}), bf16[16,2,10752]{2,1,0:T(2,128)(2,1)S(1)}, u32[]{:S(2)}, u32[]{:S(2)}) async-start(bf16[16,2,10752]{2,1,0:T(2,128)(2,1)} %reshape.239), calls=%async_computation | async-start | bytes 1376256 | tf_op jit(solution)/shard_map/all_to_all | solution.py:128
  51.4 1.6 %copy-start.1 = (bf16[16,2,10752]{2,1,0:T(2,128)(2,1)}, bf16[16,2,10752]{2,1,0:T(2,128)(2,1)S(1)}, u32[]{:S(2)}) copy-start(bf16[16,2,10752]{2,1,0:T(2,128)(2,1)S(1)} %all-to-all-done) | copy-start | bytes 2064388
  53.0 4.2 %copy-start.6 = (s32[32]{0:T(128)S(1)}, s32[32]{0:T(128)}, u32[]{:S(2)}) copy-start(s32[32]{0:T(128)} %param.14) | copy-start | bytes 388
  53.0 36.6 %all-to-all-start.2 = ((bf16[16,64,1024]{2,1,0:T(8,128)(2,1)}), bf16[16,64,1024]{2,1,0:T(8,128)(2,1)S(1)}, u32[]{:S(2)}, u32[]{:S(2)}) async-start(bf16[16,64,1024]{2,1,0:T(8,128)(2,1)} %broadcast_in_dim.30), calls=%async_computation.2 | async-start | bytes 4194304 | tf_op jit(solution)/shard_map/all_to_all | solution.py:104
  67.2 2.6 %copy-start.2 = (bf16[16,16384]{1,0:T(8,128)(2,1)S(1)}, bf16[16,16384]{1,0:T(8,128)(2,1)}, u32[]{:S(2)}) copy-start(bf16[16,16384]{1,0:T(8,128)(2,1)} %slice.51) | copy-start | bytes 1572868
  89.6 1.4 copy-start
  127.3 14.3 %all-to-all-start.4 = ((f32[16,1,1152]{2,1,0:T(1,128)}), f32[16,1,1152]{2,1,0:T(1,128)S(1)}, u32[]{:S(2)}, u32[]{:S(2)}) async-start(f32[16,1,1152]{2,1,0:T(1,128)} %reshape.243), calls=%async_computation.4 | async-start | bytes 147456 | tf_op jit(solution)/shard_map/all_to_all | solution.py:176

commit v8 on v7

--- a/solution.py
+++ b/solution.py
@@ -61,41 +61,37 @@
 
 def score_kernel(x_ref, q_ref, half_ref, keep_ref, table_ref, out_ref):
     chunk = out_ref.shape[1] - 2
-    raw = lax.dot_general(
-        x_ref[...], q_ref[...], (((0,), (0,)), ((), ())), preferred_element_type=jnp.float32
-    )
+    raw = jnp.dot(x_ref[...], q_ref[...], preferred_element_type=jnp.float32)
     values = (raw - half_ref[...]) * score_scale
     keep = keep_ref[...] > 0
     peak = jnp.max(jnp.where(keep, values, floor_score), axis=0, keepdims=True)
     weights = jnp.where(keep, jnp.exp(values - peak), 0.0).astype(jnp.bfloat16)
     mass = jnp.sum(weights.astype(jnp.float32), axis=0, keepdims=True)
-    part = lax.dot_general(
-        table_ref[...], weights, (((0,), (0,)), ((), ())), preferred_element_type=jnp.float32
-    )
+    part = jnp.dot(table_ref[...], weights, preferred_element_type=jnp.float32)
     for dest in range(out_ref.shape[0]):
         out_ref[dest, :chunk, :] = part[dest * chunk : (dest + 1) * chunk, :]
         out_ref[dest, chunk : chunk + 1, :] = mass
         out_ref[dest, chunk + 1 : chunk + 2, :] = peak
 
 
-def score_terms(decoded, queries_t, half_norm, keep_t, table, parts, block):
-    dims, rows = decoded.shape
+def score_terms(decoded_t, queries_t, half_norm, keep_t, table_t, parts, block):
+    rows, dims = decoded_t.shape
     total = queries_t.shape[1]
-    width = table.shape[1]
+    width = table_t.shape[0]
     chunk = width // parts
     return pl.pallas_call(
         score_kernel,
         grid=(total // block,),
         in_specs=[
-            pl.BlockSpec((dims, rows), lambda j: (0, 0)),
+            pl.BlockSpec((rows, dims), lambda j: (0, 0)),
             pl.BlockSpec((dims, block), lambda j: (0, j)),
             pl.BlockSpec((rows, 1), lambda j: (0, 0)),
             pl.BlockSpec((rows, block), lambda j: (0, j)),
-            pl.BlockSpec((rows, width), lambda j: (0, 0)),
+            pl.BlockSpec((width, rows), lambda j: (0, 0)),
         ],
         out_specs=pl.BlockSpec((parts, chunk + 2, block), lambda j: (0, 0, j)),
         out_shape=jax.ShapeDtypeStruct((parts, chunk + 2, total), jnp.float32),
-    )(decoded, queries_t, half_norm, keep_t, table)
+    )(decoded_t, queries_t, half_norm, keep_t, table_t)
 
 
 def gather_by_exchange(x, axis):
@@ -165,7 +161,7 @@
     table = payload.reshape(-1, pw)
     half_norm = (0.5 * sq_norm)[:, None]
     sendable = score_terms(
-        decoded, query_parts.reshape(-1, total), half_norm, keep_t, table, parts, 256
+        decoded.T, query_parts.reshape(-1, total), half_norm, keep_t, table.T, parts, 512
     )
     pieces = lax.all_to_all(sendable, "sub", split_axis=0, concat_axis=0, tiled=True)
     peaks_in = pieces[:, chunk + 1, :]

time: 157 us -> 148 us (0.943)
  local copies, waits for them, and re-layouts: 34.9 us -> 28.2 us
    unnamed x25 -> x23, local copies, waits for them, and re-layouts: 9.88 us -> 4.93 us
    reshape x1 -> x3, local copies, waits for them, and re-layouts: 0.01 us -> 3.64 us  [the longest x1 2.72 us: local(): decoded = decoded_parts.reshape(-1, decoded_parts.shape[2])]
    reshape x3, local copies, waits for them, and re-layouts: 5.1 us -> 2.84 us  [local(): got_codes = got_codes.reshape(parts, sub_count, cell_count * rows_part)]
  transfers between devices with their start and end apart: 4 -> 4, of which waited for: 3 -> 3; matrix products, arithmetic and copies ran while one was open for 18% -> 14% of each run, Pallas kernels for 8% -> 8%
where the time goes in v8:
time: 148 us; the launch traced here: 147 us
  blocking collectives  37.1 us (25%)
  local copies, waits for them, and re-layouts  28.2 us (19%)
  starting transfers between devices  27.7 us (19%)
  waiting for transfers between devices  23.8 us (16%)
  Pallas kernels  18.9 us (13%)
  other arithmetic  11.1 us (8%)
    all_to_all x1, blocking collectives, local(): lax.all_to_all(sendable, 'sub', split_axis=0, concat_axis=0, tiled=True)  27 us
    pallas_call x1, Pallas kernels, decode(): pl.pallas_call(decode_kernel, grid=(blocks,), in_specs=[pl.BlockSpec((1,...  11.7 us
    all_to_all x1, waiting for transfers between devices, local(): lax.all_to_all(tables, 'sub', split_axis=0, concat_axis=0, tiled=True)  11.2 us
    all_to_all x1, starting transfers between devices, local(): lax.all_to_all(jnp.concatenate([buffer, cell_marks], axis=1).reshape(grou...  10.1 us
    all_to_all x1, blocking collectives, gather_by_exchange(): return lax.all_to_all(copies, axis, split_axis=0, concat_axis=0, tiled=True)  10.1 us
    all_to_all x1, waiting for transfers between devices, local(): lax.all_to_all(outgoing.reshape(chunk + 2, groups, capacity), 'cell', spl...  7.68 us
    pallas_call x1, Pallas kernels, score_terms(): pl.pallas_call(score_kernel, grid=(total // block,), in_specs=[pl.BlockSp...  7.22 us
    all_to_all x1, starting transfers between devices, local(): lax.all_to_all(tables, 'sub', split_axis=0, concat_axis=0, tiled=True)  6.76 us
  transfers between devices with their start and end apart: 4, of which 3 were waited for; matrix products, arithmetic and copies ran while one was open for 14% of the time, Pallas kernels for 8%

profile of v8, /device:TPU:1, one launch (start us, length us, event | category | flops | bytes accessed | tf_op | source)
XLA Modules:
  0.0 147.2 jit_solution(2666978374602928146)
XLA Ops:
  0.0 0.7 convert_reduce_fusion
  0.7 0.6 reduce-window.6
  1.6 0.7 select_reduce_fusion
  2.3 0.7 compare_select_fusion.1
  3.3 0.8 convert_element_type.48
  4.2 0.9 copy.143
  5.1 1.8 %scatter_custom_fusion.1 = bf16[1024,16]{1,0:T(8,128)(2,1)S(1)} fusion(s32[512]{0:T(512)S(1)} %bitcast.106, bf16[512,16]{1,0:T(8,128)(2,1)S(1)} %bitcast.102, bf16[]{:T(256)} %constant.15.clone.1), kind=kCustom, calls=%fused_computation.16 | custom fusion | bytes 32770 | tf_op jit(solution)/shard_map/scatter | solution.py:30
  7.0 1.8 %scatter_custom_fusion = bf16[1024,64]{1,0:T(8,128)(2,1)S(1)} fusion(s32[512]{0:T(512)S(1)} %bitcast.107, bf16[512,64]{1,0:T(8,128)(2,1)S(1)} %bitcast.103, bf16[]{:T(256)} %constant.11.clone.1), kind=kCustom, calls=%fused_computation.18 | custom fusion | bytes 131074 | tf_op jit(solution)/shard_map/scatter | solution.py:28
  9.0 0.3 all_to_all.35
  9.3 0.5 broadcast.101
  9.8 1.6 %reduce.7 = bf16[16,5120]{1,0:T(8,128)(2,1)S(1)} reduce(bf16[16,1,5120]{2,1,0:T(2,128)(2,1)S(1)} %all_to_all.35, bf16[]{:T(256)} %broadcast.101), dimensions={1}, to_apply=%all_to_all.35.reduce_sub_computation | reduce | bytes 327682 | tf_op jit(solution)/shard_map/all_to_all | solution.py:139
  11.4 0.8 reshape.241
  12.2 10.1 %all-to-all-start.1 = ((bf16[16,2,2560]{2,1,0:T(2,128)(2,1)}), bf16[16,2,2560]{2,1,0:T(2,128)(2,1)S(1)}, u32[]{:S(2)}, u32[]{:S(2)}) async-start(bf16[16,2,2560]{2,1,0:T(2,128)(2,1)} %reshape.241), calls=%async_computation.1 | async-start | bytes 327680 | tf_op jit(solution)/shard_map/all_to_all | solution.py:139
  22.3 0.7 convert_element_type.43
  23.0 0.4 copy.133
  23.4 0.7 reshape.181
  24.4 1.2 reduce.6
  25.6 1.4 reshape.239
  26.9 4.9 %all-to-all-done.1 = bf16[16,2,2560]{2,1,0:T(2,128)(2,1)S(1)} async-done(((bf16[16,2,2560]{2,1,0:T(2,128)(2,1)}), bf16[16,2,2560]{2,1,0:T(2,128)(2,1)S(1)}, u32[]{:S(2)}, u32[]{:S(2)}) %all-to-all-start.1) | async-done | bytes 163872 | tf_op jit(solution)/shard_map/all_to_all | solution.py:139
  31.8 6.8 %all-to-all-start = ((bf16[16,2,10752]{2,1,0:T(2,128)(2,1)}), bf16[16,2,10752]{2,1,0:T(2,128)(2,1)S(1)}, u32[]{:S(2)}, u32[]{:S(2)}) async-start(bf16[16,2,10752]{2,1,0:T(2,128)(2,1)} %reshape.239), calls=%async_computation | async-start | bytes 1376256 | tf_op jit(solution)/shard_map/all_to_all | solution.py:124
  38.7 0.9 reduce.4
  39.6 0.3 reshape.193
  40.1 11.2 %all-to-all-done = bf16[16,2,10752]{2,1,0:T(2,128)(2,1)S(1)} async-done(((bf16[16,2,10752]{2,1,0:T(2,128)(2,1)}), bf16[16,2,10752]{2,1,0:T(2,128)(2,1)S(1)}, u32[]{:S(2)}, u32[]{:S(2)}) %all-to-all-start) | async-done | bytes 688160 | tf_op jit(solution)/shard_map/all_to_all | solution.py:124
  51.4 1.6 %broadcast_in_dim.30 = bf16[16,64,1024]{2,1,0:T(8,128)(2,1)} broadcast(bf16[64,1024]{1,0:T(8,128)(2,1)S(1)} %copy.146), dimensions={1,2} | broadcast | bytes 2228224 | tf_op jit(solution)/shard_map/broadcast_in_dim | solution.py:99
  52.9 4.7 %all-to-all-start.2 = ((bf16[16,64,1024]{2,1,0:T(8,128)(2,1)}), bf16[16,64,1024]{2,1,0:T(8,128)(2,1)}, u32[]{:S(2)}, u32[]{:S(2)}) async-start(bf16[16,64,1024]{2,1,0:T(8,128)(2,1)} %broadcast_in_dim.30), calls=%async_computation.2 | async-start | bytes 4194304 | tf_op jit(solution)/shard_map/all_to_all | solution.py:100
  58.0 0.9 copy.148
  59.2 0.3 fusion.1
  59.4 1.5 %fusion.keep_ref = bf16[768,1024]{1,0:T(8,128)(2,1)} fusion(pred[768]{0:T(1024)(128)(4,1)S(1)} %lt.43, pred[32,1024]{1,0:T(8,128)(4,1)S(1)} %bitcast.101), kind=kLoop, calls=%fused_computation.5 | loop fusion | flops 1572864 | bytes 1606400 | tf_op jit(solution)/shard_map/convert_element_type | solution.py:160
  61.0 0.6 reshape.240
  61.9 1.4 reshape.202
  63.4 1.3 reshape.229.codes_ref
  64.7 1.1 reshape.184.book_ref
  66.4 1.6 %copy.138.base_ref = bf16[1024,768]{1,0:T(8,128)(2,1)} copy(bf16[1024,768]{0,1:T(8,128)(2,1)S(1)} %bitcast.82) | data formatting | bytes 3145728 | tf_op jit(solution)/shard_map/reshape | solution.py:133
  68.0 11.7 %shard_map.82 = bf16[16,64,768]{2,1,0:T(8,128)(2,1)} custom-call(s32[16,4,768]{2,1,0:T(4,128)} %reshape.229.codes_ref, bf16[64,16,256]{2,1,0:T(8,128)(2,1)} %reshape.184.book_ref, bf16[1024,768]{1,0:T(8,128)(2,1)} %copy.138.base_ref), custom_call_target="tpu_custom_call" | custom-call | tf_op jit(solution)/shard_map/pallas_call | solution.py:49
  79.7 2.7 %copy.139 = bf16[1024,768]{0,1:T(8,128)(2,1)} copy(bf16[1024,768]{1,0:T(8,128)(2,1)} %bitcast.81) | data formatting | bytes 3145728 | tf_op jit(solution)/shard_map/reshape | solution.py:149
  82.4 0.4 multiply_reduce_fusion
  82.8 0.9 mul.71.half_ref
  83.7 7.2 %shard_map.83 = f32[16,18,1024]{2,1,0:T(8,128)} custom-call(bf16[768,1024]{1,0:T(8,128)(2,1)} %bitcast.83, bf16[1024,1024]{1,0:T(8,128)(2,1)} %bitcast.14.q_ref, f32[768,1]{1,0:T(8,128)} %mul.71.half_ref, bf16[768,1024]{1,0:T(8,128)(2,1)} %fusion.keep_ref, bf16[256,768]{1,0:T(8,128)(2,1)} %bitcast.89), custom_call_target="tpu_custom_call" | custom-call | tf_op jit(solution)/shard_map/pallas_call | solution.py:82
  90.9 27.0 %all_to_all.42 = f32[16,18,1024]{2,1,0:T(8,128)S(1)} all-to-all(f32[16,18,1024]{2,1,0:T(8,128)} %shard_map.83), channel_id=1, replica_groups=mesh['cell'=16,'sub'=16] {'sub'}, dimensions={0} | all-to-all | bytes 2359296 | tf_op jit(solution)/shard_map/all_to_all | solution.py:166
  118.6 0.8 reshape.243
  119.3 6.1 %all-to-all-start.4 = ((f32[16,1,1152]{2,1,0:T(1,128)}), f32[16,1,1152]{2,1,0:T(1,128)S(1)}, u32[]{:S(2)}, u32[]{:S(2)}) async-start(f32[16,1,1152]{2,1,0:T(1,128)} %reshape.243), calls=%async_computation.4 | async-start | bytes 147456 | tf_op jit(solution)/shard_map/all_to_all | solution.py:172
  125.7 7.7 %all-to-all-done.4 = f32[16,1,1152]{2,1,0:T(1,128)S(1)} async-done(((f32[16,1,1152]{2,1,0:T(1,128)}), f32[16,1,1152]{2,1,0:T(1,128)S(1)}, u32[]{:S(2)}, u32[]{:S(2)}) %all-to-all-start.4) | async-done | bytes 73760 | tf_op jit(solution)/shard_map/all_to_all | solution.py:172
  133.4 0.5 broadcast.103
  133.9 0.8 reduce.8
  134.8 0.2 copy.151
  135.1 1.0 gather_fusion
  136.4 10.1 %all_to_all.43 = bf16[16,16,256]{2,1,0:T(8,128)(2,1)S(1)} all-to-all(bf16[16,16,256]{2,1,0:T(8,128)(2,1)S(1)} %broadcast_in_dim.32), channel_id=1, replica_groups=mesh['cell'=16,'sub'=16] {'sub'}, dimensions={0} | all-to-all | bytes 262144 | tf_op jit(solution)/shard_map/all_to_all | solution.py:100
  146.5 0.8 copy.154
  (72 shorter events, 4.2 us)
Async XLA Ops:
  5.1 17.2 %copy-start.2 = (s32[32,4,384]{2,1,0:T(4,128)S(1)}, s32[32,4,384]{2,1,0:T(4,128)}, u32[]{:S(2)}) copy-start(s32[32,4,384]{2,1,0:T(4,128)} %param.13) | copy-start | bytes 589828
  12.2 12.0 %copy-start.4 = (bf16[32,64]{1,0:T(8,128)(2,1)S(1)}, bf16[32,64]{1,0:T(8,128)(2,1)}, u32[]{:S(2)}) copy-start(bf16[32,64]{1,0:T(8,128)(2,1)} %param.11) | copy-start | bytes 12292
  12.2 12.1 %copy-start.3 = (bf16[4,16,256]{2,1,0:T(8,128)(2,1)S(1)}, bf16[4,16,256]{2,1,0:T(8,128)(2,1)}, u32[]{:S(2)}) copy-start(bf16[4,16,256]{2,1,0:T(8,128)(2,1)} %param.12) | copy-start | bytes 98308
  12.2 19.6 %all-to-all-start.1 = ((bf16[16,2,2560]{2,1,0:T(2,128)(2,1)}), bf16[16,2,2560]{2,1,0:T(2,128)(2,1)S(1)}, u32[]{:S(2)}, u32[]{:S(2)}) async-start(bf16[16,2,2560]{2,1,0:T(2,128)(2,1)} %reshape.241), calls=%async_computation.1 | async-start | bytes 327680 | tf_op jit(solution)/shard_map/all_to_all | solution.py:139
  31.8 19.6 %all-to-all-start = ((bf16[16,2,10752]{2,1,0:T(2,128)(2,1)}), bf16[16,2,10752]{2,1,0:T(2,128)(2,1)S(1)}, u32[]{:S(2)}, u32[]{:S(2)}) async-start(bf16[16,2,10752]{2,1,0:T(2,128)(2,1)} %reshape.239), calls=%async_computation | async-start | bytes 1376256 | tf_op jit(solution)/shard_map/all_to_all | solution.py:124
  52.9 4.9 %copy-start.5 = (s32[32]{0:T(128)S(1)}, s32[32]{0:T(128)}, u32[]{:S(2)}) copy-start(s32[32]{0:T(128)} %param.14) | copy-start | bytes 388
  52.9 5.0 %copy-start.1 = (bf16[32,24,256]{2,1,0:T(8,128)(2,1)S(1)}, bf16[32,24,256]{2,1,0:T(8,128)(2,1)}, u32[]{:S(2)}) copy-start(bf16[32,24,256]{2,1,0:T(8,128)(2,1)} %param.15) | copy-start | bytes 1179652
  52.9 30.8 %all-to-all-start.2 = ((bf16[16,64,1024]{2,1,0:T(8,128)(2,1)}), bf16[16,64,1024]{2,1,0:T(8,128)(2,1)}, u32[]{:S(2)}, u32[]{:S(2)}) async-start(bf16[16,64,1024]{2,1,0:T(8,128)(2,1)} %broadcast_in_dim.30), calls=%async_computation.2 | async-start | bytes 4194304 | tf_op jit(solution)/shard_map/all_to_all | solution.py:100
  79.7 2.7 %copy-start = (bf16[16,64,768]{2,1,0:T(8,128)(2,1)S(1)}, bf16[16,64,768]{2,1,0:T(8,128)(2,1)}, u32[]{:S(2)}) copy-start(bf16[16,64,768]{2,1,0:T(8,128)(2,1)} %shard_map.82) | copy-start | bytes 4718596
  119.3 14.1 %all-to-all-start.4 = ((f32[16,1,1152]{2,1,0:T(1,128)}), f32[16,1,1152]{2,1,0:T(1,128)S(1)}, u32[]{:S(2)}, u32[]{:S(2)}) async-start(f32[16,1,1152]{2,1,0:T(1,128)} %reshape.243), calls=%async_computation.4 | async-start | bytes 147456 | tf_op jit(solution)/shard_map/all_to_all | solution.py:172

commit v9 on v8

--- a/solution.py
+++ b/solution.py
@@ -112,17 +112,18 @@
     cell_count, sub_count, row_count = codes.shape
     rows_part = row_count // parts
     own_codes = codes.reshape(cell_count, sub_count, parts, rows_part)
-    own_codes = jnp.transpose(own_codes, (2, 0, 1, 3)).astype(jnp.bfloat16).reshape(parts, -1)
+    own_codes = jnp.transpose(own_codes, (2, 0, 1, 3)).astype(jnp.bfloat16).reshape(parts, -1, 128)
     tables = jnp.concatenate(
         [
             own_codes,
-            jnp.broadcast_to(codebooks.reshape(1, -1), (parts, codebooks.size)),
-            jnp.broadcast_to(coarse.reshape(1, -1), (parts, coarse.size)),
+            jnp.broadcast_to(codebooks.reshape(1, -1, 128), (parts, codebooks.size // 128, 128)),
+            jnp.broadcast_to(coarse.reshape(1, -1, 128), (parts, coarse.size // 128, 128)),
         ],
         axis=1,
     )
     tables = lax.all_to_all(tables, "sub", split_axis=0, concat_axis=0, tiled=True)
-    code_size = own_codes.shape[1]
+    tables = tables.reshape(parts, -1)
+    code_size = own_codes.shape[1] * own_codes.shape[2]
     book_size = codebooks.size
     got_codes = tables[:, :code_size].reshape(parts, cell_count, sub_count, rows_part)
     got_codes = jnp.transpose(got_codes, (0, 2, 1, 3)).astype(jnp.int32)
@@ -181,8 +182,10 @@
     scale = jnp.exp(peaks - top)
     upper = jnp.sum(scale[None, :, :] * parts_back, axis=2)
     lower = jnp.sum(scale * masses, axis=1)
-    pooled = (upper / lower[None, :]).astype(jnp.bfloat16)
-    return gather_by_exchange(pooled, "sub").reshape(pw, -1).T
+    pooled = (upper / lower[None, :]).T.astype(jnp.bfloat16)
+    copies = jnp.broadcast_to(pooled[None], (parts,) + pooled.shape)
+    gathered = lax.all_to_all(copies, "sub", split_axis=0, concat_axis=2, tiled=True)
+    return gathered.reshape(pooled.shape[0], pw)
 
 
 def solution(mesh):

time: 148 us -> 147 us (level)
  blocking collectives: 37.1 us -> 34.6 us
  local copies, waits for them, and re-layouts: 28.2 us -> 26.2 us
  waiting for transfers between devices: 23.8 us -> 25.8 us
  starting transfers between devices: 27.7 us -> 29.5 us
    all_to_all x1, blocking collectives: 27 us -> 24.9 us  [local(): lax.all_to_all(sendable, 'sub', split_axis=0, concat_axis=0, tiled=True)]
    unnamed x23 -> x20, local copies, waits for them, and re-layouts: 4.93 us -> 2.86 us
    all_to_all x1, starting transfers between devices: 6.09 us -> 8.03 us  [local(): lax.all_to_all(outgoing.reshape(chunk + 2, groups, capacity), 'cell', spl...]
    all_to_all x1, waiting for transfers between devices: 4.87 us -> 6.56 us  [local(): lax.all_to_all(jnp.concatenate([buffer, cell_marks], axis=1).reshape(grou...]
  transfers between devices with their start and end apart: 4 -> 4, of which waited for: 3 -> 4; matrix products, arithmetic and copies ran while one was open for 14% -> 12% of each run, Pallas kernels for 8% -> 8%
where the time goes in v9:
time: 147 us; the launch traced here: 146 us
  blocking collectives  34.6 us (24%)
  starting transfers between devices  29.5 us (20%)
  local copies, waits for them, and re-layouts  26.2 us (18%)
  waiting for transfers between devices  25.8 us (18%)
  Pallas kernels  18.9 us (13%)
  other arithmetic  10.7 us (7%)
    all_to_all x1, blocking collectives, local(): lax.all_to_all(sendable, 'sub', split_axis=0, concat_axis=0, tiled=True)  24.9 us
    pallas_call x1, Pallas kernels, decode(): pl.pallas_call(decode_kernel, grid=(blocks,), in_specs=[pl.BlockSpec((1,...  11.7 us
    all_to_all x1, waiting for transfers between devices, local(): lax.all_to_all(tables, 'sub', split_axis=0, concat_axis=0, tiled=True)  11.2 us
    all_to_all x1, starting transfers between devices, local(): lax.all_to_all(jnp.concatenate([buffer, cell_marks], axis=1).reshape(grou...  9.97 us
    all_to_all x1, blocking collectives, local(): lax.all_to_all(copies, 'sub', split_axis=0, concat_axis=2, tiled=True)  9.72 us
    all_to_all x1, starting transfers between devices, local(): lax.all_to_all(outgoing.reshape(chunk + 2, groups, capacity), 'cell', spl...  8.03 us
    all_to_all x1, waiting for transfers between devices, local(): lax.all_to_all(outgoing.reshape(chunk + 2, groups, capacity), 'cell', spl...  7.68 us
    pallas_call x1, Pallas kernels, score_terms(): pl.pallas_call(score_kernel, grid=(total // block,), in_specs=[pl.BlockSp...  7.24 us
  transfers between devices with their start and end apart: 4, of which 4 were waited for; matrix products, arithmetic and copies ran while one was open for 12% of the time, Pallas kernels for 8%

profile of v9, /device:TPU:1, one launch (start us, length us, event | category | flops | bytes accessed | tf_op | source)
XLA Modules:
  0.0 146.3 jit_solution(6479211115804174492)
XLA Ops:
  0.0 0.7 convert_reduce_fusion
  0.7 0.6 reduce-window.6
  1.6 0.7 select_reduce_fusion
  2.3 0.7 compare_select_fusion.1
  3.3 0.8 convert_element_type.47
  4.2 0.9 copy.93
  5.1 1.8 %scatter_custom_fusion.1 = bf16[1024,16]{1,0:T(8,128)(2,1)S(1)} fusion(s32[512]{0:T(512)S(1)} %bitcast.104, bf16[512,16]{1,0:T(8,128)(2,1)S(1)} %bitcast.102, bf16[]{:T(256)} %constant.15.clone.1), kind=kCustom, calls=%fused_computation.15 | custom fusion | bytes 32770 | tf_op jit(solution)/shard_map/scatter | solution.py:30
  7.0 1.8 %scatter_custom_fusion = bf16[1024,64]{1,0:T(8,128)(2,1)S(1)} fusion(s32[512]{0:T(512)S(1)} %bitcast.105, bf16[512,64]{1,0:T(8,128)(2,1)S(1)} %bitcast.103, bf16[]{:T(256)} %constant.11.clone.1), kind=kCustom, calls=%fused_computation.17 | custom fusion | bytes 131074 | tf_op jit(solution)/shard_map/scatter | solution.py:28
  9.0 0.3 all_to_all.38
  9.3 0.5 broadcast.89
  9.8 1.6 %reduce.6 = bf16[16,5120]{1,0:T(8,128)(2,1)S(1)} reduce(bf16[16,1,5120]{2,1,0:T(2,128)(2,1)S(1)} %all_to_all.38, bf16[]{:T(256)} %broadcast.89), dimensions={1}, to_apply=%all_to_all.38.reduce_sub_computation | reduce | bytes 327682 | tf_op jit(solution)/shard_map/all_to_all | solution.py:140
  11.4 0.8 reshape.223
  12.2 10.0 %all-to-all-start.1 = ((bf16[16,2,2560]{2,1,0:T(2,128)(2,1)}), bf16[16,2,2560]{2,1,0:T(2,128)(2,1)S(1)}, u32[]{:S(2)}, u32[]{:S(2)}) async-start(bf16[16,2,2560]{2,1,0:T(2,128)(2,1)} %reshape.223), calls=%async_computation.1 | async-start | bytes 327680 | tf_op jit(solution)/shard_map/all_to_all | solution.py:140
  22.4 0.7 convert_element_type.42
  23.0 0.4 copy.84
  23.5 0.7 reshape.166
  24.2 0.9 pad_maximum_fusion
  25.1 6.6 %all-to-all-done.1 = bf16[16,2,2560]{2,1,0:T(2,128)(2,1)S(1)} async-done(((bf16[16,2,2560]{2,1,0:T(2,128)(2,1)}), bf16[16,2,2560]{2,1,0:T(2,128)(2,1)S(1)}, u32[]{:S(2)}, u32[]{:S(2)}) %all-to-all-start.1) | async-done | bytes 163872 | tf_op jit(solution)/shard_map/all_to_all | solution.py:140
  31.7 6.8 %all-to-all-start = ((bf16[16,168,128]{2,1,0:T(8,128)(2,1)}), bf16[16,168,128]{2,1,0:T(8,128)(2,1)S(1)}, u32[]{:S(2)}, u32[]{:S(2)}) async-start(bf16[16,168,128]{2,1,0:T(8,128)(2,1)} %pad_maximum_fusion), calls=%async_computation | async-start | bytes 1376256 | tf_op jit(solution)/shard_map/all_to_all | solution.py:124
  38.6 0.9 reduce.4
  39.5 0.3 reshape.179
  40.0 11.2 %all-to-all-done = bf16[16,168,128]{2,1,0:T(8,128)(2,1)S(1)} async-done(((bf16[16,168,128]{2,1,0:T(8,128)(2,1)}), bf16[16,168,128]{2,1,0:T(8,128)(2,1)S(1)}, u32[]{:S(2)}, u32[]{:S(2)}) %all-to-all-start) | async-done | bytes 688160 | tf_op jit(solution)/shard_map/all_to_all | solution.py:124
  51.3 1.6 %broadcast_in_dim.30 = bf16[16,64,1024]{2,1,0:T(8,128)(2,1)} broadcast(bf16[64,1024]{1,0:T(8,128)(2,1)S(1)} %copy.96), dimensions={1,2} | broadcast | bytes 2228224 | tf_op jit(solution)/shard_map/broadcast_in_dim | solution.py:99
  52.8 4.7 %all-to-all-start.2 = ((bf16[16,64,1024]{2,1,0:T(8,128)(2,1)}), bf16[16,64,1024]{2,1,0:T(8,128)(2,1)}, u32[]{:S(2)}, u32[]{:S(2)}) async-start(bf16[16,64,1024]{2,1,0:T(8,128)(2,1)} %broadcast_in_dim.30), calls=%async_computation.2 | async-start | bytes 4194304 | tf_op jit(solution)/shard_map/all_to_all | solution.py:100
  57.9 0.9 copy.98
  59.0 0.3 fusion.1
  59.3 1.5 %fusion.keep_ref = bf16[768,1024]{1,0:T(8,128)(2,1)} fusion(pred[768]{0:T(1024)(128)(4,1)S(1)} %lt.43, pred[32,1024]{1,0:T(8,128)(4,1)S(1)} %bitcast.101), kind=kLoop, calls=%fused_computation.5 | loop fusion | flops 1572864 | bytes 1606400 | tf_op jit(solution)/shard_map/convert_element_type | solution.py:161
  61.0 1.4 reshape.188
  62.6 1.3 reshape.215.codes_ref
  63.9 1.1 reshape.170.book_ref
  65.6 1.6 %copy.88.base_ref = bf16[1024,768]{1,0:T(8,128)(2,1)} copy(bf16[1024,768]{0,1:T(8,128)(2,1)S(1)} %bitcast.81) | data formatting | bytes 3145728 | tf_op jit(solution)/shard_map/reshape | solution.py:134
  67.2 11.7 %shard_map.82 = bf16[16,64,768]{2,1,0:T(8,128)(2,1)} custom-call(s32[16,4,768]{2,1,0:T(4,128)} %reshape.215.codes_ref, bf16[64,16,256]{2,1,0:T(8,128)(2,1)} %reshape.170.book_ref, bf16[1024,768]{1,0:T(8,128)(2,1)} %copy.88.base_ref), custom_call_target="tpu_custom_call" | custom-call | tf_op jit(solution)/shard_map/pallas_call | solution.py:49
  78.9 2.7 %copy.89 = bf16[1024,768]{0,1:T(8,128)(2,1)} copy(bf16[1024,768]{1,0:T(8,128)(2,1)} %bitcast.80) | data formatting | bytes 3145728 | tf_op jit(solution)/shard_map/reshape | solution.py:150
  81.6 0.4 multiply_reduce_fusion
  82.0 0.9 mul.71.half_ref
  82.9 0.4 all-to-all-done.2
  83.2 7.2 %shard_map.83 = f32[16,18,1024]{2,1,0:T(8,128)} custom-call(bf16[768,1024]{1,0:T(8,128)(2,1)} %bitcast.82, bf16[1024,1024]{1,0:T(8,128)(2,1)} %bitcast.13.q_ref, f32[768,1]{1,0:T(8,128)} %mul.71.half_ref, bf16[768,1024]{1,0:T(8,128)(2,1)} %fusion.keep_ref, bf16[256,768]{1,0:T(8,128)(2,1)} %bitcast.89), custom_call_target="tpu_custom_call" | custom-call | tf_op jit(solution)/shard_map/pallas_call | solution.py:82
  90.5 24.9 %all_to_all.45 = f32[16,18,1024]{2,1,0:T(8,128)S(1)} all-to-all(f32[16,18,1024]{2,1,0:T(8,128)} %shard_map.83), channel_id=1, replica_groups=mesh['cell'=16,'sub'=16] {'sub'}, dimensions={0} | all-to-all | bytes 2359296 | tf_op jit(solution)/shard_map/all_to_all | solution.py:167
  115.7 0.2 fusion.2
  116.0 0.8 reshape.225
  116.8 8.0 %all-to-all-start.4 = ((f32[16,1,1152]{2,1,0:T(1,128)}), f32[16,1,1152]{2,1,0:T(1,128)S(1)}, u32[]{:S(2)}, u32[]{:S(2)}) async-start(f32[16,1,1152]{2,1,0:T(1,128)} %reshape.225), calls=%async_computation.4 | async-start | bytes 147456 | tf_op jit(solution)/shard_map/all_to_all | solution.py:173
  125.1 7.7 %all-to-all-done.4 = f32[16,1,1152]{2,1,0:T(1,128)S(1)} async-done(((f32[16,1,1152]{2,1,0:T(1,128)}), f32[16,1,1152]{2,1,0:T(1,128)S(1)}, u32[]{:S(2)}, u32[]{:S(2)}) %all-to-all-start.4) | async-done | bytes 73760 | tf_op jit(solution)/shard_map/all_to_all | solution.py:173
  132.8 0.5 broadcast.90
  133.3 0.8 reduce.7
  134.2 0.2 copy.101
  134.5 1.0 gather_fusion
  135.8 9.7 %all_to_all.46 = bf16[16,256,16]{1,2,0:T(8,128)(2,1)S(1)} all-to-all(bf16[16,256,16]{1,2,0:T(8,128)(2,1)S(1)} %broadcast_in_dim.32), channel_id=1, replica_groups=mesh['cell'=16,'sub'=16] {'sub'}, dimensions={0} | all-to-all | bytes 262144 | tf_op jit(solution)/shard_map/all_to_all | solution.py:187
  145.5 0.8 copy.104
  (69 shorter events, 3.9 us)
Async XLA Ops:
  5.1 17.1 %copy-start.4 = (bf16[32,64]{1,0:T(8,128)(2,1)S(1)}, bf16[32,64]{1,0:T(8,128)(2,1)}, u32[]{:S(2)}) copy-start(bf16[32,64]{1,0:T(8,128)(2,1)} %param.11) | copy-start | bytes 12292
  5.1 17.2 %copy-start.3 = (bf16[4,16,256]{2,1,0:T(8,128)(2,1)S(1)}, bf16[4,16,256]{2,1,0:T(8,128)(2,1)}, u32[]{:S(2)}) copy-start(bf16[4,16,256]{2,1,0:T(8,128)(2,1)} %param.12) | copy-start | bytes 98308
  6.9 15.4 %copy-start.2 = (s32[32,4,384]{2,1,0:T(4,128)S(1)}, s32[32,4,384]{2,1,0:T(4,128)}, u32[]{:S(2)}) copy-start(s32[32,4,384]{2,1,0:T(4,128)} %param.13) | copy-start | bytes 589828
  12.2 19.5 %all-to-all-start.1 = ((bf16[16,2,2560]{2,1,0:T(2,128)(2,1)}), bf16[16,2,2560]{2,1,0:T(2,128)(2,1)S(1)}, u32[]{:S(2)}, u32[]{:S(2)}) async-start(bf16[16,2,2560]{2,1,0:T(2,128)(2,1)} %reshape.223), calls=%async_computation.1 | async-start | bytes 327680 | tf_op jit(solution)/shard_map/all_to_all | solution.py:140
  31.7 19.6 %all-to-all-start = ((bf16[16,168,128]{2,1,0:T(8,128)(2,1)}), bf16[16,168,128]{2,1,0:T(8,128)(2,1)S(1)}, u32[]{:S(2)}, u32[]{:S(2)}) async-start(bf16[16,168,128]{2,1,0:T(8,128)(2,1)} %pad_maximum_fusion), calls=%async_computation | async-start | bytes 1376256 | tf_op jit(solution)/shard_map/all_to_all | solution.py:124
  52.8 4.9 %copy-start.5 = (s32[32]{0:T(128)S(1)}, s32[32]{0:T(128)}, u32[]{:S(2)}) copy-start(s32[32]{0:T(128)} %param.14) | copy-start | bytes 388
  52.8 5.0 %copy-start.1 = (bf16[32,24,256]{2,1,0:T(8,128)(2,1)S(1)}, bf16[32,24,256]{2,1,0:T(8,128)(2,1)}, u32[]{:S(2)}) copy-start(bf16[32,24,256]{2,1,0:T(8,128)(2,1)} %param.15) | copy-start | bytes 1179652
  52.8 30.4 %all-to-all-start.2 = ((bf16[16,64,1024]{2,1,0:T(8,128)(2,1)}), bf16[16,64,1024]{2,1,0:T(8,128)(2,1)}, u32[]{:S(2)}, u32[]{:S(2)}) async-start(bf16[16,64,1024]{2,1,0:T(8,128)(2,1)} %broadcast_in_dim.30), calls=%async_computation.2 | async-start | bytes 4194304 | tf_op jit(solution)/shard_map/all_to_all | solution.py:100
  78.9 2.7 %copy-start = (bf16[16,64,768]{2,1,0:T(8,128)(2,1)S(1)}, bf16[16,64,768]{2,1,0:T(8,128)(2,1)}, u32[]{:S(2)}) copy-start(bf16[16,64,768]{2,1,0:T(8,128)(2,1)} %shard_map.82) | copy-start | bytes 4718596
  116.8 16.0 %all-to-all-start.4 = ((f32[16,1,1152]{2,1,0:T(1,128)}), f32[16,1,1152]{2,1,0:T(1,128)S(1)}, u32[]{:S(2)}, u32[]{:S(2)}) async-start(f32[16,1,1152]{2,1,0:T(1,128)} %reshape.225), calls=%async_computation.4 | async-start | bytes 147456 | tf_op jit(solution)/shard_map/all_to_all | solution.py:173

commit v10 on v9

--- a/solution.py
+++ b/solution.py
@@ -66,8 +66,9 @@
     keep = keep_ref[...] > 0
     peak = jnp.max(jnp.where(keep, values, floor_score), axis=0, keepdims=True)
     weights = jnp.where(keep, jnp.exp(values - peak), 0.0).astype(jnp.bfloat16)
-    mass = jnp.sum(weights.astype(jnp.float32), axis=0, keepdims=True)
     part = jnp.dot(table_ref[...], weights, preferred_element_type=jnp.float32)
+    width = out_ref.shape[0] * chunk
+    mass = part[width : width + 1, :]
     for dest in range(out_ref.shape[0]):
         out_ref[dest, :chunk, :] = part[dest * chunk : (dest + 1) * chunk, :]
         out_ref[dest, chunk : chunk + 1, :] = mass
@@ -79,6 +80,8 @@
     total = queries_t.shape[1]
     width = table_t.shape[0]
     chunk = width // parts
+    extra = jnp.zeros((16, rows), table_t.dtype).at[0].set(1)
+    table_t = jnp.concatenate([table_t, extra], axis=0)
     return pl.pallas_call(
         score_kernel,
         grid=(total // block,),
@@ -87,7 +90,7 @@
             pl.BlockSpec((dims, block), lambda j: (0, j)),
             pl.BlockSpec((rows, 1), lambda j: (0, 0)),
             pl.BlockSpec((rows, block), lambda j: (0, j)),
-            pl.BlockSpec((width, rows), lambda j: (0, 0)),
+            pl.BlockSpec((width + 16, rows), lambda j: (0, 0)),
         ],
         out_specs=pl.BlockSpec((parts, chunk + 2, block), lambda j: (0, 0, j)),
         out_shape=jax.ShapeDtypeStruct((parts, chunk + 2, total), jnp.float32),
@@ -162,7 +165,7 @@
     table = payload.reshape(-1, pw)
     half_norm = (0.5 * sq_norm)[:, None]
     sendable = score_terms(
-        decoded.T, query_parts.reshape(-1, total), half_norm, keep_t, table.T, parts, 512
+        decoded.T, query_parts.reshape(-1, total), half_norm, keep_t, table.T, parts, 256
     )
     pieces = lax.all_to_all(sendable, "sub", split_axis=0, concat_axis=0, tiled=True)
     peaks_in = pieces[:, chunk + 1, :]

time: 147 us -> 148 us (level)
  no operation moved by 1% of the time
where the time goes in v10:
time: 148 us; the launch traced here: 147 us
  blocking collectives  34.8 us (24%)
  starting transfers between devices  29.4 us (20%)
  waiting for transfers between devices  25.8 us (17%)
  local copies, waits for them, and re-layouts  25.5 us (17%)
  Pallas kernels  19.2 us (13%)
  other arithmetic  11.5 us (8%)
    all_to_all x1, blocking collectives, local(): lax.all_to_all(sendable, 'sub', split_axis=0, concat_axis=0, tiled=True)  25.1 us
    pallas_call x1, Pallas kernels, decode(): pl.pallas_call(decode_kernel, grid=(blocks,), in_specs=[pl.BlockSpec((1,...  11.7 us
    all_to_all x1, waiting for transfers between devices, local(): lax.all_to_all(tables, 'sub', split_axis=0, concat_axis=0, tiled=True)  11.2 us
    all_to_all x1, starting transfers between devices, local(): lax.all_to_all(jnp.concatenate([buffer, cell_marks], axis=1).reshape(grou...  9.97 us
    all_to_all x1, blocking collectives, local(): lax.all_to_all(copies, 'sub', split_axis=0, concat_axis=2, tiled=True)  9.75 us
    all_to_all x1, starting transfers between devices, local(): lax.all_to_all(outgoing.reshape(chunk + 2, groups, capacity), 'cell', spl...  7.96 us
    all_to_all x1, waiting for transfers between devices, local(): lax.all_to_all(outgoing.reshape(chunk + 2, groups, capacity), 'cell', spl...  7.68 us
    pallas_call x1, Pallas kernels, score_terms(): pl.pallas_call(score_kernel, grid=(total // block,), in_specs=[pl.BlockSp...  7.5 us
  transfers between devices with their start and end apart: 4, of which 4 were waited for; matrix products, arithmetic and copies ran while one was open for 12% of the time, Pallas kernels for 8%

profile of v10, /device:TPU:1, one launch (start us, length us, event | category | flops | bytes accessed | tf_op | source)
XLA Modules:
  0.0 146.7 jit_solution(834373681014208350)
XLA Ops:
  0.0 0.7 convert_reduce_fusion
  0.7 0.6 reduce-window.6
  1.6 0.7 select_reduce_fusion
  2.3 0.7 compare_select_fusion.1
  3.3 0.8 convert_element_type.47
  4.2 0.9 copy.93
  5.1 1.8 %scatter_custom_fusion.1 = bf16[1024,16]{1,0:T(8,128)(2,1)S(1)} fusion(s32[512]{0:T(512)S(1)} %bitcast.104, bf16[512,16]{1,0:T(8,128)(2,1)S(1)} %bitcast.102, bf16[]{:T(256)} %constant.54.clone.1), kind=kCustom, calls=%fused_computation.16 | custom fusion | bytes 32770 | tf_op jit(solution)/shard_map/scatter | solution.py:30
  7.0 1.8 %scatter_custom_fusion = bf16[1024,64]{1,0:T(8,128)(2,1)S(1)} fusion(s32[512]{0:T(512)S(1)} %bitcast.105, bf16[512,64]{1,0:T(8,128)(2,1)S(1)} %bitcast.103, bf16[]{:T(256)} %constant.50.clone.1), kind=kCustom, calls=%fused_computation.18 | custom fusion | bytes 131074 | tf_op jit(solution)/shard_map/scatter | solution.py:28
  9.0 0.3 all_to_all.38
  9.3 0.5 broadcast.111
  9.8 1.6 %reduce.8 = bf16[16,5120]{1,0:T(8,128)(2,1)S(1)} reduce(bf16[16,1,5120]{2,1,0:T(2,128)(2,1)S(1)} %all_to_all.38, bf16[]{:T(256)} %broadcast.111), dimensions={1}, to_apply=%all_to_all.38.reduce_sub_computation | reduce | bytes 327682 | tf_op jit(solution)/shard_map/all_to_all | solution.py:143
  11.4 0.8 reshape.245
  12.2 10.0 %all-to-all-start.1 = ((bf16[16,2,2560]{2,1,0:T(2,128)(2,1)}), bf16[16,2,2560]{2,1,0:T(2,128)(2,1)S(1)}, u32[]{:S(2)}, u32[]{:S(2)}) async-start(bf16[16,2,2560]{2,1,0:T(2,128)(2,1)} %reshape.245), calls=%async_computation.1 | async-start | bytes 327680 | tf_op jit(solution)/shard_map/all_to_all | solution.py:143
  22.4 0.7 convert_element_type.42
  23.0 0.4 copy.84
  23.5 0.7 reshape.188
  24.2 0.9 pad_maximum_fusion
  25.1 6.6 %all-to-all-done.1 = bf16[16,2,2560]{2,1,0:T(2,128)(2,1)S(1)} async-done(((bf16[16,2,2560]{2,1,0:T(2,128)(2,1)}), bf16[16,2,2560]{2,1,0:T(2,128)(2,1)S(1)}, u32[]{:S(2)}, u32[]{:S(2)}) %all-to-all-start.1) | async-done | bytes 163872 | tf_op jit(solution)/shard_map/all_to_all | solution.py:143
  31.7 6.8 %all-to-all-start = ((bf16[16,168,128]{2,1,0:T(8,128)(2,1)}), bf16[16,168,128]{2,1,0:T(8,128)(2,1)S(1)}, u32[]{:S(2)}, u32[]{:S(2)}) async-start(bf16[16,168,128]{2,1,0:T(8,128)(2,1)} %pad_maximum_fusion), calls=%async_computation | async-start | bytes 1376256 | tf_op jit(solution)/shard_map/all_to_all | solution.py:127
  38.6 0.9 reduce.6
  39.5 0.3 reshape.201
  40.0 11.2 %all-to-all-done = bf16[16,168,128]{2,1,0:T(8,128)(2,1)S(1)} async-done(((bf16[16,168,128]{2,1,0:T(8,128)(2,1)}), bf16[16,168,128]{2,1,0:T(8,128)(2,1)S(1)}, u32[]{:S(2)}, u32[]{:S(2)}) %all-to-all-start) | async-done | bytes 688160 | tf_op jit(solution)/shard_map/all_to_all | solution.py:127
  51.3 1.6 %broadcast_in_dim.30 = bf16[16,64,1024]{2,1,0:T(8,128)(2,1)} broadcast(bf16[64,1024]{1,0:T(8,128)(2,1)S(1)} %copy.96), dimensions={1,2} | broadcast | bytes 2228224 | tf_op jit(solution)/shard_map/broadcast_in_dim | solution.py:102
  52.8 4.7 %all-to-all-start.2 = ((bf16[16,64,1024]{2,1,0:T(8,128)(2,1)}), bf16[16,64,1024]{2,1,0:T(8,128)(2,1)}, u32[]{:S(2)}, u32[]{:S(2)}) async-start(bf16[16,64,1024]{2,1,0:T(8,128)(2,1)} %broadcast_in_dim.30), calls=%async_computation.2 | async-start | bytes 4194304 | tf_op jit(solution)/shard_map/all_to_all | solution.py:103
  58.1 0.8 pad_maximum_fusion.1.table_ref
  59.1 0.3 fusion.1
  59.4 1.5 %fusion.keep_ref = bf16[768,1024]{1,0:T(8,128)(2,1)} fusion(pred[768]{0:T(1024)(128)(4,1)S(1)} %lt.43, pred[32,1024]{1,0:T(8,128)(4,1)S(1)} %bitcast.101), kind=kLoop, calls=%fused_computation.5 | loop fusion | flops 1572864 | bytes 1606400 | tf_op jit(solution)/shard_map/convert_element_type | solution.py:164
  61.1 1.4 reshape.210
  62.6 1.3 reshape.237.codes_ref
  64.0 1.1 reshape.192.book_ref
  65.7 1.6 %copy.88.base_ref = bf16[1024,768]{1,0:T(8,128)(2,1)} copy(bf16[1024,768]{0,1:T(8,128)(2,1)S(1)} %bitcast.81) | data formatting | bytes 3145728 | tf_op jit(solution)/shard_map/reshape | solution.py:137
  67.3 11.7 %shard_map.82 = bf16[16,64,768]{2,1,0:T(8,128)(2,1)} custom-call(s32[16,4,768]{2,1,0:T(4,128)} %reshape.237.codes_ref, bf16[64,16,256]{2,1,0:T(8,128)(2,1)} %reshape.192.book_ref, bf16[1024,768]{1,0:T(8,128)(2,1)} %copy.88.base_ref), custom_call_target="tpu_custom_call" | custom-call | tf_op jit(solution)/shard_map/pallas_call | solution.py:49
  78.9 2.7 %copy.89 = bf16[1024,768]{0,1:T(8,128)(2,1)} copy(bf16[1024,768]{1,0:T(8,128)(2,1)} %bitcast.80) | data formatting | bytes 3145728 | tf_op jit(solution)/shard_map/reshape | solution.py:153
  81.7 0.4 multiply_reduce_fusion
  82.0 0.9 mul.71.half_ref
  82.9 0.3 all-to-all-done.2
  83.2 7.5 %shard_map.83 = f32[16,18,1024]{2,1,0:T(8,128)} custom-call(bf16[768,1024]{1,0:T(8,128)(2,1)} %bitcast.82, bf16[1024,1024]{1,0:T(8,128)(2,1)} %bitcast.13.q_ref, f32[768,1]{1,0:T(8,128)} %mul.71.half_ref, bf16[768,1024]{1,0:T(8,128)(2,1)} %fusion.keep_ref, bf16[272,768]{1,0:T(8,128)(2,1)} %pad_maximum_fusion.1.table_ref), custom_call_target="tpu_custom_call" | custom-call | tf_op jit(solution)/shard_map/pallas_call | solution.py:85
  90.7 25.1 %all_to_all.45 = f32[16,18,1024]{2,1,0:T(8,128)S(1)} all-to-all(f32[16,18,1024]{2,1,0:T(8,128)} %shard_map.83), channel_id=1, replica_groups=mesh['cell'=16,'sub'=16] {'sub'}, dimensions={0} | all-to-all | bytes 2359296 | tf_op jit(solution)/shard_map/all_to_all | solution.py:170
  116.1 0.2 fusion.2
  116.4 0.8 reshape.247
  117.2 8.0 %all-to-all-start.4 = ((f32[16,1,1152]{2,1,0:T(1,128)}), f32[16,1,1152]{2,1,0:T(1,128)S(1)}, u32[]{:S(2)}, u32[]{:S(2)}) async-start(f32[16,1,1152]{2,1,0:T(1,128)} %reshape.247), calls=%async_computation.4 | async-start | bytes 147456 | tf_op jit(solution)/shard_map/all_to_all | solution.py:176
  125.5 7.7 %all-to-all-done.4 = f32[16,1,1152]{2,1,0:T(1,128)S(1)} async-done(((f32[16,1,1152]{2,1,0:T(1,128)}), f32[16,1,1152]{2,1,0:T(1,128)S(1)}, u32[]{:S(2)}, u32[]{:S(2)}) %all-to-all-start.4) | async-done | bytes 73760 | tf_op jit(solution)/shard_map/all_to_all | solution.py:176
  133.2 0.5 broadcast.112
  133.7 0.8 reduce.9
  134.6 0.2 copy.101
  134.8 1.0 gather_fusion
  136.2 9.7 %all_to_all.46 = bf16[16,256,16]{1,2,0:T(8,128)(2,1)S(1)} all-to-all(bf16[16,256,16]{1,2,0:T(8,128)(2,1)S(1)} %broadcast_in_dim.32), channel_id=1, replica_groups=mesh['cell'=16,'sub'=16] {'sub'}, dimensions={0} | all-to-all | bytes 262144 | tf_op jit(solution)/shard_map/all_to_all | solution.py:190
  145.9 0.8 copy.104
  (72 shorter events, 4.1 us)
Async XLA Ops:
  5.1 17.1 %copy-start.5 = (bf16[32,64]{1,0:T(8,128)(2,1)S(1)}, bf16[32,64]{1,0:T(8,128)(2,1)}, u32[]{:S(2)}) copy-start(bf16[32,64]{1,0:T(8,128)(2,1)} %param.13) | copy-start | bytes 12292
  5.1 17.2 %copy-start.3 = (bf16[4,16,256]{2,1,0:T(8,128)(2,1)S(1)}, bf16[4,16,256]{2,1,0:T(8,128)(2,1)}, u32[]{:S(2)}) copy-start(bf16[4,16,256]{2,1,0:T(8,128)(2,1)} %param.14) | copy-start | bytes 98308
  6.9 15.4 %copy-start.2 = (s32[32,4,384]{2,1,0:T(4,128)S(1)}, s32[32,4,384]{2,1,0:T(4,128)}, u32[]{:S(2)}) copy-start(s32[32,4,384]{2,1,0:T(4,128)} %param.15) | copy-start | bytes 589828
  12.2 19.5 %all-to-all-start.1 = ((bf16[16,2,2560]{2,1,0:T(2,128)(2,1)}), bf16[16,2,2560]{2,1,0:T(2,128)(2,1)S(1)}, u32[]{:S(2)}, u32[]{:S(2)}) async-start(bf16[16,2,2560]{2,1,0:T(2,128)(2,1)} %reshape.245), calls=%async_computation.1 | async-start | bytes 327680 | tf_op jit(solution)/shard_map/all_to_all | solution.py:143
  31.7 19.6 %all-to-all-start = ((bf16[16,168,128]{2,1,0:T(8,128)(2,1)}), bf16[16,168,128]{2,1,0:T(8,128)(2,1)S(1)}, u32[]{:S(2)}, u32[]{:S(2)}) async-start(bf16[16,168,128]{2,1,0:T(8,128)(2,1)} %pad_maximum_fusion), calls=%async_computation | async-start | bytes 1376256 | tf_op jit(solution)/shard_map/all_to_all | solution.py:127
  52.8 4.9 %copy-start.6 = (s32[32]{0:T(128)S(1)}, s32[32]{0:T(128)}, u32[]{:S(2)}) copy-start(s32[32]{0:T(128)} %param.16) | copy-start | bytes 388
  52.8 5.0 %copy-start.1 = (bf16[32,24,256]{2,1,0:T(8,128)(2,1)S(1)}, bf16[32,24,256]{2,1,0:T(8,128)(2,1)}, u32[]{:S(2)}) copy-start(bf16[32,24,256]{2,1,0:T(8,128)(2,1)} %param.17) | copy-start | bytes 1179652
  52.8 5.2 %copy-start.4 = (bf16[16,768]{1,0:T(8,128)(2,1)S(1)}, bf16[16,768]{1,0:T(8,128)(2,1)}, u32[]{:S(2)}) copy-start(bf16[16,768]{1,0:T(8,128)(2,1)} %constant.60.clone.1) | copy-start | bytes 73732
  52.8 30.4 %all-to-all-start.2 = ((bf16[16,64,1024]{2,1,0:T(8,128)(2,1)}), bf16[16,64,1024]{2,1,0:T(8,128)(2,1)}, u32[]{:S(2)}, u32[]{:S(2)}) async-start(bf16[16,64,1024]{2,1,0:T(8,128)(2,1)} %broadcast_in_dim.30), calls=%async_computation.2 | async-start | bytes 4194304 | tf_op jit(solution)/shard_map/all_to_all | solution.py:103
  78.9 2.7 %copy-start = (bf16[16,64,768]{2,1,0:T(8,128)(2,1)S(1)}, bf16[16,64,768]{2,1,0:T(8,128)(2,1)}, u32[]{:S(2)}) copy-start(bf16[16,64,768]{2,1,0:T(8,128)(2,1)} %shard_map.82) | copy-start | bytes 4718596
  117.2 15.9 %all-to-all-start.4 = ((f32[16,1,1152]{2,1,0:T(1,128)}), f32[16,1,1152]{2,1,0:T(1,128)S(1)}, u32[]{:S(2)}, u32[]{:S(2)}) async-start(f32[16,1,1152]{2,1,0:T(1,128)} %reshape.247), calls=%async_computation.4 | async-start | bytes 147456 | tf_op jit(solution)/shard_map/all_to_all | solution.py:176

commit v11 on v6

--- a/solution.py
+++ b/solution.py
@@ -77,17 +77,18 @@
     cell_count, sub_count, row_count = codes.shape
     rows_part = row_count // parts
     own_codes = codes.reshape(cell_count, sub_count, parts, rows_part)
-    own_codes = jnp.transpose(own_codes, (2, 0, 1, 3)).astype(jnp.bfloat16).reshape(parts, -1)
+    own_codes = jnp.transpose(own_codes, (2, 0, 1, 3)).astype(jnp.bfloat16).reshape(parts, -1, 128)
     tables = jnp.concatenate(
         [
             own_codes,
-            jnp.broadcast_to(codebooks.reshape(1, -1), (parts, codebooks.size)),
-            jnp.broadcast_to(coarse.reshape(1, -1), (parts, coarse.size)),
+            jnp.broadcast_to(codebooks.reshape(1, -1, 128), (parts, codebooks.size // 128, 128)),
+            jnp.broadcast_to(coarse.reshape(1, -1, 128), (parts, coarse.size // 128, 128)),
         ],
         axis=1,
     )
     tables = lax.all_to_all(tables, "sub", split_axis=0, concat_axis=0, tiled=True)
-    code_size = own_codes.shape[1]
+    tables = tables.reshape(parts, -1)
+    code_size = own_codes.shape[1] * own_codes.shape[2]
     book_size = codebooks.size
     got_codes = tables[:, :code_size].reshape(parts, cell_count, sub_count, rows_part)
     got_codes = jnp.transpose(got_codes, (0, 2, 1, 3)).astype(jnp.int32)
@@ -140,7 +141,9 @@
         ],
         axis=1,
     )
-    pieces = lax.all_to_all(sendable, "sub", split_axis=0, concat_axis=0, tiled=True)
+    pieces = lax.all_to_all(
+        sendable.reshape(parts, -1, 128), "sub", split_axis=0, concat_axis=0, tiled=True
+    ).reshape(sendable.shape)
     peaks_in = pieces[:, chunk + 1, :]
     peak = jnp.max(peaks_in, axis=0)
     shift = jnp.exp(peaks_in - peak[None, :])
@@ -158,8 +161,10 @@
     scale = jnp.exp(peaks - top)
     upper = jnp.sum(scale[None, :, :] * parts_back, axis=2)
     lower = jnp.sum(scale * masses, axis=1)
-    pooled = (upper / lower[None, :]).astype(jnp.bfloat16)
-    return gather_by_exchange(pooled, "sub").reshape(pw, -1).T
+    pooled = (upper / lower[None, :]).T.astype(jnp.bfloat16)
+    copies = jnp.broadcast_to(pooled[None], (parts,) + pooled.shape)
+    gathered = lax.all_to_all(copies, "sub", split_axis=0, concat_axis=2, tiled=True)
+    return gathered.reshape(pooled.shape[0], pw)
 
 
 def solution(mesh):

time: 146 us -> 143 us (0.979)
  blocking collectives: 33.9 us -> 30 us
  waiting for transfers between devices: 28.1 us -> 30.5 us
    all_to_all x2, blocking collectives: 33.9 us -> 30 us  [the longest x1 20.1 us: local(): lax.all_to_all(sendable.reshape(parts, -1, 128), 'sub', split_axis=0, con...]
    reshape x1 -> x4, local copies, waits for them, and re-layouts: 0.01 us -> 2.37 us  [the longest x1 1.41 us: local(): pieces = lax.all_to_all(sendable.reshape(parts, -1, 128), 'sub', split_ax...]
    unnamed x23 -> x20, local copies, waits for them, and re-layouts: 4.95 us -> 2.86 us
    all_to_all x1, waiting for transfers between devices: 4.88 us -> 6.55 us  [local(): lax.all_to_all(jnp.concatenate([buffer, cell_marks], axis=1).reshape(grou...]
  transfers between devices with their start and end apart: 4 -> 4, of which waited for: 4 -> 4; matrix products, arithmetic and copies ran while one was open for 11% -> 10% of each run, Pallas kernels for 8% -> 8%
where the time goes in v11:
time: 143 us; the launch traced here: 142 us
  waiting for transfers between devices  30.5 us (21%)
  blocking collectives  30 us (21%)
  starting transfers between devices  29.4 us (21%)
  local copies, waits for them, and re-layouts  23.3 us (16%)
  other arithmetic  12.1 us (8%)
  Pallas kernels  11.7 us (8%)
  matrix products  4.53 us (3%)
    all_to_all x1, blocking collectives, local(): lax.all_to_all(sendable.reshape(parts, -1, 128), 'sub', split_axis=0, con...  20.1 us
    pallas_call x1, Pallas kernels, decode(): pl.pallas_call(decode_kernel, grid=(blocks,), in_specs=[pl.BlockSpec((1,...  11.7 us
    all_to_all x1, waiting for transfers between devices, local(): lax.all_to_all(tables, 'sub', split_axis=0, concat_axis=0, tiled=True)  11.2 us
    all_to_all x1, starting transfers between devices, local(): lax.all_to_all(jnp.concatenate([buffer, cell_marks], axis=1).reshape(grou...  10.1 us
    all_to_all x1, blocking collectives, local(): lax.all_to_all(copies, 'sub', split_axis=0, concat_axis=2, tiled=True)  9.87 us
    all_to_all x1, starting transfers between devices, local(): lax.all_to_all(outgoing.reshape(chunk + 2, groups, capacity), 'cell', spl...  7.83 us
    all_to_all x1, waiting for transfers between devices, local(): lax.all_to_all(outgoing.reshape(chunk + 2, groups, capacity), 'cell', spl...  7.68 us
    all_to_all x1, starting transfers between devices, local(): lax.all_to_all(tables, 'sub', split_axis=0, concat_axis=0, tiled=True)  6.76 us
  transfers between devices with their start and end apart: 4, of which 4 were waited for; matrix products, arithmetic and copies ran while one was open for 10% of the time, Pallas kernels for 8%

profile of v11, /device:TPU:1, one launch (start us, length us, event | category | flops | bytes accessed | tf_op | source)
XLA Modules:
  0.0 142.0 jit_solution(10977955743654922999)
XLA Ops:
  0.0 0.7 convert_reduce_fusion.1
  0.7 0.6 reduce-window.6
  1.6 0.7 select_reduce_fusion.1
  2.4 0.7 compare_select_fusion.1
  3.3 0.9 copy.75
  4.2 0.8 convert_element_type.45
  5.2 1.8 %scatter_custom_fusion = bf16[1024,64]{1,0:T(8,128)(2,1)S(1)} fusion(s32[512]{0:T(512)S(1)} %bitcast.115, bf16[512,64]{1,0:T(8,128)(2,1)S(1)} %bitcast.114, bf16[]{:T(256)} %constant.13.clone.1), kind=kCustom, calls=%fused_computation.22 | custom fusion | bytes 131074 | tf_op jit(solution)/shard_map/scatter | solution.py:28
  7.0 1.8 %scatter_custom_fusion.1 = bf16[1024,16]{1,0:T(8,128)(2,1)S(1)} fusion(s32[512]{0:T(512)S(1)} %bitcast.116, bf16[512,16]{1,0:T(8,128)(2,1)S(1)} %bitcast.113, bf16[]{:T(256)} %constant.17.clone.1), kind=kCustom, calls=%fused_computation.20 | custom fusion | bytes 32770 | tf_op jit(solution)/shard_map/scatter | solution.py:30
  9.0 0.3 all_to_all.38
  9.4 0.5 broadcast.89
  9.9 1.6 %reduce.6 = bf16[16,5120]{1,0:T(8,128)(2,1)S(1)} reduce(bf16[16,1,5120]{2,1,0:T(2,128)(2,1)S(1)} %all_to_all.38, bf16[]{:T(256)} %broadcast.89), dimensions={1}, to_apply=%all_to_all.38.reduce_sub_computation | reduce | bytes 327682 | tf_op jit(solution)/shard_map/all_to_all | solution.py:105
  11.5 0.8 reshape.229
  12.2 10.1 %all-to-all-start = ((bf16[16,2,2560]{2,1,0:T(2,128)(2,1)}), bf16[16,2,2560]{2,1,0:T(2,128)(2,1)S(1)}, u32[]{:S(2)}, u32[]{:S(2)}) async-start(bf16[16,2,2560]{2,1,0:T(2,128)(2,1)} %reshape.229), calls=%async_computation | async-start | bytes 327680 | tf_op jit(solution)/shard_map/all_to_all | solution.py:105
  22.4 0.7 convert_element_type.49
  23.1 0.4 copy.81
  23.5 0.7 reshape.175
  24.4 0.9 pad_maximum_fusion.1
  25.3 6.5 %all-to-all-done = bf16[16,2,2560]{2,1,0:T(2,128)(2,1)S(1)} async-done(((bf16[16,2,2560]{2,1,0:T(2,128)(2,1)}), bf16[16,2,2560]{2,1,0:T(2,128)(2,1)S(1)}, u32[]{:S(2)}, u32[]{:S(2)}) %all-to-all-start) | async-done | bytes 163872 | tf_op jit(solution)/shard_map/all_to_all | solution.py:105
  31.9 6.8 %all-to-all-start.2 = ((bf16[16,168,128]{2,1,0:T(8,128)(2,1)}), bf16[16,168,128]{2,1,0:T(8,128)(2,1)S(1)}, u32[]{:S(2)}, u32[]{:S(2)}) async-start(bf16[16,168,128]{2,1,0:T(8,128)(2,1)} %pad_maximum_fusion.1), calls=%async_computation.2 | async-start | bytes 1376256 | tf_op jit(solution)/shard_map/all_to_all | solution.py:89
  38.8 0.9 reduce.4
  39.7 0.3 reshape.174
  40.2 11.2 %all-to-all-done.2 = bf16[16,168,128]{2,1,0:T(8,128)(2,1)S(1)} async-done(((bf16[16,168,128]{2,1,0:T(8,128)(2,1)}), bf16[16,168,128]{2,1,0:T(8,128)(2,1)S(1)}, u32[]{:S(2)}, u32[]{:S(2)}) %all-to-all-start.2) | async-done | bytes 688160 | tf_op jit(solution)/shard_map/all_to_all | solution.py:89
  51.4 1.6 %broadcast_in_dim.36 = bf16[16,64,1024]{2,1,0:T(8,128)(2,1)} broadcast(bf16[64,1024]{1,0:T(8,128)(2,1)S(1)} %copy.79), dimensions={1,2} | broadcast | bytes 2228224 | tf_op jit(solution)/shard_map/broadcast_in_dim | solution.py:64
  53.0 4.7 %all-to-all-start.1 = ((bf16[16,64,1024]{2,1,0:T(8,128)(2,1)}), bf16[16,64,1024]{2,1,0:T(8,128)(2,1)}, u32[]{:S(2)}, u32[]{:S(2)}) async-start(bf16[16,64,1024]{2,1,0:T(8,128)(2,1)} %broadcast_in_dim.36), calls=%async_computation.1 | async-start | bytes 4194304 | tf_op jit(solution)/shard_map/all_to_all | solution.py:65
  58.3 0.3 fusion.1
  59.3 1.6 %copy.85.base_ref = bf16[1024,768]{1,0:T(8,128)(2,1)} copy(bf16[1024,768]{0,1:T(8,128)(2,1)S(1)} %bitcast.96) | data formatting | bytes 3145728 | tf_op jit(solution)/shard_map/reshape | solution.py:99
  60.9 1.4 reshape.193
  62.5 1.3 reshape.221.codes_ref
  63.8 1.0 reshape.179.book_ref
  64.8 11.7 %shard_map.82 = bf16[16,64,768]{2,1,0:T(8,128)(2,1)} custom-call(s32[16,4,768]{2,1,0:T(4,128)} %reshape.221.codes_ref, bf16[64,16,256]{2,1,0:T(8,128)(2,1)} %reshape.179.book_ref, bf16[1024,768]{1,0:T(8,128)(2,1)} %copy.85.base_ref), custom_call_target="tpu_custom_call" | custom-call | tf_op jit(solution)/shard_map/pallas_call | solution.py:49
  76.5 1.9 %multiply_reduce_fusion = f32[768]{0:T(1024)S(1)} fusion(bf16[16,64,768]{2,1,0:T(8,128)(2,1)} %shard_map.82), kind=kLoop, calls=%fused_computation.8 | loop fusion | flops 2358528 | bytes 1575936 | tf_op jit(solution)/shard_map/reduce_sum | solution.py:122
  78.4 5.0 %all-to-all-done.1 = bf16[16,64,1024]{2,1,0:T(8,128)(2,1)} async-done(((bf16[16,64,1024]{2,1,0:T(8,128)(2,1)}), bf16[16,64,1024]{2,1,0:T(8,128)(2,1)}, u32[]{:S(2)}, u32[]{:S(2)}) %all-to-all-start.1) | async-done | bytes 2097184 | tf_op jit(solution)/shard_map/all_to_all | solution.py:65
  83.4 3.9 %select_reduce_fusion = (f32[1024]{0:T(1024)S(1)}, f32[1024,768,1]{0,1,2:T(8,128)S(1)}) fusion(f32[768]{0:T(1024)S(1)} %broadcast_multiply_fusion, pred[768]{0:T(1024)(128)(4,1)S(1)} %lt.43, pred[1024,32]{0,1:T(8,128)(4,1)S(1)} %fusion.1, bf16[16,64,1024]{2,1,0:T(8,128)(2,1)} %all-to-all-done.1, bf16[16,64,768]{2,1,0:T(8,128)(2,1)S(1)} %copy-done.1), kind=kOutput, calls=%fused_computation.7 | convolution fusion | flops 1614543872 | bytes 6856448 | tf_op jit(solution)/shard_map/sdq,sdr->qr/dot_general | solution.py:128
  87.3 1.1 convert_reduce_fusion
  88.5 0.6 fusion.13
  89.2 0.2 pad_maximum_fusion
  89.4 0.2 reshape.185
  89.6 20.1 %all_to_all.45 = f32[16,144,128]{2,1,0:T(8,128)} all-to-all(f32[16,144,128]{2,1,0:T(8,128)S(1)} %reshape.185), channel_id=1, replica_groups=mesh['cell'=16,'sub'=16] {'sub'}, dimensions={0} | all-to-all | bytes 2359296 | tf_op jit(solution)/shard_map/all_to_all | solution.py:144
  109.7 1.4 reshape.186
  111.8 0.8 reshape.231
  112.6 7.8 %all-to-all-start.4 = ((f32[16,1,1152]{2,1,0:T(1,128)}), f32[16,1,1152]{2,1,0:T(1,128)S(1)}, u32[]{:S(2)}, u32[]{:S(2)}) async-start(f32[16,1,1152]{2,1,0:T(1,128)} %reshape.231), calls=%async_computation.4 | async-start | bytes 147456 | tf_op jit(solution)/shard_map/all_to_all | solution.py:152
  120.7 7.7 %all-to-all-done.4 = f32[16,1,1152]{2,1,0:T(1,128)S(1)} async-done(((f32[16,1,1152]{2,1,0:T(1,128)}), f32[16,1,1152]{2,1,0:T(1,128)S(1)}, u32[]{:S(2)}, u32[]{:S(2)}) %all-to-all-start.4) | async-done | bytes 73760 | tf_op jit(solution)/shard_map/all_to_all | solution.py:152
  128.4 0.5 broadcast.90
  128.9 0.8 reduce.7
  129.8 0.2 copy.87
  130.0 1.0 gather_fusion
  131.4 9.9 %all_to_all.46 = bf16[16,256,16]{1,2,0:T(8,128)(2,1)S(1)} all-to-all(bf16[16,256,16]{1,2,0:T(8,128)(2,1)S(1)} %broadcast_in_dim.47), channel_id=1, replica_groups=mesh['cell'=16,'sub'=16] {'sub'}, dimensions={0} | all-to-all | bytes 262144 | tf_op jit(solution)/shard_map/all_to_all | solution.py:166
  141.2 0.8 copy.90
  (72 shorter events, 4.1 us)
Async XLA Ops:
  0.0 88.5 %copy-start = (bf16[32,24,256]{2,1,0:T(8,128)(2,1)S(1)}, bf16[32,24,256]{2,1,0:T(8,128)(2,1)}, u32[]{:S(2)}) copy-start(bf16[32,24,256]{2,1,0:T(8,128)(2,1)} %param.15) | copy-start | bytes 1179652
  5.2 17.1 %copy-start.2 = (s32[32,4,384]{2,1,0:T(4,128)S(1)}, s32[32,4,384]{2,1,0:T(4,128)}, u32[]{:S(2)}) copy-start(s32[32,4,384]{2,1,0:T(4,128)} %param.13) | copy-start | bytes 589828
  12.2 11.9 %copy-start.3 = (bf16[4,16,256]{2,1,0:T(8,128)(2,1)S(1)}, bf16[4,16,256]{2,1,0:T(8,128)(2,1)}, u32[]{:S(2)}) copy-start(bf16[4,16,256]{2,1,0:T(8,128)(2,1)} %param.12) | copy-start | bytes 98308
  12.2 12.0 %copy-start.4 = (bf16[32,64]{1,0:T(8,128)(2,1)S(1)}, bf16[32,64]{1,0:T(8,128)(2,1)}, u32[]{:S(2)}) copy-start(bf16[32,64]{1,0:T(8,128)(2,1)} %param.11) | copy-start | bytes 12292
  12.2 19.6 %all-to-all-start = ((bf16[16,2,2560]{2,1,0:T(2,128)(2,1)}), bf16[16,2,2560]{2,1,0:T(2,128)(2,1)S(1)}, u32[]{:S(2)}, u32[]{:S(2)}) async-start(bf16[16,2,2560]{2,1,0:T(2,128)(2,1)} %reshape.229), calls=%async_computation | async-start | bytes 327680 | tf_op jit(solution)/shard_map/all_to_all | solution.py:105
  31.9 19.6 %all-to-all-start.2 = ((bf16[16,168,128]{2,1,0:T(8,128)(2,1)}), bf16[16,168,128]{2,1,0:T(8,128)(2,1)S(1)}, u32[]{:S(2)}, u32[]{:S(2)}) async-start(bf16[16,168,128]{2,1,0:T(8,128)(2,1)} %pad_maximum_fusion.1), calls=%async_computation.2 | async-start | bytes 1376256 | tf_op jit(solution)/shard_map/all_to_all | solution.py:89
  53.0 4.9 %copy-start.5 = (s32[32]{0:T(128)S(1)}, s32[32]{0:T(128)}, u32[]{:S(2)}) copy-start(s32[32]{0:T(128)} %param.14) | copy-start | bytes 388
  53.0 30.4 %all-to-all-start.1 = ((bf16[16,64,1024]{2,1,0:T(8,128)(2,1)}), bf16[16,64,1024]{2,1,0:T(8,128)(2,1)}, u32[]{:S(2)}, u32[]{:S(2)}) async-start(bf16[16,64,1024]{2,1,0:T(8,128)(2,1)} %broadcast_in_dim.36), calls=%async_computation.1 | async-start | bytes 4194304 | tf_op jit(solution)/shard_map/all_to_all | solution.py:65
  76.5 6.9 %copy-start.1 = (bf16[16,64,768]{2,1,0:T(8,128)(2,1)S(1)}, bf16[16,64,768]{2,1,0:T(8,128)(2,1)}, u32[]{:S(2)}) copy-start(bf16[16,64,768]{2,1,0:T(8,128)(2,1)} %shard_map.82) | copy-start | bytes 4718596
  112.6 15.8 %all-to-all-start.4 = ((f32[16,1,1152]{2,1,0:T(1,128)}), f32[16,1,1152]{2,1,0:T(1,128)S(1)}, u32[]{:S(2)}, u32[]{:S(2)}) async-start(f32[16,1,1152]{2,1,0:T(1,128)} %reshape.231), calls=%async_computation.4 | async-start | bytes 147456 | tf_op jit(solution)/shard_map/all_to_all | solution.py:152

commit v12 on v11

--- a/solution.py
+++ b/solution.py
@@ -143,11 +143,12 @@
     )
     pieces = lax.all_to_all(
         sendable.reshape(parts, -1, 128), "sub", split_axis=0, concat_axis=0, tiled=True
-    ).reshape(sendable.shape)
-    peaks_in = pieces[:, chunk + 1, :]
+    ).reshape(parts, chunk + 2, -1, 128)
+    peaks_in = pieces[:, chunk + 1]
     peak = jnp.max(peaks_in, axis=0)
-    shift = jnp.exp(peaks_in - peak[None, :])
-    reduced = jnp.sum(shift[:, None, :] * pieces[:, : chunk + 1, :], axis=0)
+    shift = jnp.exp(peaks_in - peak[None])
+    reduced = jnp.sum(shift[:, None] * pieces[:, : chunk + 1], axis=0).reshape(chunk + 1, total)
+    peak = peak.reshape(total)
     outgoing = jnp.concatenate([reduced, peak[None, :]], axis=0)
     back = lax.all_to_all(
         outgoing.reshape(chunk + 2, groups, capacity), "cell", split_axis=1, concat_axis=1, tiled=True

time: 143 us -> 141 us (0.986)
  local copies, waits for them, and re-layouts: 23.3 us -> 21.8 us
where the time goes in v12:
time: 141 us; the launch traced here: 140 us
  waiting for transfers between devices  30.5 us (22%)
  blocking collectives  29.9 us (21%)
  starting transfers between devices  29.4 us (21%)
  local copies, waits for them, and re-layouts  21.8 us (15%)
  other arithmetic  11.9 us (8%)
  Pallas kernels  11.7 us (8%)
  matrix products  4.53 us (3%)
    all_to_all x1, blocking collectives, local(): lax.all_to_all(sendable.reshape(parts, -1, 128), 'sub', split_axis=0, con...  20 us
    pallas_call x1, Pallas kernels, decode(): pl.pallas_call(decode_kernel, grid=(blocks,), in_specs=[pl.BlockSpec((1,...  11.7 us
    all_to_all x1, waiting for transfers between devices, local(): lax.all_to_all(tables, 'sub', split_axis=0, concat_axis=0, tiled=True)  11.2 us
    all_to_all x1, starting transfers between devices, local(): lax.all_to_all(jnp.concatenate([buffer, cell_marks], axis=1).reshape(grou...  10.1 us
    all_to_all x1, blocking collectives, local(): lax.all_to_all(copies, 'sub', split_axis=0, concat_axis=2, tiled=True)  9.87 us
    all_to_all x1, starting transfers between devices, local(): lax.all_to_all(outgoing.reshape(chunk + 2, groups, capacity), 'cell', spl...  7.83 us
    all_to_all x1, waiting for transfers between devices, local(): lax.all_to_all(outgoing.reshape(chunk + 2, groups, capacity), 'cell', spl...  7.68 us
    all_to_all x1, starting transfers between devices, local(): lax.all_to_all(tables, 'sub', split_axis=0, concat_axis=0, tiled=True)  6.76 us
  transfers between devices with their start and end apart: 4, of which 4 were waited for; matrix products, arithmetic and copies ran while one was open for 10% of the time, Pallas kernels for 8%

profile of v12, /device:TPU:1, one launch (start us, length us, event | category | flops | bytes accessed | tf_op | source)
XLA Modules:
  0.0 140.2 jit_solution(4113810421302677427)
XLA Ops:
  0.0 0.7 convert_reduce_fusion.1
  0.7 0.6 reduce-window.6
  1.6 0.7 select_reduce_fusion.1
  2.4 0.7 compare_select_fusion.1
  3.3 0.9 copy.75
  4.2 0.8 convert_element_type.45
  5.2 1.8 %scatter_custom_fusion = bf16[1024,64]{1,0:T(8,128)(2,1)S(1)} fusion(s32[512]{0:T(512)S(1)} %bitcast.117, bf16[512,64]{1,0:T(8,128)(2,1)S(1)} %bitcast.116, bf16[]{:T(256)} %constant.13.clone.1), kind=kCustom, calls=%fused_computation.22 | custom fusion | bytes 131074 | tf_op jit(solution)/shard_map/scatter | solution.py:28
  7.0 1.8 %scatter_custom_fusion.1 = bf16[1024,16]{1,0:T(8,128)(2,1)S(1)} fusion(s32[512]{0:T(512)S(1)} %bitcast.118, bf16[512,16]{1,0:T(8,128)(2,1)S(1)} %bitcast.115, bf16[]{:T(256)} %constant.17.clone.1), kind=kCustom, calls=%fused_computation.20 | custom fusion | bytes 32770 | tf_op jit(solution)/shard_map/scatter | solution.py:30
  9.0 0.3 all_to_all.38
  9.4 0.5 broadcast.88
  9.9 1.6 %reduce.6 = bf16[16,5120]{1,0:T(8,128)(2,1)S(1)} reduce(bf16[16,1,5120]{2,1,0:T(2,128)(2,1)S(1)} %all_to_all.38, bf16[]{:T(256)} %broadcast.88), dimensions={1}, to_apply=%all_to_all.38.reduce_sub_computation | reduce | bytes 327682 | tf_op jit(solution)/shard_map/all_to_all | solution.py:105
  11.5 0.8 reshape.226
  12.2 10.1 %all-to-all-start = ((bf16[16,2,2560]{2,1,0:T(2,128)(2,1)}), bf16[16,2,2560]{2,1,0:T(2,128)(2,1)S(1)}, u32[]{:S(2)}, u32[]{:S(2)}) async-start(bf16[16,2,2560]{2,1,0:T(2,128)(2,1)} %reshape.226), calls=%async_computation | async-start | bytes 327680 | tf_op jit(solution)/shard_map/all_to_all | solution.py:105
  22.4 0.7 convert_element_type.49
  23.1 0.4 copy.81
  23.5 0.7 reshape.172
  24.4 0.9 pad_maximum_fusion.1
  25.3 6.5 %all-to-all-done = bf16[16,2,2560]{2,1,0:T(2,128)(2,1)S(1)} async-done(((bf16[16,2,2560]{2,1,0:T(2,128)(2,1)}), bf16[16,2,2560]{2,1,0:T(2,128)(2,1)S(1)}, u32[]{:S(2)}, u32[]{:S(2)}) %all-to-all-start) | async-done | bytes 163872 | tf_op jit(solution)/shard_map/all_to_all | solution.py:105
  31.9 6.8 %all-to-all-start.2 = ((bf16[16,168,128]{2,1,0:T(8,128)(2,1)}), bf16[16,168,128]{2,1,0:T(8,128)(2,1)S(1)}, u32[]{:S(2)}, u32[]{:S(2)}) async-start(bf16[16,168,128]{2,1,0:T(8,128)(2,1)} %pad_maximum_fusion.1), calls=%async_computation.2 | async-start | bytes 1376256 | tf_op jit(solution)/shard_map/all_to_all | solution.py:89
  38.8 0.9 reduce.4
  39.7 0.3 reshape.171
  40.2 11.2 %all-to-all-done.2 = bf16[16,168,128]{2,1,0:T(8,128)(2,1)S(1)} async-done(((bf16[16,168,128]{2,1,0:T(8,128)(2,1)}), bf16[16,168,128]{2,1,0:T(8,128)(2,1)S(1)}, u32[]{:S(2)}, u32[]{:S(2)}) %all-to-all-start.2) | async-done | bytes 688160 | tf_op jit(solution)/shard_map/all_to_all | solution.py:89
  51.4 1.6 %broadcast_in_dim.36 = bf16[16,64,1024]{2,1,0:T(8,128)(2,1)} broadcast(bf16[64,1024]{1,0:T(8,128)(2,1)S(1)} %copy.79), dimensions={1,2} | broadcast | bytes 2228224 | tf_op jit(solution)/shard_map/broadcast_in_dim | solution.py:64
  53.0 4.7 %all-to-all-start.1 = ((bf16[16,64,1024]{2,1,0:T(8,128)(2,1)}), bf16[16,64,1024]{2,1,0:T(8,128)(2,1)}, u32[]{:S(2)}, u32[]{:S(2)}) async-start(bf16[16,64,1024]{2,1,0:T(8,128)(2,1)} %broadcast_in_dim.36), calls=%async_computation.1 | async-start | bytes 4194304 | tf_op jit(solution)/shard_map/all_to_all | solution.py:65
  58.3 0.3 fusion.1
  59.1 0.2 broadcast_in_dim.41
  59.3 1.6 %copy.85.base_ref = bf16[1024,768]{1,0:T(8,128)(2,1)} copy(bf16[1024,768]{0,1:T(8,128)(2,1)S(1)} %bitcast.96) | data formatting | bytes 3145728 | tf_op jit(solution)/shard_map/reshape | solution.py:99
  60.9 1.4 reshape.190
  62.5 1.3 reshape.218.codes_ref
  63.8 1.0 reshape.176.book_ref
  64.8 11.7 %shard_map.82 = bf16[16,64,768]{2,1,0:T(8,128)(2,1)} custom-call(s32[16,4,768]{2,1,0:T(4,128)} %reshape.218.codes_ref, bf16[64,16,256]{2,1,0:T(8,128)(2,1)} %reshape.176.book_ref, bf16[1024,768]{1,0:T(8,128)(2,1)} %copy.85.base_ref), custom_call_target="tpu_custom_call" | custom-call | tf_op jit(solution)/shard_map/pallas_call | solution.py:49
  76.5 1.9 %multiply_reduce_fusion = f32[768]{0:T(1024)S(1)} fusion(bf16[16,64,768]{2,1,0:T(8,128)(2,1)} %shard_map.82), kind=kLoop, calls=%fused_computation.8 | loop fusion | flops 2358528 | bytes 1575936 | tf_op jit(solution)/shard_map/reduce_sum | solution.py:122
  78.4 5.0 %all-to-all-done.1 = bf16[16,64,1024]{2,1,0:T(8,128)(2,1)} async-done(((bf16[16,64,1024]{2,1,0:T(8,128)(2,1)}), bf16[16,64,1024]{2,1,0:T(8,128)(2,1)}, u32[]{:S(2)}, u32[]{:S(2)}) %all-to-all-start.1) | async-done | bytes 2097184 | tf_op jit(solution)/shard_map/all_to_all | solution.py:65
  83.4 3.9 %select_reduce_fusion = (f32[1024]{0:T(1024)S(1)}, f32[1024,768,1]{0,1,2:T(8,128)S(1)}) fusion(f32[768]{0:T(1024)S(1)} %broadcast_multiply_fusion, pred[768]{0:T(1024)(128)(4,1)S(1)} %lt.43, pred[1024,32]{0,1:T(8,128)(4,1)S(1)} %fusion.1, bf16[16,64,1024]{2,1,0:T(8,128)(2,1)} %all-to-all-done.1, bf16[16,64,768]{2,1,0:T(8,128)(2,1)S(1)} %copy-done.1), kind=kOutput, calls=%fused_computation.7 | convolution fusion | flops 1614543872 | bytes 6856448 | tf_op jit(solution)/shard_map/sdq,sdr->qr/dot_general | solution.py:128
  87.3 1.1 convert_reduce_fusion
  88.5 0.6 fusion.13
  89.2 0.2 pad_maximum_fusion
  89.4 0.2 reshape.182
  89.6 20.0 %all_to_all.45 = f32[16,144,128]{2,1,0:T(8,128)S(1)} all-to-all(f32[16,144,128]{2,1,0:T(8,128)S(1)} %reshape.182), channel_id=1, replica_groups=mesh['cell'=16,'sub'=16] {'sub'}, dimensions={0} | all-to-all | bytes 2359296 | tf_op jit(solution)/shard_map/all_to_all | solution.py:144
  110.0 0.8 reshape.228
  110.8 7.8 %all-to-all-start.4 = ((f32[16,1,1152]{2,1,0:T(1,128)}), f32[16,1,1152]{2,1,0:T(1,128)S(1)}, u32[]{:S(2)}, u32[]{:S(2)}) async-start(f32[16,1,1152]{2,1,0:T(1,128)} %reshape.228), calls=%async_computation.4 | async-start | bytes 147456 | tf_op jit(solution)/shard_map/all_to_all | solution.py:153
  118.9 7.7 %all-to-all-done.4 = f32[16,1,1152]{2,1,0:T(1,128)S(1)} async-done(((f32[16,1,1152]{2,1,0:T(1,128)}), f32[16,1,1152]{2,1,0:T(1,128)S(1)}, u32[]{:S(2)}, u32[]{:S(2)}) %all-to-all-start.4) | async-done | bytes 73760 | tf_op jit(solution)/shard_map/all_to_all | solution.py:153
  126.6 0.5 broadcast.89
  127.1 0.8 reduce.7
  128.0 0.2 copy.87
  128.2 1.0 gather_fusion
  129.6 9.9 %all_to_all.46 = bf16[16,256,16]{1,2,0:T(8,128)(2,1)S(1)} all-to-all(bf16[16,256,16]{1,2,0:T(8,128)(2,1)S(1)} %broadcast_in_dim.92), channel_id=1, replica_groups=mesh['cell'=16,'sub'=16] {'sub'}, dimensions={0} | all-to-all | bytes 262144 | tf_op jit(solution)/shard_map/all_to_all | solution.py:167
  139.4 0.8 copy.90
  (70 shorter events, 3.7 us)
Async XLA Ops:
  0.0 88.5 %copy-start = (bf16[32,24,256]{2,1,0:T(8,128)(2,1)S(1)}, bf16[32,24,256]{2,1,0:T(8,128)(2,1)}, u32[]{:S(2)}) copy-start(bf16[32,24,256]{2,1,0:T(8,128)(2,1)} %param.15) | copy-start | bytes 1179652
  5.2 17.1 %copy-start.2 = (s32[32,4,384]{2,1,0:T(4,128)S(1)}, s32[32,4,384]{2,1,0:T(4,128)}, u32[]{:S(2)}) copy-start(s32[32,4,384]{2,1,0:T(4,128)} %param.13) | copy-start | bytes 589828
  12.2 11.9 %copy-start.3 = (bf16[4,16,256]{2,1,0:T(8,128)(2,1)S(1)}, bf16[4,16,256]{2,1,0:T(8,128)(2,1)}, u32[]{:S(2)}) copy-start(bf16[4,16,256]{2,1,0:T(8,128)(2,1)} %param.12) | copy-start | bytes 98308
  12.2 12.0 %copy-start.4 = (bf16[32,64]{1,0:T(8,128)(2,1)S(1)}, bf16[32,64]{1,0:T(8,128)(2,1)}, u32[]{:S(2)}) copy-start(bf16[32,64]{1,0:T(8,128)(2,1)} %param.11) | copy-start | bytes 12292
  12.2 19.6 %all-to-all-start = ((bf16[16,2,2560]{2,1,0:T(2,128)(2,1)}), bf16[16,2,2560]{2,1,0:T(2,128)(2,1)S(1)}, u32[]{:S(2)}, u32[]{:S(2)}) async-start(bf16[16,2,2560]{2,1,0:T(2,128)(2,1)} %reshape.226), calls=%async_computation | async-start | bytes 327680 | tf_op jit(solution)/shard_map/all_to_all | solution.py:105
  31.9 19.6 %all-to-all-start.2 = ((bf16[16,168,128]{2,1,0:T(8,128)(2,1)}), bf16[16,168,128]{2,1,0:T(8,128)(2,1)S(1)}, u32[]{:S(2)}, u32[]{:S(2)}) async-start(bf16[16,168,128]{2,1,0:T(8,128)(2,1)} %pad_maximum_fusion.1), calls=%async_computation.2 | async-start | bytes 1376256 | tf_op jit(solution)/shard_map/all_to_all | solution.py:89
  53.0 4.9 %copy-start.5 = (s32[32]{0:T(128)S(1)}, s32[32]{0:T(128)}, u32[]{:S(2)}) copy-start(s32[32]{0:T(128)} %param.14) | copy-start | bytes 388
  53.0 30.4 %all-to-all-start.1 = ((bf16[16,64,1024]{2,1,0:T(8,128)(2,1)}), bf16[16,64,1024]{2,1,0:T(8,128)(2,1)}, u32[]{:S(2)}, u32[]{:S(2)}) async-start(bf16[16,64,1024]{2,1,0:T(8,128)(2,1)} %broadcast_in_dim.36), calls=%async_computation.1 | async-start | bytes 4194304 | tf_op jit(solution)/shard_map/all_to_all | solution.py:65
  76.5 6.9 %copy-start.1 = (bf16[16,64,768]{2,1,0:T(8,128)(2,1)S(1)}, bf16[16,64,768]{2,1,0:T(8,128)(2,1)}, u32[]{:S(2)}) copy-start(bf16[16,64,768]{2,1,0:T(8,128)(2,1)} %shard_map.82) | copy-start | bytes 4718596
  110.8 15.8 %all-to-all-start.4 = ((f32[16,1,1152]{2,1,0:T(1,128)}), f32[16,1,1152]{2,1,0:T(1,128)S(1)}, u32[]{:S(2)}, u32[]{:S(2)}) async-start(f32[16,1,1152]{2,1,0:T(1,128)} %reshape.228), calls=%async_computation.4 | async-start | bytes 147456 | tf_op jit(solution)/shard_map/all_to_all | solution.py:153

commit v13 on v12

--- a/solution.py
+++ b/solution.py
@@ -102,16 +102,18 @@
     slots = slot_table(probe_groups, groups, capacity)
     buffer, cell_marks = pack_slots(queries, probe_cells, slots, total)
     width = buffer.shape[1]
+    outbound = jnp.concatenate([buffer, cell_marks], axis=1).T.reshape(-1, groups, capacity)
     arrived_all = lax.all_to_all(
-        jnp.concatenate([buffer, cell_marks], axis=1).reshape(groups, -1),
+        jnp.transpose(outbound, (1, 0, 2)).reshape(groups, -1),
         "cell",
         split_axis=0,
         concat_axis=0,
         tiled=True,
-    ).reshape(total, -1)
-    arrived = arrived_all[:, :width]
-    arrived_cells = arrived_all[:, width:]
-    query_parts = gather_by_exchange(arrived.T, "sub")
+    ).reshape(groups, -1, capacity)
+    arrived_all = jnp.transpose(arrived_all, (1, 0, 2)).reshape(-1, total)
+    arrived_t = arrived_all[:width]
+    arrived_cells = arrived_all[width:].T
+    query_parts = gather_by_exchange(arrived_t, "sub")
     decoded = decoded_parts.reshape(-1, decoded_parts.shape[2])
     cell_ids = arrived_cells.astype(jnp.int32)
     probed = jnp.any(

time: 141 us -> 141 us (level)
    unnamed x19 -> x18, local copies, waits for them, and re-layouts: 2.84 us -> 2.73 us
where the time goes in v13:
time: 141 us; the launch traced here: 140 us
  waiting for transfers between devices  30.4 us (22%)
  blocking collectives  29.9 us (21%)
  starting transfers between devices  29.4 us (21%)
  local copies, waits for them, and re-layouts  22 us (16%)
  other arithmetic  11.9 us (8%)
  Pallas kernels  11.7 us (8%)
  matrix products  4.53 us (3%)
    all_to_all x1, blocking collectives, local(): lax.all_to_all(sendable.reshape(parts, -1, 128), 'sub', split_axis=0, con...  20 us
    pallas_call x1, Pallas kernels, decode(): pl.pallas_call(decode_kernel, grid=(blocks,), in_specs=[pl.BlockSpec((1,...  11.7 us
    all_to_all x1, waiting for transfers between devices, local(): lax.all_to_all(tables, 'sub', split_axis=0, concat_axis=0, tiled=True)  11.1 us
    all_to_all x1, starting transfers between devices, local(): lax.all_to_all(jnp.transpose(outbound, (1, 0, 2)).reshape(groups, -1), 'c...  10.1 us
    all_to_all x1, blocking collectives, local(): lax.all_to_all(copies, 'sub', split_axis=0, concat_axis=2, tiled=True)  9.87 us
    all_to_all x1, starting transfers between devices, local(): lax.all_to_all(outgoing.reshape(chunk + 2, groups, capacity), 'cell', spl...  7.83 us
    all_to_all x1, waiting for transfers between devices, local(): lax.all_to_all(outgoing.reshape(chunk + 2, groups, capacity), 'cell', spl...  7.68 us
    all_to_all x1, starting transfers between devices, local(): lax.all_to_all(tables, 'sub', split_axis=0, concat_axis=0, tiled=True)  6.76 us
  transfers between devices with their start and end apart: 4, of which 4 were waited for; matrix products, arithmetic and copies ran while one was open for 10% of the time, Pallas kernels for 8%

profile of v13, /device:TPU:1, one launch (start us, length us, event | category | flops | bytes accessed | tf_op | source)
XLA Modules:
  0.0 140.3 jit_solution(3838150422483223320)
XLA Ops:
  0.0 0.7 convert_reduce_fusion.1
  0.7 0.6 reduce-window.6
  1.6 0.7 select_reduce_fusion.1
  2.4 0.7 compare_select_fusion.1
  3.3 0.9 copy.102
  4.2 0.8 convert_element_type.51
  5.2 1.8 %scatter_custom_fusion = bf16[1024,64]{1,0:T(8,128)(2,1)S(1)} fusion(s32[512]{0:T(512)S(1)} %bitcast.127, bf16[512,64]{1,0:T(8,128)(2,1)S(1)} %bitcast.126, bf16[]{:T(256)} %constant.13.clone.1), kind=kCustom, calls=%fused_computation.21 | custom fusion | bytes 131074 | tf_op jit(solution)/shard_map/scatter | solution.py:28
  7.0 1.8 %scatter_custom_fusion.1 = bf16[1024,16]{1,0:T(8,128)(2,1)S(1)} fusion(s32[512]{0:T(512)S(1)} %bitcast.128, bf16[512,16]{1,0:T(8,128)(2,1)S(1)} %bitcast.125, bf16[]{:T(256)} %constant.17.clone.1), kind=kCustom, calls=%fused_computation.19 | custom fusion | bytes 32770 | tf_op jit(solution)/shard_map/scatter | solution.py:30
  9.0 0.2 copy.105
  9.4 0.5 broadcast.87
  9.9 1.6 %reduce.6 = bf16[16,5120]{1,0:T(8,128)(2,1)S(1)} reduce(bf16[16,1,5120]{2,1,0:T(2,128)(2,1)S(1)} %all_to_all.38, bf16[]{:T(256)} %broadcast.87), dimensions={1}, to_apply=%all_to_all.38.reduce_sub_computation | reduce | bytes 327682 | tf_op jit(solution)/shard_map/all_to_all | solution.py:106
  11.5 0.8 reshape.237
  12.3 10.1 %all-to-all-start = ((bf16[16,2,2560]{2,1,0:T(2,128)(2,1)}), bf16[16,2,2560]{2,1,0:T(2,128)(2,1)S(1)}, u32[]{:S(2)}, u32[]{:S(2)}) async-start(bf16[16,2,2560]{2,1,0:T(2,128)(2,1)} %reshape.237), calls=%async_computation | async-start | bytes 327680 | tf_op jit(solution)/shard_map/all_to_all | solution.py:106
  22.5 0.7 convert_element_type.57
  23.2 0.4 copy.110
  23.6 0.7 reshape.182
  24.5 0.9 pad_maximum_fusion.1
  25.4 6.5 %all-to-all-done = bf16[16,2,2560]{2,1,0:T(2,128)(2,1)S(1)} async-done(((bf16[16,2,2560]{2,1,0:T(2,128)(2,1)}), bf16[16,2,2560]{2,1,0:T(2,128)(2,1)S(1)}, u32[]{:S(2)}, u32[]{:S(2)}) %all-to-all-start) | async-done | bytes 163872 | tf_op jit(solution)/shard_map/all_to_all | solution.py:106
  31.9 6.8 %all-to-all-start.2 = ((bf16[16,168,128]{2,1,0:T(8,128)(2,1)}), bf16[16,168,128]{2,1,0:T(8,128)(2,1)S(1)}, u32[]{:S(2)}, u32[]{:S(2)}) async-start(bf16[16,168,128]{2,1,0:T(8,128)(2,1)} %pad_maximum_fusion.1), calls=%async_computation.2 | async-start | bytes 1376256 | tf_op jit(solution)/shard_map/all_to_all | solution.py:89
  38.8 0.9 reduce.4
  39.8 0.2 reshape.181
  40.2 0.2 broadcast_in_dim.38
  40.4 11.1 %all-to-all-done.2 = bf16[16,168,128]{2,1,0:T(8,128)(2,1)S(1)} async-done(((bf16[16,168,128]{2,1,0:T(8,128)(2,1)}), bf16[16,168,128]{2,1,0:T(8,128)(2,1)S(1)}, u32[]{:S(2)}, u32[]{:S(2)}) %all-to-all-start.2) | async-done | bytes 688160 | tf_op jit(solution)/shard_map/all_to_all | solution.py:89
  51.5 1.6 %broadcast_in_dim.39 = bf16[16,64,1024]{2,1,0:T(8,128)(2,1)} broadcast(bf16[64,1024]{1,0:T(8,128)(2,1)S(1)} %broadcast_in_dim.38), dimensions={1,2} | broadcast | bytes 2228224 | tf_op jit(solution)/shard_map/broadcast_in_dim | solution.py:64
  53.1 4.7 %all-to-all-start.1 = ((bf16[16,64,1024]{2,1,0:T(8,128)(2,1)}), bf16[16,64,1024]{2,1,0:T(8,128)(2,1)}, u32[]{:S(2)}, u32[]{:S(2)}) async-start(bf16[16,64,1024]{2,1,0:T(8,128)(2,1)} %broadcast_in_dim.39), calls=%async_computation.1 | async-start | bytes 4194304 | tf_op jit(solution)/shard_map/all_to_all | solution.py:65
  58.3 0.3 fusion.1
  59.3 1.6 %copy.114.base_ref = bf16[1024,768]{1,0:T(8,128)(2,1)} copy(bf16[1024,768]{0,1:T(8,128)(2,1)S(1)} %bitcast.102) | data formatting | bytes 3145728 | tf_op jit(solution)/shard_map/reshape | solution.py:99
  60.9 1.4 reshape.201
  62.4 1.3 reshape.229.codes_ref
  63.8 1.0 reshape.186.book_ref
  64.8 11.7 %shard_map.82 = bf16[16,64,768]{2,1,0:T(8,128)(2,1)} custom-call(s32[16,4,768]{2,1,0:T(4,128)} %reshape.229.codes_ref, bf16[64,16,256]{2,1,0:T(8,128)(2,1)} %reshape.186.book_ref, bf16[1024,768]{1,0:T(8,128)(2,1)} %copy.114.base_ref), custom_call_target="tpu_custom_call" | custom-call | tf_op jit(solution)/shard_map/pallas_call | solution.py:49
  76.5 1.9 %multiply_reduce_fusion = f32[768]{0:T(1024)S(1)} fusion(bf16[16,64,768]{2,1,0:T(8,128)(2,1)} %shard_map.82), kind=kLoop, calls=%fused_computation.8 | loop fusion | flops 2358528 | bytes 1575936 | tf_op jit(solution)/shard_map/reduce_sum | solution.py:124
  78.4 5.1 %all-to-all-done.1 = bf16[16,64,1024]{2,1,0:T(8,128)(2,1)} async-done(((bf16[16,64,1024]{2,1,0:T(8,128)(2,1)}), bf16[16,64,1024]{2,1,0:T(8,128)(2,1)}, u32[]{:S(2)}, u32[]{:S(2)}) %all-to-all-start.1) | async-done | bytes 2097184 | tf_op jit(solution)/shard_map/all_to_all | solution.py:65
  83.5 3.9 %select_reduce_fusion = (f32[1024]{0:T(1024)S(1)}, f32[1024,768,1]{0,1,2:T(8,128)S(1)}) fusion(f32[768]{0:T(1024)S(1)} %broadcast_multiply_fusion, pred[768]{0:T(1024)(128)(4,1)S(1)} %lt.43, pred[1024,32]{0,1:T(8,128)(4,1)S(1)} %fusion.1, bf16[16,64,1024]{2,1,0:T(8,128)(2,1)} %all-to-all-done.1, bf16[16,64,768]{2,1,0:T(8,128)(2,1)S(1)} %copy-done.1), kind=kOutput, calls=%fused_computation.7 | convolution fusion | flops 1614543872 | bytes 6856448 | tf_op jit(solution)/shard_map/sdq,sdr->qr/dot_general | solution.py:130
  87.4 1.1 convert_reduce_fusion
  88.5 0.6 fusion.13
  89.3 0.2 pad_maximum_fusion
  89.5 0.2 reshape.192
  89.7 20.0 %all_to_all.45 = f32[16,144,128]{2,1,0:T(8,128)S(1)} all-to-all(f32[16,144,128]{2,1,0:T(8,128)S(1)} %reshape.192), channel_id=1, replica_groups=mesh['cell'=16,'sub'=16] {'sub'}, dimensions={0} | all-to-all | bytes 2359296 | tf_op jit(solution)/shard_map/all_to_all | solution.py:146
  110.1 0.8 reshape.239
  110.8 7.8 %all-to-all-start.4 = ((f32[16,1,1152]{2,1,0:T(1,128)}), f32[16,1,1152]{2,1,0:T(1,128)S(1)}, u32[]{:S(2)}, u32[]{:S(2)}) async-start(f32[16,1,1152]{2,1,0:T(1,128)} %reshape.239), calls=%async_computation.4 | async-start | bytes 147456 | tf_op jit(solution)/shard_map/all_to_all | solution.py:155
  119.0 7.7 %all-to-all-done.4 = f32[16,1,1152]{2,1,0:T(1,128)S(1)} async-done(((f32[16,1,1152]{2,1,0:T(1,128)}), f32[16,1,1152]{2,1,0:T(1,128)S(1)}, u32[]{:S(2)}, u32[]{:S(2)}) %all-to-all-start.4) | async-done | bytes 73760 | tf_op jit(solution)/shard_map/all_to_all | solution.py:155
  126.6 0.5 broadcast.88
  127.2 0.8 reduce.7
  128.1 0.2 copy.116
  128.3 1.0 gather_fusion
  129.6 9.9 %all_to_all.46 = bf16[16,256,16]{1,2,0:T(8,128)(2,1)S(1)} all-to-all(bf16[16,256,16]{1,2,0:T(8,128)(2,1)S(1)} %broadcast_in_dim.95), channel_id=1, replica_groups=mesh['cell'=16,'sub'=16] {'sub'}, dimensions={0} | all-to-all | bytes 262144 | tf_op jit(solution)/shard_map/all_to_all | solution.py:169
  139.5 0.8 copy.119
  (72 shorter events, 4.0 us)
Async XLA Ops:
  0.0 88.5 %copy-start = (bf16[32,24,256]{2,1,0:T(8,128)(2,1)S(1)}, bf16[32,24,256]{2,1,0:T(8,128)(2,1)}, u32[]{:S(2)}) copy-start(bf16[32,24,256]{2,1,0:T(8,128)(2,1)} %param.15) | copy-start | bytes 1179652
  8.9 13.5 %copy-start.2 = (s32[32,4,384]{2,1,0:T(4,128)S(1)}, s32[32,4,384]{2,1,0:T(4,128)}, u32[]{:S(2)}) copy-start(s32[32,4,384]{2,1,0:T(4,128)} %param.13) | copy-start | bytes 589828
  12.3 11.9 %copy-start.3 = (bf16[4,16,256]{2,1,0:T(8,128)(2,1)S(1)}, bf16[4,16,256]{2,1,0:T(8,128)(2,1)}, u32[]{:S(2)}) copy-start(bf16[4,16,256]{2,1,0:T(8,128)(2,1)} %param.12) | copy-start | bytes 98308
  12.3 12.0 %copy-start.4 = (bf16[32,64]{1,0:T(8,128)(2,1)S(1)}, bf16[32,64]{1,0:T(8,128)(2,1)}, u32[]{:S(2)}) copy-start(bf16[32,64]{1,0:T(8,128)(2,1)} %param.11) | copy-start | bytes 12292
  12.3 19.6 %all-to-all-start = ((bf16[16,2,2560]{2,1,0:T(2,128)(2,1)}), bf16[16,2,2560]{2,1,0:T(2,128)(2,1)S(1)}, u32[]{:S(2)}, u32[]{:S(2)}) async-start(bf16[16,2,2560]{2,1,0:T(2,128)(2,1)} %reshape.237), calls=%async_computation | async-start | bytes 327680 | tf_op jit(solution)/shard_map/all_to_all | solution.py:106
  31.9 19.6 %all-to-all-start.2 = ((bf16[16,168,128]{2,1,0:T(8,128)(2,1)}), bf16[16,168,128]{2,1,0:T(8,128)(2,1)S(1)}, u32[]{:S(2)}, u32[]{:S(2)}) async-start(bf16[16,168,128]{2,1,0:T(8,128)(2,1)} %pad_maximum_fusion.1), calls=%async_computation.2 | async-start | bytes 1376256 | tf_op jit(solution)/shard_map/all_to_all | solution.py:89
  53.1 4.9 %copy-start.5 = (s32[32]{0:T(128)S(1)}, s32[32]{0:T(128)}, u32[]{:S(2)}) copy-start(s32[32]{0:T(128)} %param.14) | copy-start | bytes 388
  53.1 30.4 %all-to-all-start.1 = ((bf16[16,64,1024]{2,1,0:T(8,128)(2,1)}), bf16[16,64,1024]{2,1,0:T(8,128)(2,1)}, u32[]{:S(2)}, u32[]{:S(2)}) async-start(bf16[16,64,1024]{2,1,0:T(8,128)(2,1)} %broadcast_in_dim.39), calls=%async_computation.1 | async-start | bytes 4194304 | tf_op jit(solution)/shard_map/all_to_all | solution.py:65
  76.5 7.0 %copy-start.1 = (bf16[16,64,768]{2,1,0:T(8,128)(2,1)S(1)}, bf16[16,64,768]{2,1,0:T(8,128)(2,1)}, u32[]{:S(2)}) copy-start(bf16[16,64,768]{2,1,0:T(8,128)(2,1)} %shard_map.82) | copy-start | bytes 4718596
  110.8 15.8 %all-to-all-start.4 = ((f32[16,1,1152]{2,1,0:T(1,128)}), f32[16,1,1152]{2,1,0:T(1,128)S(1)}, u32[]{:S(2)}, u32[]{:S(2)}) async-start(f32[16,1,1152]{2,1,0:T(1,128)} %reshape.239), calls=%async_computation.4 | async-start | bytes 147456 | tf_op jit(solution)/shard_map/all_to_all | solution.py:155

commit v14 on v13

--- a/solution.py
+++ b/solution.py
@@ -149,13 +149,12 @@
     peaks_in = pieces[:, chunk + 1]
     peak = jnp.max(peaks_in, axis=0)
     shift = jnp.exp(peaks_in - peak[None])
-    reduced = jnp.sum(shift[:, None] * pieces[:, : chunk + 1], axis=0).reshape(chunk + 1, total)
-    peak = peak.reshape(total)
-    outgoing = jnp.concatenate([reduced, peak[None, :]], axis=0)
-    back = lax.all_to_all(
-        outgoing.reshape(chunk + 2, groups, capacity), "cell", split_axis=1, concat_axis=1, tiled=True
-    )
-    back = back.reshape(chunk + 2, total)
+    reduced = jnp.sum(shift[:, None] * pieces[:, : chunk + 1], axis=0)
+    outgoing = jnp.concatenate([reduced, peak[None]], axis=0)
+    outgoing = outgoing.reshape(chunk + 2, total).reshape(chunk + 2, groups, capacity)
+    outgoing = jnp.transpose(outgoing, (1, 0, 2)).reshape(groups, -1)
+    back = lax.all_to_all(outgoing, "cell", split_axis=0, concat_axis=0, tiled=True)
+    back = jnp.transpose(back.reshape(groups, chunk + 2, capacity), (1, 0, 2)).reshape(chunk + 2, total)
     picked = back[:, slots]
     parts_back = picked[:chunk]
     masses = picked[chunk]

time: 141 us -> 140 us (level)
  no operation moved by 1% of the time
where the time goes in v14:
time: 140 us; the launch traced here: 139 us
  waiting for transfers between devices  30.4 us (22%)
  blocking collectives  29.9 us (21%)
  starting transfers between devices  29.4 us (21%)
  local copies, waits for them, and re-layouts  21.4 us (15%)
  Pallas kernels  11.7 us (8%)
  other arithmetic  11.3 us (8%)
  matrix products  4.53 us (3%)
    all_to_all x1, blocking collectives, local(): lax.all_to_all(sendable.reshape(parts, -1, 128), 'sub', split_axis=0, con...  20 us
    pallas_call x1, Pallas kernels, decode(): pl.pallas_call(decode_kernel, grid=(blocks,), in_specs=[pl.BlockSpec((1,...  11.7 us
    all_to_all x1, waiting for transfers between devices, local(): lax.all_to_all(tables, 'sub', split_axis=0, concat_axis=0, tiled=True)  11.1 us
    all_to_all x1, starting transfers between devices, local(): lax.all_to_all(jnp.transpose(outbound, (1, 0, 2)).reshape(groups, -1), 'c...  10.1 us
    all_to_all x1, blocking collectives, local(): lax.all_to_all(copies, 'sub', split_axis=0, concat_axis=2, tiled=True)  9.87 us
    all_to_all x1, starting transfers between devices, local(): lax.all_to_all(outgoing, 'cell', split_axis=0, concat_axis=0, tiled=True)  7.83 us
    all_to_all x1, waiting for transfers between devices, local(): lax.all_to_all(outgoing, 'cell', split_axis=0, concat_axis=0, tiled=True)  7.68 us
    all_to_all x1, starting transfers between devices, local(): lax.all_to_all(tables, 'sub', split_axis=0, concat_axis=0, tiled=True)  6.76 us
  transfers between devices with their start and end apart: 4, of which 4 were waited for; matrix products, arithmetic and copies ran while one was open for 10% of the time, Pallas kernels for 8%

profile of v14, /device:TPU:1, one launch (start us, length us, event | category | flops | bytes accessed | tf_op | source)
XLA Modules:
  0.0 139.1 jit_solution(5634836484870453261)
XLA Ops:
  0.0 0.7 convert_reduce_fusion.1
  0.7 0.6 reduce-window.6
  1.6 0.7 select_reduce_fusion.1
  2.4 0.7 compare_select_fusion.1
  3.3 0.9 copy.105
  4.2 0.8 convert_element_type.51
  5.2 1.8 %scatter_custom_fusion = bf16[1024,64]{1,0:T(8,128)(2,1)S(1)} fusion(s32[512]{0:T(512)S(1)} %bitcast.125, bf16[512,64]{1,0:T(8,128)(2,1)S(1)} %bitcast.124, bf16[]{:T(256)} %constant.13.clone.1), kind=kCustom, calls=%fused_computation.21 | custom fusion | bytes 131074 | tf_op jit(solution)/shard_map/scatter | solution.py:28
  7.0 1.8 %scatter_custom_fusion.1 = bf16[1024,16]{1,0:T(8,128)(2,1)S(1)} fusion(s32[512]{0:T(512)S(1)} %bitcast.126, bf16[512,16]{1,0:T(8,128)(2,1)S(1)} %bitcast.123, bf16[]{:T(256)} %constant.17.clone.1), kind=kCustom, calls=%fused_computation.19 | custom fusion | bytes 32770 | tf_op jit(solution)/shard_map/scatter | solution.py:30
  9.0 0.2 copy.108
  9.2 0.2 all_to_all.42
  9.4 0.5 broadcast.88
  9.9 1.6 %reduce.7 = bf16[16,5120]{1,0:T(8,128)(2,1)S(1)} reduce(bf16[16,1,5120]{2,1,0:T(2,128)(2,1)S(1)} %all_to_all.42, bf16[]{:T(256)} %broadcast.88), dimensions={1}, to_apply=%all_to_all.42.reduce_sub_computation | reduce | bytes 327682 | tf_op jit(solution)/shard_map/all_to_all | solution.py:106
  11.5 0.8 reshape.244
  12.3 10.1 %all-to-all-start = ((bf16[16,2,2560]{2,1,0:T(2,128)(2,1)}), bf16[16,2,2560]{2,1,0:T(2,128)(2,1)S(1)}, u32[]{:S(2)}, u32[]{:S(2)}) async-start(bf16[16,2,2560]{2,1,0:T(2,128)(2,1)} %reshape.244), calls=%async_computation | async-start | bytes 327680 | tf_op jit(solution)/shard_map/all_to_all | solution.py:106
  22.5 0.7 convert_element_type.57
  23.2 0.4 copy.113
  23.6 0.7 reshape.187
  24.5 0.9 pad_maximum_fusion.1
  25.4 6.5 %all-to-all-done = bf16[16,2,2560]{2,1,0:T(2,128)(2,1)S(1)} async-done(((bf16[16,2,2560]{2,1,0:T(2,128)(2,1)}), bf16[16,2,2560]{2,1,0:T(2,128)(2,1)S(1)}, u32[]{:S(2)}, u32[]{:S(2)}) %all-to-all-start) | async-done | bytes 163872 | tf_op jit(solution)/shard_map/all_to_all | solution.py:106
  31.9 6.8 %all-to-all-start.2 = ((bf16[16,168,128]{2,1,0:T(8,128)(2,1)}), bf16[16,168,128]{2,1,0:T(8,128)(2,1)S(1)}, u32[]{:S(2)}, u32[]{:S(2)}) async-start(bf16[16,168,128]{2,1,0:T(8,128)(2,1)} %pad_maximum_fusion.1), calls=%async_computation.2 | async-start | bytes 1376256 | tf_op jit(solution)/shard_map/all_to_all | solution.py:89
  38.8 0.9 reduce.4
  39.8 0.2 reshape.186
  40.2 0.2 broadcast_in_dim.38
  40.4 11.1 %all-to-all-done.2 = bf16[16,168,128]{2,1,0:T(8,128)(2,1)S(1)} async-done(((bf16[16,168,128]{2,1,0:T(8,128)(2,1)}), bf16[16,168,128]{2,1,0:T(8,128)(2,1)S(1)}, u32[]{:S(2)}, u32[]{:S(2)}) %all-to-all-start.2) | async-done | bytes 688160 | tf_op jit(solution)/shard_map/all_to_all | solution.py:89
  51.5 1.6 %broadcast_in_dim.39 = bf16[16,64,1024]{2,1,0:T(8,128)(2,1)} broadcast(bf16[64,1024]{1,0:T(8,128)(2,1)S(1)} %broadcast_in_dim.38), dimensions={1,2} | broadcast | bytes 2228224 | tf_op jit(solution)/shard_map/broadcast_in_dim | solution.py:64
  53.1 4.7 %all-to-all-start.1 = ((bf16[16,64,1024]{2,1,0:T(8,128)(2,1)}), bf16[16,64,1024]{2,1,0:T(8,128)(2,1)}, u32[]{:S(2)}, u32[]{:S(2)}) async-start(bf16[16,64,1024]{2,1,0:T(8,128)(2,1)} %broadcast_in_dim.39), calls=%async_computation.1 | async-start | bytes 4194304 | tf_op jit(solution)/shard_map/all_to_all | solution.py:65
  58.3 0.3 fusion.1
  59.1 0.2 broadcast_in_dim.44
  59.3 1.6 %copy.117.base_ref = bf16[1024,768]{1,0:T(8,128)(2,1)} copy(bf16[1024,768]{0,1:T(8,128)(2,1)S(1)} %bitcast.101) | data formatting | bytes 3145728 | tf_op jit(solution)/shard_map/reshape | solution.py:99
  60.9 1.4 %reshape.207 = s32[16,32,4,24]{3,2,1,0:T(4,128)S(1)} reshape(s32[16,3072]{1,0:T(8,128)S(1)} %slice_convert_fusion) | data formatting | bytes 393216 | tf_op jit(solution)/shard_map/reshape | solution.py:95
  62.4 1.3 reshape.235.codes_ref
  63.8 1.0 reshape.191.book_ref
  64.8 11.7 %shard_map.82 = bf16[16,64,768]{2,1,0:T(8,128)(2,1)} custom-call(s32[16,4,768]{2,1,0:T(4,128)} %reshape.235.codes_ref, bf16[64,16,256]{2,1,0:T(8,128)(2,1)} %reshape.191.book_ref, bf16[1024,768]{1,0:T(8,128)(2,1)} %copy.117.base_ref), custom_call_target="tpu_custom_call" | custom-call | tf_op jit(solution)/shard_map/pallas_call | solution.py:49
  76.5 1.9 %multiply_reduce_fusion = f32[768]{0:T(1024)S(1)} fusion(bf16[16,64,768]{2,1,0:T(8,128)(2,1)} %shard_map.82), kind=kLoop, calls=%fused_computation.8 | loop fusion | flops 2358528 | bytes 1575936 | tf_op jit(solution)/shard_map/reduce_sum | solution.py:124
  78.4 5.1 %all-to-all-done.1 = bf16[16,64,1024]{2,1,0:T(8,128)(2,1)} async-done(((bf16[16,64,1024]{2,1,0:T(8,128)(2,1)}), bf16[16,64,1024]{2,1,0:T(8,128)(2,1)}, u32[]{:S(2)}, u32[]{:S(2)}) %all-to-all-start.1) | async-done | bytes 2097184 | tf_op jit(solution)/shard_map/all_to_all | solution.py:65
  83.5 3.9 %select_reduce_fusion = (f32[1024]{0:T(1024)S(1)}, f32[1024,768,1]{0,1,2:T(8,128)S(1)}) fusion(f32[768]{0:T(1024)S(1)} %broadcast_multiply_fusion, pred[768]{0:T(1024)(128)(4,1)S(1)} %lt.43, pred[1024,32]{0,1:T(8,128)(4,1)S(1)} %fusion.1, bf16[16,64,1024]{2,1,0:T(8,128)(2,1)} %all-to-all-done.1, bf16[16,64,768]{2,1,0:T(8,128)(2,1)S(1)} %copy-done.1), kind=kOutput, calls=%fused_computation.7 | convolution fusion | flops 1614543872 | bytes 6856448 | tf_op jit(solution)/shard_map/sdq,sdr->qr/dot_general | solution.py:130
  87.4 1.1 convert_reduce_fusion
  88.5 0.6 fusion.13
  89.3 0.2 pad_maximum_fusion
  89.5 0.2 reshape.197
  89.7 20.0 %all_to_all.50 = f32[16,144,128]{2,1,0:T(8,128)S(1)} all-to-all(f32[16,144,128]{2,1,0:T(8,128)S(1)} %reshape.197), channel_id=1, replica_groups=mesh['cell'=16,'sub'=16] {'sub'}, dimensions={0} | all-to-all | bytes 2359296 | tf_op jit(solution)/shard_map/all_to_all | solution.py:146
  110.1 0.8 all_to_all.43
  110.8 7.8 %all-to-all-start.4 = ((f32[16,1,1152]{2,1,0:T(1,128)}), f32[16,1,1152]{2,1,0:T(1,128)S(1)}, u32[]{:S(2)}, u32[]{:S(2)}) async-start(f32[16,1,1152]{2,1,0:T(1,128)} %all_to_all.43), calls=%async_computation.4 | async-start | bytes 147456 | tf_op jit(solution)/shard_map/all_to_all | solution.py:156
  119.0 7.7 %all-to-all-done.4 = f32[16,1,1152]{2,1,0:T(1,128)S(1)} async-done(((f32[16,1,1152]{2,1,0:T(1,128)}), f32[16,1,1152]{2,1,0:T(1,128)S(1)}, u32[]{:S(2)}, u32[]{:S(2)}) %all-to-all-start.4) | async-done | bytes 73760 | tf_op jit(solution)/shard_map/all_to_all | solution.py:156
  126.9 0.2 copy.120
  127.2 1.0 gather_fusion
  128.5 9.9 %all_to_all.51 = bf16[16,256,16]{1,2,0:T(8,128)(2,1)S(1)} all-to-all(bf16[16,256,16]{1,2,0:T(8,128)(2,1)S(1)} %broadcast_in_dim.96), channel_id=1, replica_groups=mesh['cell'=16,'sub'=16] {'sub'}, dimensions={0} | all-to-all | bytes 262144 | tf_op jit(solution)/shard_map/all_to_all | solution.py:168
  138.4 0.8 copy.123
  (71 shorter events, 3.8 us)
Async XLA Ops:
  0.0 88.5 %copy-start = (bf16[32,24,256]{2,1,0:T(8,128)(2,1)S(1)}, bf16[32,24,256]{2,1,0:T(8,128)(2,1)}, u32[]{:S(2)}) copy-start(bf16[32,24,256]{2,1,0:T(8,128)(2,1)} %param.15) | copy-start | bytes 1179652
  8.9 13.5 %copy-start.2 = (s32[32,4,384]{2,1,0:T(4,128)S(1)}, s32[32,4,384]{2,1,0:T(4,128)}, u32[]{:S(2)}) copy-start(s32[32,4,384]{2,1,0:T(4,128)} %param.13) | copy-start | bytes 589828
  12.3 11.9 %copy-start.3 = (bf16[4,16,256]{2,1,0:T(8,128)(2,1)S(1)}, bf16[4,16,256]{2,1,0:T(8,128)(2,1)}, u32[]{:S(2)}) copy-start(bf16[4,16,256]{2,1,0:T(8,128)(2,1)} %param.12) | copy-start | bytes 98308
  12.3 12.0 %copy-start.4 = (bf16[32,64]{1,0:T(8,128)(2,1)S(1)}, bf16[32,64]{1,0:T(8,128)(2,1)}, u32[]{:S(2)}) copy-start(bf16[32,64]{1,0:T(8,128)(2,1)} %param.11) | copy-start | bytes 12292
  12.3 19.6 %all-to-all-start = ((bf16[16,2,2560]{2,1,0:T(2,128)(2,1)}), bf16[16,2,2560]{2,1,0:T(2,128)(2,1)S(1)}, u32[]{:S(2)}, u32[]{:S(2)}) async-start(bf16[16,2,2560]{2,1,0:T(2,128)(2,1)} %reshape.244), calls=%async_computation | async-start | bytes 327680 | tf_op jit(solution)/shard_map/all_to_all | solution.py:106
  31.9 19.6 %all-to-all-start.2 = ((bf16[16,168,128]{2,1,0:T(8,128)(2,1)}), bf16[16,168,128]{2,1,0:T(8,128)(2,1)S(1)}, u32[]{:S(2)}, u32[]{:S(2)}) async-start(bf16[16,168,128]{2,1,0:T(8,128)(2,1)} %pad_maximum_fusion.1), calls=%async_computation.2 | async-start | bytes 1376256 | tf_op jit(solution)/shard_map/all_to_all | solution.py:89
  53.1 4.9 %copy-start.5 = (s32[32]{0:T(128)S(1)}, s32[32]{0:T(128)}, u32[]{:S(2)}) copy-start(s32[32]{0:T(128)} %param.14) | copy-start | bytes 388
  53.1 30.4 %all-to-all-start.1 = ((bf16[16,64,1024]{2,1,0:T(8,128)(2,1)}), bf16[16,64,1024]{2,1,0:T(8,128)(2,1)}, u32[]{:S(2)}, u32[]{:S(2)}) async-start(bf16[16,64,1024]{2,1,0:T(8,128)(2,1)} %broadcast_in_dim.39), calls=%async_computation.1 | async-start | bytes 4194304 | tf_op jit(solution)/shard_map/all_to_all | solution.py:65
  76.5 7.0 %copy-start.1 = (bf16[16,64,768]{2,1,0:T(8,128)(2,1)S(1)}, bf16[16,64,768]{2,1,0:T(8,128)(2,1)}, u32[]{:S(2)}) copy-start(bf16[16,64,768]{2,1,0:T(8,128)(2,1)} %shard_map.82) | copy-start | bytes 4718596
  110.8 15.8 %all-to-all-start.4 = ((f32[16,1,1152]{2,1,0:T(1,128)}), f32[16,1,1152]{2,1,0:T(1,128)S(1)}, u32[]{:S(2)}, u32[]{:S(2)}) async-start(f32[16,1,1152]{2,1,0:T(1,128)} %all_to_all.43), calls=%async_computation.4 | async-start | bytes 147456 | tf_op jit(solution)/shard_map/all_to_all | solution.py:156

commit v15 on v14

--- a/solution.py
+++ b/solution.py
@@ -77,7 +77,8 @@
     cell_count, sub_count, row_count = codes.shape
     rows_part = row_count // parts
     own_codes = codes.reshape(cell_count, sub_count, parts, rows_part)
-    own_codes = jnp.transpose(own_codes, (2, 0, 1, 3)).astype(jnp.bfloat16).reshape(parts, -1, 128)
+    own_codes = lax.optimization_barrier(jnp.transpose(own_codes, (2, 0, 1, 3)).reshape(parts, -1, 128))
+    own_codes = own_codes.astype(jnp.bfloat16)
     tables = jnp.concatenate(
         [
             own_codes,
@@ -104,7 +105,7 @@
     width = buffer.shape[1]
     outbound = jnp.concatenate([buffer, cell_marks], axis=1).T.reshape(-1, groups, capacity)
     arrived_all = lax.all_to_all(
-        jnp.transpose(outbound, (1, 0, 2)).reshape(groups, -1),
+        jnp.transpose(outbound, (1, 0, 2)).reshape(groups, 2, -1),
         "cell",
         split_axis=0,
         concat_axis=0,

time: 140 us -> 138 us (0.986)
  other arithmetic: 11.3 us -> 8.75 us
    all_to_all x2 -> x0, other arithmetic: 2.52 us -> none  [local(): lax.all_to_all(jnp.transpose(outbound, (1, 0, 2)).reshape(groups, -1), 'c...]
    reshape x2 -> x4, local copies, waits for them, and re-layouts: 0.66 us -> 2.75 us  [the longest x1 1.21 us: local(): jnp.transpose(own_codes, (2, 0, 1, 3)).reshape(parts, -1, 128)]
  transfers between devices with their start and end apart: 4 -> 4, of which waited for: 4 -> 4; matrix products, arithmetic and copies ran while one was open for 10% -> 10% of each run, Pallas kernels for 8% -> 9%
where the time goes in v15:
time: 138 us; the launch traced here: 137 us
  waiting for transfers between devices  30.7 us (22%)
  blocking collectives  29.9 us (22%)
  starting transfers between devices  29.3 us (21%)
  local copies, waits for them, and re-layouts  21.6 us (16%)
  Pallas kernels  11.7 us (8%)
  other arithmetic  8.75 us (6%)
  matrix products  4.53 us (3%)
    all_to_all x1, blocking collectives, local(): lax.all_to_all(sendable.reshape(parts, -1, 128), 'sub', split_axis=0, con...  20 us
    all_to_all x1, waiting for transfers between devices, local(): lax.all_to_all(tables, 'sub', split_axis=0, concat_axis=0, tiled=True)  12.1 us
    pallas_call x1, Pallas kernels, decode(): pl.pallas_call(decode_kernel, grid=(blocks,), in_specs=[pl.BlockSpec((1,...  11.7 us
    all_to_all x1, starting transfers between devices, local(): lax.all_to_all(jnp.transpose(outbound, (1, 0, 2)).reshape(groups, 2, -1),...  9.97 us
    all_to_all x1, blocking collectives, local(): lax.all_to_all(copies, 'sub', split_axis=0, concat_axis=2, tiled=True)  9.87 us
    all_to_all x1, starting transfers between devices, local(): lax.all_to_all(outgoing, 'cell', split_axis=0, concat_axis=0, tiled=True)  7.83 us
    all_to_all x1, waiting for transfers between devices, local(): lax.all_to_all(outgoing, 'cell', split_axis=0, concat_axis=0, tiled=True)  7.68 us
    all_to_all x1, starting transfers between devices, local(): lax.all_to_all(tables, 'sub', split_axis=0, concat_axis=0, tiled=True)  6.76 us
  transfers between devices with their start and end apart: 4, of which 4 were waited for; matrix products, arithmetic and copies ran while one was open for 10% of the time, Pallas kernels for 9%

profile of v15, /device:TPU:1, one launch (start us, length us, event | category | flops | bytes accessed | tf_op | source)
XLA Modules:
  0.0 136.8 jit_solution(5528740676028074004)
XLA Ops:
  0.0 0.7 convert_reduce_fusion.1
  0.7 0.6 reduce-window.6
  1.3 0.2 slice_reduce_fusion.1
  1.6 0.7 select_reduce_fusion.1
  2.4 0.7 compare_select_fusion.1
  3.3 0.9 copy.104
  4.2 0.8 convert_element_type.45
  5.2 1.8 %scatter_custom_fusion = bf16[1024,64]{1,0:T(8,128)(2,1)S(1)} fusion(s32[512]{0:T(512)S(1)} %bitcast.125, bf16[512,64]{1,0:T(8,128)(2,1)S(1)} %bitcast.124, bf16[]{:T(256)} %constant.13.clone.1), kind=kCustom, calls=%fused_computation.21 | custom fusion | bytes 131074 | tf_op jit(solution)/shard_map/scatter | solution.py:28
  7.1 1.8 %scatter_custom_fusion.1 = bf16[1024,16]{1,0:T(8,128)(2,1)S(1)} fusion(s32[512]{0:T(512)S(1)} %bitcast.126, bf16[512,16]{1,0:T(8,128)(2,1)S(1)} %bitcast.123, bf16[]{:T(256)} %constant.17.clone.1), kind=kCustom, calls=%fused_computation.19 | custom fusion | bytes 32770 | tf_op jit(solution)/shard_map/scatter | solution.py:30
  9.1 0.2 copy.107
  9.3 0.9 reshape.185
  10.2 10.0 %all-to-all-start = ((bf16[16,2,2560]{2,1,0:T(2,128)(2,1)}), bf16[16,2,2560]{2,1,0:T(2,128)(2,1)S(1)}, u32[]{:S(2)}, u32[]{:S(2)}) async-start(bf16[16,2,2560]{2,1,0:T(2,128)(2,1)} %reshape.185), calls=%async_computation | async-start | bytes 327680 | tf_op jit(solution)/shard_map/all_to_all | solution.py:107
  20.2 0.6 reshape.187
  20.8 0.7 copy.111
  21.5 1.2 reshape.188
  23.0 0.9 pad_maximum_fusion.1
  23.9 5.8 %all-to-all-done = bf16[16,2,2560]{2,1,0:T(2,128)(2,1)S(1)} async-done(((bf16[16,2,2560]{2,1,0:T(2,128)(2,1)}), bf16[16,2,2560]{2,1,0:T(2,128)(2,1)S(1)}, u32[]{:S(2)}, u32[]{:S(2)}) %all-to-all-start) | async-done | bytes 163872 | tf_op jit(solution)/shard_map/all_to_all | solution.py:107
  29.7 6.8 %all-to-all-start.2 = ((bf16[16,168,128]{2,1,0:T(8,128)(2,1)}), bf16[16,168,128]{2,1,0:T(8,128)(2,1)S(1)}, u32[]{:S(2)}, u32[]{:S(2)}) async-start(bf16[16,168,128]{2,1,0:T(8,128)(2,1)} %pad_maximum_fusion.1), calls=%async_computation.2 | async-start | bytes 1376256 | tf_op jit(solution)/shard_map/all_to_all | solution.py:90
  36.4 0.2 reshape.186
  36.7 0.2 copy.109
  36.9 0.2 broadcast_in_dim.38
  37.1 12.1 %all-to-all-done.2 = bf16[16,168,128]{2,1,0:T(8,128)(2,1)S(1)} async-done(((bf16[16,168,128]{2,1,0:T(8,128)(2,1)}), bf16[16,168,128]{2,1,0:T(8,128)(2,1)S(1)}, u32[]{:S(2)}, u32[]{:S(2)}) %all-to-all-start.2) | async-done | bytes 688160 | tf_op jit(solution)/shard_map/all_to_all | solution.py:90
  49.2 1.6 %broadcast_in_dim.39 = bf16[16,64,1024]{2,1,0:T(8,128)(2,1)} broadcast(bf16[64,1024]{1,0:T(8,128)(2,1)S(1)} %broadcast_in_dim.38), dimensions={1,2} | broadcast | bytes 2228224 | tf_op jit(solution)/shard_map/broadcast_in_dim | solution.py:64
  50.8 4.7 %all-to-all-start.1 = ((bf16[16,64,1024]{2,1,0:T(8,128)(2,1)}), bf16[16,64,1024]{2,1,0:T(8,128)(2,1)}, u32[]{:S(2)}, u32[]{:S(2)}) async-start(bf16[16,64,1024]{2,1,0:T(8,128)(2,1)} %broadcast_in_dim.39), calls=%async_computation.1 | async-start | bytes 4194304 | tf_op jit(solution)/shard_map/all_to_all | solution.py:65
  56.0 0.3 fusion.1
  56.4 0.2 reshape.193
  56.8 0.2 broadcast_in_dim.44
  57.0 1.6 %copy.115.base_ref = bf16[1024,768]{1,0:T(8,128)(2,1)} copy(bf16[1024,768]{0,1:T(8,128)(2,1)S(1)} %bitcast.101) | data formatting | bytes 3145728 | tf_op jit(solution)/shard_map/reshape | solution.py:100
  58.6 1.4 %reshape.208 = s32[16,32,4,24]{3,2,1,0:T(4,128)S(1)} reshape(s32[16,3072]{1,0:T(8,128)S(1)} %slice_convert_fusion) | data formatting | bytes 393216 | tf_op jit(solution)/shard_map/reshape | solution.py:96
  60.2 1.3 reshape.236.codes_ref
  61.5 1.0 reshape.192.book_ref
  62.5 11.7 %shard_map.82 = bf16[16,64,768]{2,1,0:T(8,128)(2,1)} custom-call(s32[16,4,768]{2,1,0:T(4,128)} %reshape.236.codes_ref, bf16[64,16,256]{2,1,0:T(8,128)(2,1)} %reshape.192.book_ref, bf16[1024,768]{1,0:T(8,128)(2,1)} %copy.115.base_ref), custom_call_target="tpu_custom_call" | custom-call | tf_op jit(solution)/shard_map/pallas_call | solution.py:49
  74.2 1.9 %multiply_reduce_fusion = f32[768]{0:T(1024)S(1)} fusion(bf16[16,64,768]{2,1,0:T(8,128)(2,1)} %shard_map.82), kind=kLoop, calls=%fused_computation.8 | loop fusion | flops 2358528 | bytes 1575936 | tf_op jit(solution)/shard_map/reduce_sum | solution.py:125
  76.1 5.1 %all-to-all-done.1 = bf16[16,64,1024]{2,1,0:T(8,128)(2,1)} async-done(((bf16[16,64,1024]{2,1,0:T(8,128)(2,1)}), bf16[16,64,1024]{2,1,0:T(8,128)(2,1)}, u32[]{:S(2)}, u32[]{:S(2)}) %all-to-all-start.1) | async-done | bytes 2097184 | tf_op jit(solution)/shard_map/all_to_all | solution.py:65
  81.2 3.9 %select_reduce_fusion = (f32[1024]{0:T(1024)S(1)}, f32[1024,768,1]{0,1,2:T(8,128)S(1)}) fusion(f32[768]{0:T(1024)S(1)} %broadcast_multiply_fusion, pred[768]{0:T(1024)(128)(4,1)S(1)} %lt.43, pred[1024,32]{0,1:T(8,128)(4,1)S(1)} %fusion.1, bf16[16,64,1024]{2,1,0:T(8,128)(2,1)} %all-to-all-done.1, bf16[16,64,768]{2,1,0:T(8,128)(2,1)S(1)} %copy-done.1), kind=kOutput, calls=%fused_computation.7 | convolution fusion | flops 1614543872 | bytes 6856448 | tf_op jit(solution)/shard_map/sdq,sdr->qr/dot_general | solution.py:131
  85.1 1.1 convert_reduce_fusion
  86.3 0.6 fusion.13
  87.0 0.2 pad_maximum_fusion
  87.2 0.2 reshape.198
  87.4 20.0 %all_to_all.45 = f32[16,144,128]{2,1,0:T(8,128)S(1)} all-to-all(f32[16,144,128]{2,1,0:T(8,128)S(1)} %reshape.198), channel_id=1, replica_groups=mesh['cell'=16,'sub'=16] {'sub'}, dimensions={0} | all-to-all | bytes 2359296 | tf_op jit(solution)/shard_map/all_to_all | solution.py:147
  107.8 0.8 all_to_all.38
  108.6 7.8 %all-to-all-start.4 = ((f32[16,1,1152]{2,1,0:T(1,128)}), f32[16,1,1152]{2,1,0:T(1,128)S(1)}, u32[]{:S(2)}, u32[]{:S(2)}) async-start(f32[16,1,1152]{2,1,0:T(1,128)} %all_to_all.38), calls=%async_computation.4 | async-start | bytes 147456 | tf_op jit(solution)/shard_map/all_to_all | solution.py:157
  116.7 7.7 %all-to-all-done.4 = f32[16,1,1152]{2,1,0:T(1,128)S(1)} async-done(((f32[16,1,1152]{2,1,0:T(1,128)}), f32[16,1,1152]{2,1,0:T(1,128)S(1)}, u32[]{:S(2)}, u32[]{:S(2)}) %all-to-all-start.4) | async-done | bytes 73760 | tf_op jit(solution)/shard_map/all_to_all | solution.py:157
  124.4 0.2 reduce.4
  124.6 0.2 copy.118
  124.9 1.0 gather_fusion
  126.2 9.9 %all_to_all.46 = bf16[16,256,16]{1,2,0:T(8,128)(2,1)S(1)} all-to-all(bf16[16,256,16]{1,2,0:T(8,128)(2,1)S(1)} %broadcast_in_dim.96), channel_id=1, replica_groups=mesh['cell'=16,'sub'=16] {'sub'}, dimensions={0} | all-to-all | bytes 262144 | tf_op jit(solution)/shard_map/all_to_all | solution.py:169
  136.1 0.8 copy.121
  (66 shorter events, 3.0 us)
Async XLA Ops:
  0.0 86.3 %copy-start = (bf16[32,24,256]{2,1,0:T(8,128)(2,1)S(1)}, bf16[32,24,256]{2,1,0:T(8,128)(2,1)}, u32[]{:S(2)}) copy-start(bf16[32,24,256]{2,1,0:T(8,128)(2,1)} %param.15) | copy-start | bytes 1179652
  4.2 15.9 %copy-start.2 = (s32[32,4,384]{2,1,0:T(4,128)S(1)}, s32[32,4,384]{2,1,0:T(4,128)}, u32[]{:S(2)}) copy-start(s32[32,4,384]{2,1,0:T(4,128)} %param.13) | copy-start | bytes 589828
  10.2 19.5 %all-to-all-start = ((bf16[16,2,2560]{2,1,0:T(2,128)(2,1)}), bf16[16,2,2560]{2,1,0:T(2,128)(2,1)S(1)}, u32[]{:S(2)}, u32[]{:S(2)}) async-start(bf16[16,2,2560]{2,1,0:T(2,128)(2,1)} %reshape.185), calls=%async_computation | async-start | bytes 327680 | tf_op jit(solution)/shard_map/all_to_all | solution.py:107
  20.8 1.9 %copy-start.3 = (bf16[4,16,256]{2,1,0:T(8,128)(2,1)S(1)}, bf16[4,16,256]{2,1,0:T(8,128)(2,1)}, u32[]{:S(2)}) copy-start(bf16[4,16,256]{2,1,0:T(8,128)(2,1)} %param.12) | copy-start | bytes 98308
  20.8 2.0 %copy-start.4 = (bf16[32,64]{1,0:T(8,128)(2,1)S(1)}, bf16[32,64]{1,0:T(8,128)(2,1)}, u32[]{:S(2)}) copy-start(bf16[32,64]{1,0:T(8,128)(2,1)} %param.11) | copy-start | bytes 12292
  29.7 19.6 %all-to-all-start.2 = ((bf16[16,168,128]{2,1,0:T(8,128)(2,1)}), bf16[16,168,128]{2,1,0:T(8,128)(2,1)S(1)}, u32[]{:S(2)}, u32[]{:S(2)}) async-start(bf16[16,168,128]{2,1,0:T(8,128)(2,1)} %pad_maximum_fusion.1), calls=%async_computation.2 | async-start | bytes 1376256 | tf_op jit(solution)/shard_map/all_to_all | solution.py:90
  50.8 4.9 %copy-start.5 = (s32[32]{0:T(128)S(1)}, s32[32]{0:T(128)}, u32[]{:S(2)}) copy-start(s32[32]{0:T(128)} %param.14) | copy-start | bytes 388
  50.8 30.4 %all-to-all-start.1 = ((bf16[16,64,1024]{2,1,0:T(8,128)(2,1)}), bf16[16,64,1024]{2,1,0:T(8,128)(2,1)}, u32[]{:S(2)}, u32[]{:S(2)}) async-start(bf16[16,64,1024]{2,1,0:T(8,128)(2,1)} %broadcast_in_dim.39), calls=%async_computation.1 | async-start | bytes 4194304 | tf_op jit(solution)/shard_map/all_to_all | solution.py:65
  74.2 7.0 %copy-start.1 = (bf16[16,64,768]{2,1,0:T(8,128)(2,1)S(1)}, bf16[16,64,768]{2,1,0:T(8,128)(2,1)}, u32[]{:S(2)}) copy-start(bf16[16,64,768]{2,1,0:T(8,128)(2,1)} %shard_map.82) | copy-start | bytes 4718596
  108.6 15.8 %all-to-all-start.4 = ((f32[16,1,1152]{2,1,0:T(1,128)}), f32[16,1,1152]{2,1,0:T(1,128)S(1)}, u32[]{:S(2)}, u32[]{:S(2)}) async-start(f32[16,1,1152]{2,1,0:T(1,128)} %all_to_all.38), calls=%async_computation.4 | async-start | bytes 147456 | tf_op jit(solution)/shard_map/all_to_all | solution.py:157

commit v16 on v14

--- a/solution.py
+++ b/solution.py
@@ -104,7 +104,7 @@
     width = buffer.shape[1]
     outbound = jnp.concatenate([buffer, cell_marks], axis=1).T.reshape(-1, groups, capacity)
     arrived_all = lax.all_to_all(
-        jnp.transpose(outbound, (1, 0, 2)).reshape(groups, -1),
+        jnp.transpose(outbound, (1, 0, 2)).reshape(groups, 2, -1),
         "cell",
         split_axis=0,
         concat_axis=0,
@@ -164,9 +164,10 @@
     upper = jnp.sum(scale[None, :, :] * parts_back, axis=2)
     lower = jnp.sum(scale * masses, axis=1)
     pooled = (upper / lower[None, :]).T.astype(jnp.bfloat16)
-    copies = jnp.broadcast_to(pooled[None], (parts,) + pooled.shape)
-    gathered = lax.all_to_all(copies, "sub", split_axis=0, concat_axis=2, tiled=True)
-    return gathered.reshape(pooled.shape[0], pw)
+    copies = jnp.broadcast_to(pooled.reshape(1, 2, -1), (parts, 2, pooled.size // 2))
+    gathered = lax.all_to_all(copies, "sub", split_axis=0, concat_axis=0, tiled=True)
+    gathered = gathered.reshape((parts,) + pooled.shape)
+    return jnp.transpose(gathered, (1, 0, 2)).reshape(pooled.shape[0], pw)
 
 
 def solution(mesh):

time: 140 us -> 139 us (level)
  other arithmetic: 11.3 us -> 8.77 us
    all_to_all x2 -> x0, other arithmetic: 2.52 us -> none  [local(): lax.all_to_all(jnp.transpose(outbound, (1, 0, 2)).reshape(groups, -1), 'c...]
    reshape x2 -> x4, local copies, waits for them, and re-layouts: 0.76 us -> 2.36 us  [the longest x1 0.89 us: local(): jnp.transpose(outbound, (1, 0, 2)).reshape(groups, 2, -1)]
  transfers between devices with their start and end apart: 4 -> 4, of which waited for: 4 -> 4; matrix products, arithmetic and copies ran while one was open for 10% -> 9% of each run, Pallas kernels for 8% -> 8%
where the time goes in v16:
time: 139 us; the launch traced here: 138 us
  waiting for transfers between devices  31.5 us (23%)
  blocking collectives  29.9 us (22%)
  starting transfers between devices  29.4 us (21%)
  local copies, waits for them, and re-layouts  22.1 us (16%)
  Pallas kernels  11.7 us (8%)
  other arithmetic  8.77 us (6%)
  matrix products  4.53 us (3%)
    all_to_all x1, blocking collectives, local(): lax.all_to_all(sendable.reshape(parts, -1, 128), 'sub', split_axis=0, con...  20 us
    all_to_all x1, waiting for transfers between devices, local(): lax.all_to_all(tables, 'sub', split_axis=0, concat_axis=0, tiled=True)  12.1 us
    pallas_call x1, Pallas kernels, decode(): pl.pallas_call(decode_kernel, grid=(blocks,), in_specs=[pl.BlockSpec((1,...  11.7 us
    all_to_all x1, starting transfers between devices, local(): lax.all_to_all(jnp.transpose(outbound, (1, 0, 2)).reshape(groups, 2, -1),...  10.1 us
    all_to_all x1, blocking collectives, local(): lax.all_to_all(copies, 'sub', split_axis=0, concat_axis=0, tiled=True)  9.87 us
    all_to_all x1, starting transfers between devices, local(): lax.all_to_all(outgoing, 'cell', split_axis=0, concat_axis=0, tiled=True)  7.83 us
    all_to_all x1, waiting for transfers between devices, local(): lax.all_to_all(outgoing, 'cell', split_axis=0, concat_axis=0, tiled=True)  7.68 us
    all_to_all x1, starting transfers between devices, local(): lax.all_to_all(tables, 'sub', split_axis=0, concat_axis=0, tiled=True)  6.76 us
  transfers between devices with their start and end apart: 4, of which 4 were waited for; matrix products, arithmetic and copies ran while one was open for 9% of the time, Pallas kernels for 8%

profile of v16, /device:TPU:1, one launch (start us, length us, event | category | flops | bytes accessed | tf_op | source)
XLA Modules:
  0.0 138.3 jit_solution(13368643152281708461)
XLA Ops:
  0.0 0.7 convert_reduce_fusion.1
  0.7 0.6 reduce-window.6
  1.3 0.2 slice_reduce_fusion.1
  1.6 0.7 select_reduce_fusion.1
  2.4 0.7 compare_select_fusion.1
  3.3 0.9 copy.109
  4.2 0.8 convert_element_type.51
  5.2 1.8 %scatter_custom_fusion = bf16[1024,64]{1,0:T(8,128)(2,1)S(1)} fusion(s32[512]{0:T(512)S(1)} %bitcast.123, bf16[512,64]{1,0:T(8,128)(2,1)S(1)} %bitcast.122, bf16[]{:T(256)} %constant.13.clone.1), kind=kCustom, calls=%fused_computation.21 | custom fusion | bytes 131074 | tf_op jit(solution)/shard_map/scatter | solution.py:28
  7.1 1.8 %scatter_custom_fusion.1 = bf16[1024,16]{1,0:T(8,128)(2,1)S(1)} fusion(s32[512]{0:T(512)S(1)} %bitcast.124, bf16[512,16]{1,0:T(8,128)(2,1)S(1)} %bitcast.121, bf16[]{:T(256)} %constant.17.clone.1), kind=kCustom, calls=%fused_computation.19 | custom fusion | bytes 32770 | tf_op jit(solution)/shard_map/scatter | solution.py:30
  9.1 0.2 copy.112
  9.3 0.9 reshape.187
  10.2 10.1 %all-to-all-start = ((bf16[16,2,2560]{2,1,0:T(2,128)(2,1)}), bf16[16,2,2560]{2,1,0:T(2,128)(2,1)S(1)}, u32[]{:S(2)}, u32[]{:S(2)}) async-start(bf16[16,2,2560]{2,1,0:T(2,128)(2,1)} %reshape.187), calls=%async_computation | async-start | bytes 327680 | tf_op jit(solution)/shard_map/all_to_all | solution.py:106
  20.3 0.7 convert_element_type.57
  21.0 0.4 copy.116
  21.4 0.7 reshape.189
  22.3 0.9 pad_maximum_fusion.1
  23.3 6.5 %all-to-all-done = bf16[16,2,2560]{2,1,0:T(2,128)(2,1)S(1)} async-done(((bf16[16,2,2560]{2,1,0:T(2,128)(2,1)}), bf16[16,2,2560]{2,1,0:T(2,128)(2,1)S(1)}, u32[]{:S(2)}, u32[]{:S(2)}) %all-to-all-start) | async-done | bytes 163872 | tf_op jit(solution)/shard_map/all_to_all | solution.py:106
  29.8 6.8 %all-to-all-start.2 = ((bf16[16,168,128]{2,1,0:T(8,128)(2,1)}), bf16[16,168,128]{2,1,0:T(8,128)(2,1)S(1)}, u32[]{:S(2)}, u32[]{:S(2)}) async-start(bf16[16,168,128]{2,1,0:T(8,128)(2,1)} %pad_maximum_fusion.1), calls=%async_computation.2 | async-start | bytes 1376256 | tf_op jit(solution)/shard_map/all_to_all | solution.py:89
  36.6 0.2 reshape.188
  36.8 0.2 copy.114
  37.0 0.2 broadcast_in_dim.40
  37.2 12.1 %all-to-all-done.2 = bf16[16,168,128]{2,1,0:T(8,128)(2,1)S(1)} async-done(((bf16[16,168,128]{2,1,0:T(8,128)(2,1)}), bf16[16,168,128]{2,1,0:T(8,128)(2,1)S(1)}, u32[]{:S(2)}, u32[]{:S(2)}) %all-to-all-start.2) | async-done | bytes 688160 | tf_op jit(solution)/shard_map/all_to_all | solution.py:89
  49.4 1.6 %broadcast_in_dim.41 = bf16[16,64,1024]{2,1,0:T(8,128)(2,1)} broadcast(bf16[64,1024]{1,0:T(8,128)(2,1)S(1)} %broadcast_in_dim.40), dimensions={1,2} | broadcast | bytes 2228224 | tf_op jit(solution)/shard_map/broadcast_in_dim | solution.py:64
  50.9 4.7 %all-to-all-start.1 = ((bf16[16,64,1024]{2,1,0:T(8,128)(2,1)}), bf16[16,64,1024]{2,1,0:T(8,128)(2,1)}, u32[]{:S(2)}, u32[]{:S(2)}) async-start(bf16[16,64,1024]{2,1,0:T(8,128)(2,1)} %broadcast_in_dim.41), calls=%async_computation.1 | async-start | bytes 4194304 | tf_op jit(solution)/shard_map/all_to_all | solution.py:65
  56.1 0.3 fusion.1
  56.9 0.2 broadcast_in_dim.46
  57.1 1.6 %copy.120.base_ref = bf16[1024,768]{1,0:T(8,128)(2,1)} copy(bf16[1024,768]{0,1:T(8,128)(2,1)S(1)} %bitcast.98) | data formatting | bytes 3145728 | tf_op jit(solution)/shard_map/reshape | solution.py:99
  58.8 1.4 %reshape.210 = s32[16,32,4,24]{3,2,1,0:T(4,128)S(1)} reshape(s32[16,3072]{1,0:T(8,128)S(1)} %slice_convert_fusion) | data formatting | bytes 393216 | tf_op jit(solution)/shard_map/reshape | solution.py:95
  60.3 1.3 reshape.238.codes_ref
  61.6 1.0 reshape.193.book_ref
  62.6 11.7 %shard_map.82 = bf16[16,64,768]{2,1,0:T(8,128)(2,1)} custom-call(s32[16,4,768]{2,1,0:T(4,128)} %reshape.238.codes_ref, bf16[64,16,256]{2,1,0:T(8,128)(2,1)} %reshape.193.book_ref, bf16[1024,768]{1,0:T(8,128)(2,1)} %copy.120.base_ref), custom_call_target="tpu_custom_call" | custom-call | tf_op jit(solution)/shard_map/pallas_call | solution.py:49
  74.3 1.9 %multiply_reduce_fusion = f32[768]{0:T(1024)S(1)} fusion(bf16[16,64,768]{2,1,0:T(8,128)(2,1)} %shard_map.82), kind=kLoop, calls=%fused_computation.8 | loop fusion | flops 2358528 | bytes 1575936 | tf_op jit(solution)/shard_map/reduce_sum | solution.py:124
  76.2 5.1 %all-to-all-done.1 = bf16[16,64,1024]{2,1,0:T(8,128)(2,1)} async-done(((bf16[16,64,1024]{2,1,0:T(8,128)(2,1)}), bf16[16,64,1024]{2,1,0:T(8,128)(2,1)}, u32[]{:S(2)}, u32[]{:S(2)}) %all-to-all-start.1) | async-done | bytes 2097184 | tf_op jit(solution)/shard_map/all_to_all | solution.py:65
  81.3 3.9 %select_reduce_fusion = (f32[1024]{0:T(1024)S(1)}, f32[1024,768,1]{0,1,2:T(8,128)S(1)}) fusion(f32[768]{0:T(1024)S(1)} %broadcast_multiply_fusion, pred[768]{0:T(1024)(128)(4,1)S(1)} %lt.43, pred[1024,32]{0,1:T(8,128)(4,1)S(1)} %fusion.1, bf16[16,64,1024]{2,1,0:T(8,128)(2,1)} %all-to-all-done.1, bf16[16,64,768]{2,1,0:T(8,128)(2,1)S(1)} %copy-done.1), kind=kOutput, calls=%fused_computation.7 | convolution fusion | flops 1614543872 | bytes 6856448 | tf_op jit(solution)/shard_map/sdq,sdr->qr/dot_general | solution.py:130
  85.3 1.1 convert_reduce_fusion
  86.4 0.6 fusion.13
  87.1 0.2 pad_maximum_fusion
  87.4 0.2 reshape.199
  87.6 20.0 %all_to_all.35 = f32[16,144,128]{2,1,0:T(8,128)S(1)} all-to-all(f32[16,144,128]{2,1,0:T(8,128)S(1)} %reshape.199), channel_id=1, replica_groups=mesh['cell'=16,'sub'=16] {'sub'}, dimensions={0} | all-to-all | bytes 2359296 | tf_op jit(solution)/shard_map/all_to_all | solution.py:146
  107.9 0.8 all_to_all.28
  108.7 7.8 %all-to-all-start.4 = ((f32[16,1,1152]{2,1,0:T(1,128)}), f32[16,1,1152]{2,1,0:T(1,128)S(1)}, u32[]{:S(2)}, u32[]{:S(2)}) async-start(f32[16,1,1152]{2,1,0:T(1,128)} %all_to_all.28), calls=%async_computation.4 | async-start | bytes 147456 | tf_op jit(solution)/shard_map/all_to_all | solution.py:156
  116.8 7.7 %all-to-all-done.4 = f32[16,1,1152]{2,1,0:T(1,128)S(1)} async-done(((f32[16,1,1152]{2,1,0:T(1,128)}), f32[16,1,1152]{2,1,0:T(1,128)S(1)}, u32[]{:S(2)}, u32[]{:S(2)}) %all-to-all-start.4) | async-done | bytes 73760 | tf_op jit(solution)/shard_map/all_to_all | solution.py:156
  124.8 0.2 copy.123
  125.0 1.0 gather_fusion
  126.7 9.9 %all_to_all.36 = bf16[16,2,2048]{2,1,0:T(2,128)(2,1)S(1)} all-to-all(bf16[16,2,2048]{2,1,0:T(2,128)(2,1)S(1)} %broadcast_in_dim.98), channel_id=1, replica_groups=mesh['cell'=16,'sub'=16] {'sub'}, dimensions={0} | all-to-all | bytes 262144 | tf_op jit(solution)/shard_map/all_to_all | solution.py:168
  136.5 0.7 reshape.203
  137.2 0.3 copy.127
  137.5 0.8 copy.128
  (70 shorter events, 3.6 us)
Async XLA Ops:
  0.0 86.4 %copy-start = (bf16[32,24,256]{2,1,0:T(8,128)(2,1)S(1)}, bf16[32,24,256]{2,1,0:T(8,128)(2,1)}, u32[]{:S(2)}) copy-start(bf16[32,24,256]{2,1,0:T(8,128)(2,1)} %param.15) | copy-start | bytes 1179652
  4.2 16.1 %copy-start.2 = (s32[32,4,384]{2,1,0:T(4,128)S(1)}, s32[32,4,384]{2,1,0:T(4,128)}, u32[]{:S(2)}) copy-start(s32[32,4,384]{2,1,0:T(4,128)} %param.13) | copy-start | bytes 589828
  10.2 11.9 %copy-start.3 = (bf16[4,16,256]{2,1,0:T(8,128)(2,1)S(1)}, bf16[4,16,256]{2,1,0:T(8,128)(2,1)}, u32[]{:S(2)}) copy-start(bf16[4,16,256]{2,1,0:T(8,128)(2,1)} %param.12) | copy-start | bytes 98308
  10.2 12.0 %copy-start.4 = (bf16[32,64]{1,0:T(8,128)(2,1)S(1)}, bf16[32,64]{1,0:T(8,128)(2,1)}, u32[]{:S(2)}) copy-start(bf16[32,64]{1,0:T(8,128)(2,1)} %param.11) | copy-start | bytes 12292
  10.2 19.6 %all-to-all-start = ((bf16[16,2,2560]{2,1,0:T(2,128)(2,1)}), bf16[16,2,2560]{2,1,0:T(2,128)(2,1)S(1)}, u32[]{:S(2)}, u32[]{:S(2)}) async-start(bf16[16,2,2560]{2,1,0:T(2,128)(2,1)} %reshape.187), calls=%async_computation | async-start | bytes 327680 | tf_op jit(solution)/shard_map/all_to_all | solution.py:106
  29.8 19.6 %all-to-all-start.2 = ((bf16[16,168,128]{2,1,0:T(8,128)(2,1)}), bf16[16,168,128]{2,1,0:T(8,128)(2,1)S(1)}, u32[]{:S(2)}, u32[]{:S(2)}) async-start(bf16[16,168,128]{2,1,0:T(8,128)(2,1)} %pad_maximum_fusion.1), calls=%async_computation.2 | async-start | bytes 1376256 | tf_op jit(solution)/shard_map/all_to_all | solution.py:89
  50.9 4.9 %copy-start.5 = (s32[32]{0:T(128)S(1)}, s32[32]{0:T(128)}, u32[]{:S(2)}) copy-start(s32[32]{0:T(128)} %param.14) | copy-start | bytes 388
  50.9 30.4 %all-to-all-start.1 = ((bf16[16,64,1024]{2,1,0:T(8,128)(2,1)}), bf16[16,64,1024]{2,1,0:T(8,128)(2,1)}, u32[]{:S(2)}, u32[]{:S(2)}) async-start(bf16[16,64,1024]{2,1,0:T(8,128)(2,1)} %broadcast_in_dim.41), calls=%async_computation.1 | async-start | bytes 4194304 | tf_op jit(solution)/shard_map/all_to_all | solution.py:65
  74.3 7.0 %copy-start.1 = (bf16[16,64,768]{2,1,0:T(8,128)(2,1)S(1)}, bf16[16,64,768]{2,1,0:T(8,128)(2,1)}, u32[]{:S(2)}) copy-start(bf16[16,64,768]{2,1,0:T(8,128)(2,1)} %shard_map.82) | copy-start | bytes 4718596
  108.7 15.8 %all-to-all-start.4 = ((f32[16,1,1152]{2,1,0:T(1,128)}), f32[16,1,1152]{2,1,0:T(1,128)S(1)}, u32[]{:S(2)}, u32[]{:S(2)}) async-start(f32[16,1,1152]{2,1,0:T(1,128)} %all_to_all.28), calls=%async_computation.4 | async-start | bytes 147456 | tf_op jit(solution)/shard_map/all_to_all | solution.py:156
